TPU v7x, 32 devices: a whole 2x2x4 slice. The times are simulated.
32 devices in a mesh: grp: 2 (over y), var: 8 (over z, x), smp: 2 (over core).
Axes of the slice: x: 2, y: 2, z: 4, core: 2. Of those that a mesh axis runs over, the one named last changes fastest.
Arguments:
- genotypes: bfloat16 [15360, 1024], P(('grp', 'smp'), 'var'), parts along dimension 0, may hold values from 0 to 2, as said below
- ancestry_counts: int32 [15360, 32], P(('grp', 'smp')), parts along dimension 0, may hold values from 1 to 100
- residuals: int32 [15360, 16], P(('grp', 'smp')), parts along dimension 0, may hold values from -3000 to 3000
- freqs: float32 [64, 1024], P('grp', 'var'), parts along dimension 0, may hold values from 0.05 to 0.95
Outputs:
- q_new: float32 [15360, 32], P(('grp', 'smp', 'var')), parts along dimension 0
- q_gradient: float32 [15360, 32], P(('grp', 'smp', 'var')), parts along dimension 0
- p_new: float32 [64, 1024], P('grp', 'var'), parts along dimension 0
- p_gradient: float32 [64, 1024], P('grp', 'var'), parts along dimension 0
- z_score: float32 [64, 16, 1024], P('grp', None, 'var'), parts along dimension 0
There are 2 independent parts, one for each index of `grp`. A program takes and returns all parts, laid end to end along the dimension named above; each array names one. Nothing has to cross between parts.
Inputs may be any that keep to these rules, and one draw needn't show every extreme that they name: `genotypes`: dosages lie in the closed range from 0 to 2.
All inputs are finite; a program needn't handle non-finite values.
Results may differ from a plain program's by a relative error of at most 0.0003.
Values sent between devices are 32-bit elements; how exact they have to be, the bound alone decides.
No kernel may reach another device: no remote copies, remote signals or barrier semaphores. Data moves between devices by JAX's collectives and lax.ppermute only.
A program may use at most 64 MiB of HBM per device.

v0:
```python
import math

import jax
import jax.numpy as jnp
from jax import lax
from jax.sharding import PartitionSpec as P


def normalize(fractions, gradient, second):
    weighted = fractions * (gradient + second[:, None])
    return weighted / jnp.sum(weighted, axis=1, keepdims=True)


def update_freqs(freqs, excess_sum, second_sum, sample_count):
    allele_sum = excess_sum + second_sum
    freq_next = freqs * allele_sum / (freqs * allele_sum + (1.0 - freqs) * second_sum)
    freq_gradient = excess_sum * freqs.shape[0] / math.sqrt(sample_count)
    return (freq_next, freq_gradient)


def shards(genotypes, ancestry_counts, residuals, freqs):
    highest = lax.Precision.HIGHEST
    var_count = lax.axis_size("var")
    sample_rows = genotypes.shape[0]
    sample_count = sample_rows * lax.axis_size("smp")
    variant_count = genotypes.shape[1] * var_count
    anc_count = freqs.shape[0]
    trait_count = residuals.shape[1]
    counts = ancestry_counts.astype(jnp.float32)
    fractions = counts / jnp.sum(counts, axis=1, keepdims=True)
    dosage = genotypes.astype(jnp.float32)
    recon_rows = jnp.dot(fractions, freqs, precision=highest)
    ratio_a = dosage / recon_rows
    ratio_b = (2.0 - dosage) / (1.0 - recon_rows)
    excess = ratio_a - ratio_b
    gradient_part = jnp.dot(excess, freqs.T, precision=highest)
    second_part = jnp.sum(ratio_b, axis=1)
    excess_part = jnp.dot(fractions.T, excess, precision=highest)
    return_part = jnp.dot(fractions.T, ratio_b, precision=highest)
    share_rows = sample_rows // var_count
    first_row = lax.axis_index("var") * share_rows
    excess_sum, second_sum = lax.psum((excess_part, return_part), "smp")
    freq_next, freq_gradient = update_freqs(freqs, excess_sum, second_sum, sample_count)
    gradient_all, second_all = lax.psum((gradient_part, second_part), "var")
    fraction_next = normalize(fractions, gradient_all, second_all)
    own_next = lax.dynamic_slice_in_dim(fraction_next, first_row, share_rows, 0)
    own_gradient = lax.dynamic_slice_in_dim(gradient_all, first_row, share_rows, 0)
    scaled_gradient = own_gradient / math.sqrt(variant_count)
    ratio_next = dosage / jnp.dot(fraction_next, freqs, precision=highest)
    residual = residuals.astype(jnp.float32) / 1000.0
    trait_rows = (fraction_next[:, :, None] * residual[:, None, :]).reshape(
        sample_rows, anc_count * trait_count
    )
    score_part = jnp.dot(trait_rows.T, ratio_next, precision=highest)
    info_part = jnp.dot(
        (fraction_next * fraction_next).T, ratio_next * ratio_next, precision=highest
    )
    score_sum, info_sum = lax.psum((score_part, info_part), "smp")
    score_tiles = score_sum.reshape(anc_count, trait_count, genotypes.shape[1])
    z_score = score_tiles / jnp.sqrt(info_sum + 1e-06)[:, None, :]
    return (own_next, scaled_gradient, freq_next, freq_gradient, z_score)


def solution(mesh):
    in_specs = (
        P(("grp", "smp"), "var"),
        P(("grp", "smp"), None),
        P(("grp", "smp"), None),
        P("grp", "var"),
    )
    out_specs = (
        P(("grp", "smp", "var"), None),
        P(("grp", "smp", "var"), None),
        P("grp", "var"),
        P("grp", "var"),
        P("grp", None, "var"),
    )
    return jax.shard_map(shards, mesh=mesh, in_specs=in_specs, out_specs=out_specs, check_vma=False)
```

profile of v0, /device:TPU:0, one launch (start us, length us, event | category | flops | bytes accessed | tf_op | source)
XLA Modules:
  0.0 131.7 jit_solution(6251124722498044201)
XLA Ops:
  7.2 0.0 copy-start
  7.2 0.0 copy-start.2
  7.2 0.0 all-reduce.4.cloned.1.call-start
  7.2 1.1 convert_reduce_fusion
  8.4 1.6 %copy.13 = bf16[3840,128]{0,1:T(8,128)(2,1)S(1)} copy(bf16[3840,128]{1,0:T(8,128)(2,1)} %param.4) | data formatting | bytes 1966080 | tf_op args[0]
  9.9 0.0 copy-done
  9.9 0.0 copy-done.2
  10.0 3.5 %fusion.8 = (f32[3840]{0:T(1024)S(1)}, f32[3840,128]{0,1:T(8,128)S(1)}, f32[3840,128]{0,1:T(8,128)}) fusion(bf16[3840,128]{0,1:T(8,128)(2,1)S(1)} %copy.13, f32[32,128]{1,0:T(8,128)S(1)} %copy-done.2, s32[3840,32]{0,1:T(8,128)S(1)} %copy-done, f32[3840]{0:T(1024)S(1)} %convert_reduce_fusion), kind=kOutput, calls=%fused_computation.22 | convolution fusion | flops 192426240 | bytes 5453824 | tf_op jit(solution)/shard_map/dot_general | solution.py:32
  13.5 2.0 %fusion.11 = f32[3840,32]{0,1:T(8,128)} fusion(f32[3840,128]{0,1:T(8,128)S(1)} %get-tuple-element.9, f32[32,128]{1,0:T(8,128)S(1)} %copy-done.2), kind=kOutput, calls=%fused_computation.25 | convolution fusion | flops 188743680 | bytes 2473984 | tf_op jit(solution)/shard_map/dot_general | solution.py:36
  15.4 0.0 all-reduce.4.cloned.1.call-update
  15.5 0.0 all-reduce.6.cloned.1.call-start
  15.5 1.7 %convert_multiply_fusion = f32[3840,16]{0,1:T(8,128)} fusion(s32[3840,16]{0,1:T(8,128)} %param.6), kind=kLoop, calls=%fused_computation.12 | loop fusion | flops 122880 | bytes 491520 | tf_op jit(solution)/shard_map/div | solution.py:50
  17.2 2.0 %fusion.9 = f32[32,128]{1,0:T(8,128)S(1)} fusion(f32[3840,128]{0,1:T(8,128)S(1)} %get-tuple-element.9, s32[3840,32]{0,1:T(8,128)S(1)} %copy-done, f32[3840]{0:T(1024)S(1)} %convert_reduce_fusion), kind=kOutput, calls=%fused_computation.23 | convolution fusion | flops 188989440 | bytes 2489344 | tf_op jit(solution)/shard_map/dot_general | solution.py:38
  19.2 38.9 %psum.43 = f32[3840]{0:T(1024)S(1)} all-reduce(f32[3840]{0:T(1024)S(1)} %get-tuple-element.8), channel_id=1, replica_groups=mesh['grp'=2,'var'=8,'smp'=2] {'var'}, use_global_device_ids=true, to_apply=%region_3.0 | all-reduce | flops 3840 | bytes 30720 | tf_op jit(solution)/shard_map/psum | solution.py:44
  58.0 3.5 %fusion.6 = f32[32,128]{1,0:T(8,128)S(1)} fusion(bf16[3840,128]{0,1:T(8,128)(2,1)S(1)} %copy.13, f32[3840,128]{0,1:T(8,128)} %get-tuple-element.12, s32[3840,32]{0,1:T(8,128)S(1)} %copy-done, f32[3840]{0:T(1024)S(1)} %convert_reduce_fusion), kind=kOutput, calls=%fused_computation.21 | convolution fusion | flops 190955520 | bytes 3472384 | tf_op jit(solution)/shard_map/dot_general | solution.py:39
  61.6 29.5 %all-reduce.4.cloned.1.call-done = f32[3840,32]{0,1:T(8,128)} async-done(((f32[3840,32]{0,1:T(8,128)}), f32[3840,32]{0,1:T(8,128)}) %all-reduce.4.cloned.1.call-update) | async-done | bytes 491536 | tf_op jit(solution)/shard_map/psum | solution.py:44
  91.1 1.1 fusion.5
  92.3 1.1 broadcast_divide_fusion
  93.4 1.8 %convolution_divide_fusion = f32[3840,128]{0,1:T(8,128)S(1)} fusion(f32[3840,32]{0,1:T(8,128)S(1)} %broadcast_divide_fusion, f32[32,128]{1,0:T(8,128)S(1)} %copy-done.2, bf16[3840,128]{0,1:T(8,128)(2,1)S(1)} %copy.13), kind=kOutput, calls=%fused_computation | convolution fusion | flops 189726720 | bytes 3457024 | tf_op jit(solution)/shard_map/dot_general | solution.py:49
  95.2 0.0 copy-start.1
  95.2 0.7 constant_dynamic-slice_fusion
  95.9 2.0 %fusion.2 = f32[32,128]{1,0:T(8,128)S(1)} fusion(f32[3840,128]{0,1:T(8,128)S(1)} %convolution_divide_fusion, f32[3840,32]{0,1:T(8,128)S(1)} %broadcast_divide_fusion), kind=kOutput, calls=%fused_computation.6 | convolution fusion | flops 189358080 | bytes 2473984 | tf_op jit(solution)/shard_map/dot_general | solution.py:55
  97.9 0.0 copy-done.1
  98.0 0.9 broadcast_multiply_fusion
  98.8 6.9 %fusion.12 = f32[512,128]{1,0:T(8,128)} fusion(f32[3840,512]{0,1:T(8,128)S(1)} %bitcast.10, f32[3840,128]{0,1:T(8,128)S(1)} %convolution_divide_fusion), kind=kOutput, calls=%fused_computation.26 | convolution fusion | flops 3019898880 | bytes 10092544 | tf_op jit(solution)/shard_map/dot_general | solution.py:54
  105.8 0.0 all-reduce.6.cloned.1.call-update
  105.8 1.6 %dynamic-slice_multiply_fusion = f32[480,32]{0,1:T(8,128)} fusion(f32[3840,32]{0,1:T(8,128)} %all-reduce.4.cloned.1.call-done, s32[]{:T(128)S(6)} %select_n.4), kind=kLoop, calls=%fused_computation.16 | loop fusion | flops 15360 | bytes 122884 | tf_op jit(solution)/shard_map/div | solution.py:48
  107.4 3.5 %all-reduce = (f32[32,128]{1,0:T(8,128)S(1)}, f32[32,128]{1,0:T(8,128)S(1)}, f32[32,128]{1,0:T(8,128)S(1)}) all-reduce(f32[32,128]{1,0:T(8,128)S(1)} %fusion.6, f32[32,128]{1,0:T(8,128)S(1)} %fusion.9, f32[32,128]{1,0:T(8,128)S(1)} %fusion.2), channel_id=1, replica_groups=mesh['grp'=2,'var'=8,'smp'=2] {'smp'}, use_global_device_ids=true, to_apply=%region_6.0 | all-reduce | flops 12288 | bytes 98304 | tf_op jit(solution)/shard_map/psum | solution.py:42
  111.0 0.6 broadcast_multiply_fusion.1
  111.6 11.6 %all-reduce.6.cloned.1.call-done = f32[32,16,128]{2,1,0:T(8,128)} async-done(((f32[32,16,128]{2,1,0:T(8,128)}), f32[32,16,128]{2,1,0:T(8,128)}) %all-reduce.6.cloned.1.call-update) | async-done | bytes 262160 | tf_op jit(solution)/shard_map/psum | solution.py:58
  123.2 1.7 %broadcast_divide_fusion.1 = f32[32,16,128]{2,1,0:T(8,128)} fusion(f32[32,16,128]{2,1,0:T(8,128)} %all-reduce.6.cloned.1.call-done, f32[32,128]{1,0:T(8,128)S(1)} %get-tuple-element.13), kind=kLoop, calls=%fused_computation.15 | loop fusion | flops 65536 | bytes 540672 | tf_op jit(solution)/shard_map/div | solution.py:60
Async XLA Ops:
  7.2 2.8 %copy-start = (s32[3840,32]{0,1:T(8,128)S(1)}, s32[3840,32]{0,1:T(8,128)}, u32[]{:S(2)}) copy-start(s32[3840,32]{0,1:T(8,128)} %param.5) | copy-start | bytes 1474564
  7.2 2.8 %copy-start.2 = (f32[32,128]{1,0:T(8,128)S(1)}, f32[32,128]{1,0:T(8,128)}, u32[]{:S(2)}) copy-start(f32[32,128]{1,0:T(8,128)} %param.7) | copy-start | bytes 49156
  7.2 83.9 %all-reduce.4.cloned.1.call-start = ((), (), s32[]{:S(2)}) async-start(), calls=%async_computation | async-start | bytes 983040 | tf_op jit(solution)/shard_map/psum | solution.py:44
  15.5 107.7 %all-reduce.6.cloned.1.call-start = ((), (), s32[]{:S(2)}) async-start(), calls=%async_computation.1 | async-start | bytes 524288 | tf_op jit(solution)/shard_map/psum | solution.py:58
  95.2 2.8 %copy-start.1 = (f32[3840,16]{0,1:T(8,128)S(1)}, f32[3840,16]{0,1:T(8,128)}, u32[]{:S(2)}) copy-start(f32[3840,16]{0,1:T(8,128)} %convert_multiply_fusion) | copy-start | bytes 737284
Sparse Core Ops, SparseCore 0:
  15.6 75.4 all-reduce.3
  105.9 17.2 all-reduce.5
where the time goes:
time: 132 us
  blocking collectives  42.4 us (32%)
  waiting for transfers between devices  41.2 us (31%)
  matrix products  21.7 us (16%)
  between operations  14.2 us (11%)
  other arithmetic  9.86 us (7%)
  local copies, waits for them, and re-layouts  2.3 us (2%)
    psum x1, blocking collectives, shards(): gradient_all, second_all = lax.psum((gradient_part, second_part), 'var')  38.9 us
    psum x1, waiting for transfers between devices, shards(): gradient_all, second_all = lax.psum((gradient_part, second_part), 'var')  29.5 us
    psum x1, waiting for transfers between devices, shards(): score_sum, info_sum = lax.psum((score_part, info_part), 'smp')  11.6 us
    dot_general x1, matrix products, shards(): score_part = jnp.dot(trait_rows.T, ratio_next, precision=highest)  6.95 us
    psum x1, blocking collectives, shards(): excess_sum, second_sum = lax.psum((excess_part, return_part), 'smp')  3.54 us
    dot_general x1, matrix products, shards(): return_part = jnp.dot(fractions.T, ratio_b, precision=highest)  3.53 us
    dot_general x1, matrix products, shards(): recon_rows = jnp.dot(fractions, freqs, precision=highest)  3.49 us
  transfers between devices with their start and end apart: 2, of which 2 were waited for; matrix products, arithmetic and copies ran while one was open for 7% of the time, Pallas kernels for 0%

commit v1 on v0

v1 whole, which is shorter than its diff:
```python
import functools
import math

import jax
import jax.numpy as jnp
from jax import lax
from jax.experimental import pallas as pl
from jax.experimental.pallas import tpu as pltpu
from jax.sharding import PartitionSpec as P

F32 = jnp.float32
BF16 = jnp.bfloat16


def split(x):
    high = x.astype(BF16)
    return high, (x - high.astype(F32)).astype(BF16)


def dot(a, b, dims):
    return lax.dot_general(a, b, (dims, ((), ())), preferred_element_type=F32)


NN = ((1,), (0,))
NT = ((1,), (1,))
TN = ((0,), (0,))


def first_kernel(geno_ref, counts_ref, freqs_ref, resid_ref, grad_ref, sums_ref, traits_ref):
    freqs = freqs_ref[...]
    freq_high, freq_low = split(freqs)
    ones = jnp.ones_like(freq_high)
    counts = counts_ref[...].astype(F32).astype(BF16)
    table = jnp.concatenate(
        [
            jnp.concatenate([freq_high, ones], axis=1),
            jnp.concatenate([freq_low, jnp.zeros_like(ones)], axis=1),
        ],
        axis=0,
    )
    width = freqs.shape[1]
    both = dot(jnp.concatenate([counts, counts], axis=1), table, NN)
    recon, total = both[:, :width], both[:, width:]
    rest = total - recon
    dosage = geno_ref[...].astype(F32)
    inverse = 1.0 / (recon * rest)
    part_b = (2.0 - dosage) * recon * inverse
    part = dosage * rest * inverse - part_b
    excess = part * total
    excess_high, excess_low = split(excess)
    left = jnp.concatenate([freq_high, freq_low], axis=0)
    left = jnp.concatenate([left, left], axis=1)
    right = jnp.concatenate([excess_high, excess_low], axis=1)
    grads = dot(left, right, NT)
    anc = freqs.shape[0]
    grad_ref[0] = grads[:anc] + grads[anc:]

    part_high, part_low = split(part)
    b_high, b_low = split(part_b)
    counts_t = counts.T
    sums = dot(counts_t, jnp.concatenate([part_high, b_high], axis=1), NN) + dot(
        counts_t, jnp.concatenate([part_low, b_low], axis=1), NN
    )

    @pl.when(pl.program_id(0) == 0)
    def _():
        sums_ref[...] = sums

    @pl.when(pl.program_id(0) > 0)
    def _():
        sums_ref[...] += sums

    traits_ref[0] = (resid_ref[...].astype(F32) / 1000.0).T


def share_kernel(variants, index_ref, parts_ref, counts_ref, q_ref, q_own_ref, g_own_ref):
    gradient = jnp.sum(parts_ref[...], axis=0)
    counts = counts_ref[...].astype(F32).T
    fractions = counts / jnp.sum(counts, axis=0, keepdims=True)
    second = 2.0 * variants - jnp.sum(fractions * gradient, axis=0, keepdims=True)
    weighted = fractions * (gradient + second)
    q_new = weighted / jnp.sum(weighted, axis=0, keepdims=True)
    for i in range(q_ref.shape[0]):
        q_ref[i] = q_new
    q_own_ref[...] = q_new.T
    g_own_ref[...] = (gradient / math.sqrt(variants)).T


def second_kernel(q_ref, geno_ref, traits_ref, freqs_ref, score_ref, info_ref):
    q_new = q_ref[0]
    anc, rows = q_new.shape
    freq_high, freq_low = split(freqs_ref[...])
    q_high, q_low = split(q_new)
    q_three = jnp.concatenate([q_high, q_low, q_high], axis=0)
    f_three = jnp.concatenate([freq_high, freq_high, freq_low], axis=0)
    recon = dot(q_three, f_three, TN)
    ratio = geno_ref[...].astype(F32) / recon
    ratio_high, ratio_low = split(ratio)
    traits = traits_ref[0]
    products = (q_new[:, None, :] * traits[None, :, :]).reshape(anc * traits.shape[0], rows)
    high, low = split(products)
    width = ratio.shape[1]
    wide = dot(high, jnp.concatenate([ratio_high, ratio_low], axis=1), NN)
    score = wide[:, :width] + wide[:, width:] + dot(low, ratio_high, NN)
    square_high, square_low = split(ratio * ratio)
    q2_high, q2_low = split(q_new * q_new)
    wide2 = dot(
        jnp.concatenate([q2_high, q2_low], axis=0),
        jnp.concatenate([square_high, square_low], axis=1),
        NN,
    )
    info = wide2[:anc, :width] + wide2[:anc, width:] + wide2[anc:, :width]

    @pl.when(pl.program_id(0) == 0)
    def _():
        score_ref[...] = score
        info_ref[...] = info

    @pl.when(pl.program_id(0) > 0)
    def _():
        score_ref[...] += score
        info_ref[...] += info


def update_freqs(freqs, excess_sum, second_sum, sample_count):
    allele_sum = excess_sum + second_sum
    freq_next = freqs * allele_sum / (freqs * allele_sum + (1.0 - freqs) * second_sum)
    freq_gradient = excess_sum * freqs.shape[0] / math.sqrt(sample_count)
    return (freq_next, freq_gradient)


def other_sum(tree):
    count = lax.axis_size("smp")
    if count != 2:
        return lax.psum(tree, "smp")
    swap = [(0, 1), (1, 0)]
    return jax.tree.map(lambda x: x + lax.ppermute(x, "smp", swap), tree)


def shards(genotypes, ancestry_counts, residuals, freqs):
    var_count = lax.axis_size("var")
    rows, width = genotypes.shape
    share = rows // var_count
    anc = freqs.shape[0]
    traits = residuals.shape[1]
    sample_count = rows * lax.axis_size("smp")
    variants = width * var_count
    shape = jax.ShapeDtypeStruct

    grads, sums, trait_cols = pl.pallas_call(
        first_kernel,
        grid=(var_count,),
        in_specs=[
            pl.BlockSpec((share, width), lambda i: (i, 0)),
            pl.BlockSpec((share, anc), lambda i: (i, 0)),
            pl.BlockSpec((anc, width), lambda i: (0, 0)),
            pl.BlockSpec((share, traits), lambda i: (i, 0)),
        ],
        out_specs=[
            pl.BlockSpec((1, anc, share), lambda i: (i, 0, 0)),
            pl.BlockSpec((anc, 2 * width), lambda i: (0, 0)),
            pl.BlockSpec((1, traits, share), lambda i: (i, 0, 0)),
        ],
        out_shape=[
            shape((var_count, anc, share), F32),
            shape((anc, 2 * width), F32),
            shape((var_count, traits, share), F32),
        ],
        name="first",
    )(genotypes, ancestry_counts, freqs, residuals)

    parts = lax.all_to_all(grads, "var", 0, 0, tiled=True)

    sums_all = other_sum(sums)
    freq_next, freq_gradient = update_freqs(
        freqs, sums_all[:, :width], sums_all[:, width:], sample_count
    )

    own = lax.axis_index("var").astype(jnp.int32).reshape(1)
    q_send, own_next, own_gradient = pl.pallas_call(
        functools.partial(share_kernel, variants),
        grid_spec=pltpu.PrefetchScalarGridSpec(
            num_scalar_prefetch=1,
            grid=(1,),
            in_specs=[
                pl.BlockSpec((var_count, anc, share), lambda i, own: (0, 0, 0)),
                pl.BlockSpec((share, anc), lambda i, own: (own[0], 0)),
            ],
            out_specs=[
                pl.BlockSpec((var_count, anc, share), lambda i, own: (0, 0, 0)),
                pl.BlockSpec((share, anc), lambda i, own: (0, 0)),
                pl.BlockSpec((share, anc), lambda i, own: (0, 0)),
            ],
        ),
        out_shape=[
            shape((var_count, anc, share), F32),
            shape((share, anc), F32),
            shape((share, anc), F32),
        ],
        name="share",
    )(own, parts, ancestry_counts)

    q_all = lax.all_to_all(q_send, "var", 0, 0, tiled=True)

    score, info = pl.pallas_call(
        second_kernel,
        grid=(var_count,),
        in_specs=[
            pl.BlockSpec((1, anc, share), lambda i: (i, 0, 0)),
            pl.BlockSpec((share, width), lambda i: (i, 0)),
            pl.BlockSpec((1, traits, share), lambda i: (i, 0, 0)),
            pl.BlockSpec((anc, width), lambda i: (0, 0)),
        ],
        out_specs=[
            pl.BlockSpec((anc * traits, width), lambda i: (0, 0)),
            pl.BlockSpec((anc, width), lambda i: (0, 0)),
        ],
        out_shape=[shape((anc * traits, width), F32), shape((anc, width), F32)],
        name="second",
    )(q_all, genotypes, trait_cols, freqs)

    score, info = other_sum((score, info))
    tiles = score.reshape(anc, traits, width)
    z_score = tiles / jnp.sqrt(info + 1e-06)[:, None, :]
    return (own_next, own_gradient, freq_next, freq_gradient, z_score)


def plain_shards(genotypes, ancestry_counts, residuals, freqs):
    highest = lax.Precision.HIGHEST
    var_count = lax.axis_size("var")
    rows, width = genotypes.shape
    share = rows // var_count
    anc = freqs.shape[0]
    traits = residuals.shape[1]
    counts = ancestry_counts.astype(F32)
    fractions = counts / jnp.sum(counts, axis=1, keepdims=True)
    dosage = genotypes.astype(F32)
    recon = jnp.dot(fractions, freqs, precision=highest)
    ratio_a = dosage / recon
    ratio_b = (2.0 - dosage) / (1.0 - recon)
    excess = ratio_a - ratio_b
    gradient, second = lax.psum(
        (jnp.dot(excess, freqs.T, precision=highest), jnp.sum(ratio_b, axis=1)), "var"
    )
    excess_sum, second_sum = lax.psum(
        (
            jnp.dot(fractions.T, excess, precision=highest),
            jnp.dot(fractions.T, ratio_b, precision=highest),
        ),
        "smp",
    )
    freq_next, freq_gradient = update_freqs(
        freqs, excess_sum, second_sum, rows * lax.axis_size("smp")
    )
    weighted = fractions * (gradient + second[:, None])
    q_new = weighted / jnp.sum(weighted, axis=1, keepdims=True)
    first_row = lax.axis_index("var") * share
    own_next = lax.dynamic_slice_in_dim(q_new, first_row, share, 0)
    own_gradient = lax.dynamic_slice_in_dim(gradient, first_row, share, 0)
    ratio = dosage / jnp.dot(q_new, freqs, precision=highest)
    residual = residuals.astype(F32) / 1000.0
    products = (q_new[:, :, None] * residual[:, None, :]).reshape(rows, anc * traits)
    score, info = lax.psum(
        (
            jnp.dot(products.T, ratio, precision=highest),
            jnp.dot((q_new * q_new).T, ratio * ratio, precision=highest),
        ),
        "smp",
    )
    tiles = score.reshape(anc, traits, width)
    z_score = tiles / jnp.sqrt(info + 1e-06)[:, None, :]
    return (own_next, own_gradient / math.sqrt(width * var_count), freq_next, freq_gradient, z_score)


def solution(mesh):
    sizes = dict(mesh.shape)

    def step(genotypes, ancestry_counts, residuals, freqs):
        rows = genotypes.shape[0] // (sizes["grp"] * sizes["smp"])
        whole_tiles = rows % (16 * sizes["var"]) == 0
        in_specs = (
            P(("grp", "smp"), "var"),
            P(("grp", "smp"), None),
            P(("grp", "smp"), None),
            P("grp", "var"),
        )
        out_specs = (
            P(("grp", "smp", "var"), None),
            P(("grp", "smp", "var"), None),
            P("grp", "var"),
            P("grp", "var"),
            P("grp", None, "var"),
        )
        return jax.shard_map(
            shards if whole_tiles else plain_shards,
            mesh=mesh,
            in_specs=in_specs,
            out_specs=out_specs,
            check_vma=False,
        )(genotypes, ancestry_counts, residuals, freqs)

    return step
```

time: 132 us -> 71.8 us (0.54)
  blocking collectives: 42.4 us -> 0 us
  matrix products: 21.7 us -> 0 us
  Pallas kernels: 0 us -> 18.8 us
  between operations: 14.2 us -> 0.69 us
  waiting for transfers between devices: 41.2 us -> 29.1 us
  starting transfers between devices: 0.08 us -> 11.6 us
  other arithmetic: 9.86 us -> 3.06 us
  local copies, waits for them, and re-layouts: 2.3 us -> 7.88 us
    psum x2 -> x0, blocking collectives: 42.4 us -> none  [the longest x1 38.9 us: shards(): gradient_all, second_all = lax.psum((gradient_part, second_part), 'var')]
    psum x2 -> x0, waiting for transfers between devices: 41.1 us -> none  [the longest x1 29.5 us: shards(): gradient_all, second_all = lax.psum((gradient_part, second_part), 'var')]
    all_to_all x0 -> x2, waiting for transfers between devices: none -> 27.9 us  [the longest x1 14.5 us: shards(): parts = lax.all_to_all(grads, 'var', 0, 0, tiled=True)]
    dot_general x7 -> x0, matrix products: 21.7 us -> none  [the longest x1 6.95 us: shards(): score_part = jnp.dot(trait_rows.T, ratio_next, precision=highest)]
    pallas_call x0 -> x3, Pallas kernels: none -> 18.8 us  [the longest x1 8.46 us: shards(): pl.pallas_call(first_kernel, grid=(var_count,), in_specs=[pl.BlockSpec((s...]
    all_to_all x0 -> x2, starting transfers between devices: none -> 11.1 us  [the longest x1 7.28 us: shards(): parts = lax.all_to_all(grads, 'var', 0, 0, tiled=True)]
    unnamed x7 -> x18, local copies, waits for them, and re-layouts: 1.57 us -> 7.88 us
    div x4 -> x1, other arithmetic: 6.08 us -> 0.73 us  [shards(): z_score = tiles / jnp.sqrt(info + 1e-06)[:, None, :]]
  transfers between devices with their start and end apart: 2 -> 5, of which waited for: 2 -> 3; matrix products, arithmetic and copies ran while one was open for 7% -> 4% of each run, Pallas kernels for 0% -> 0%
where the time goes in v1:
time: 71.8 us; the launch traced here: 71.1 us
  waiting for transfers between devices  29.1 us (41%)
  Pallas kernels  18.8 us (26%)
  starting transfers between devices  11.6 us (16%)
  local copies, waits for them, and re-layouts  7.88 us (11%)
  other arithmetic  3.06 us (4%)
    all_to_all x1, waiting for transfers between devices, shards(): parts = lax.all_to_all(grads, 'var', 0, 0, tiled=True)  14.5 us
    all_to_all x1, waiting for transfers between devices, shards(): q_all = lax.all_to_all(q_send, 'var', 0, 0, tiled=True)  13.4 us
    pallas_call x1, Pallas kernels, shards(): pl.pallas_call(first_kernel, grid=(var_count,), in_specs=[pl.BlockSpec((s...  8.46 us
    pallas_call x1, Pallas kernels, shards(): pl.pallas_call(second_kernel, grid=(var_count,), in_specs=[pl.BlockSpec((...  8.02 us
    unnamed x18, local copies, waits for them, and re-layouts  7.88 us
    all_to_all x1, starting transfers between devices, shards(): parts = lax.all_to_all(grads, 'var', 0, 0, tiled=True)  7.28 us
    all_to_all x1, starting transfers between devices, shards(): q_all = lax.all_to_all(q_send, 'var', 0, 0, tiled=True)  3.78 us
    pallas_call x1, Pallas kernels, shards(): pl.pallas_call(functools.partial(share_kernel, variants), grid_spec=pltpu...  2.27 us
  transfers between devices with their start and end apart: 5, of which 3 were waited for; matrix products, arithmetic and copies ran while one was open for 4% of the time, Pallas kernels for 0%

profile of v1, /device:TPU:0, one launch (start us, length us, event | category | flops | bytes accessed | tf_op | source)
XLA Modules:
  0.0 71.1 jit_solution(6843395531168322597)
XLA Ops:
  0.6 0.0 copy-start.4
  0.6 2.9 %copy.9.counts_ref = s32[3840,32]{1,0:T(8,128)} copy(s32[3840,32]{0,1:T(8,128)} %param.5) | data formatting | bytes 983040 | tf_op args[1]
  3.6 0.0 copy-done.4
  3.6 1.8 %copy.10.resid_ref = s32[3840,16]{1,0:T(8,128)} copy(s32[3840,16]{0,1:T(8,128)S(1)} %copy-done.4) | data formatting | bytes 491520 | tf_op args[2]
  5.4 8.5 %first.1 = (f32[8,32,480]{2,1,0:T(8,128)}, f32[32,256]{1,0:T(8,128)}, f32[8,16,480]{2,1,0:T(8,128)}) custom-call(bf16[3840,128]{1,0:T(8,128)(2,1)} %geno_ref.3, s32[3840,32]{1,0:T(8,128)} %copy.9.counts_ref, f32[32,128]{1,0:T(8,128)} %freqs_ref.3, s32[3840,16]{1,0:T(8,128)} %copy.10.resid_ref), custom_call_target="tpu_custom_call" | custom-call | tf_op jit(solution)/shard_map/first/pallas_call | solution.py:150
  13.9 7.3 %all-to-all-start = ((f32[8,32,480]{2,1,0:T(8,128)}), f32[8,32,480]{2,1,0:T(8,128)S(1)}, u32[]{:S(2)}, u32[]{:S(2)}) async-start(f32[8,32,480]{2,1,0:T(8,128)} %get-tuple-element.13), calls=%async_computation | async-start | bytes 1048576 | tf_op jit(solution)/shard_map/all_to_all | solution.py:172
  21.2 0.0 copy-start.6
  21.2 14.5 %all-to-all-done.parts_ref = f32[8,32,480]{2,1,0:T(8,128)S(1)} async-done(((f32[8,32,480]{2,1,0:T(8,128)}), f32[8,32,480]{2,1,0:T(8,128)S(1)}, u32[]{:S(2)}, u32[]{:S(2)}) %all-to-all-start) | async-done | bytes 491552 | tf_op jit(solution)/shard_map/all_to_all | solution.py:172
  35.7 0.0 copy-start.1
  35.7 0.8 %copy-done.1 = f32[8,32,480]{2,1,0:T(8,128)} copy-done((f32[8,32,480]{2,1,0:T(8,128)}, f32[8,32,480]{2,1,0:T(8,128)S(1)}, u32[]{:S(2)}) %copy-start.1) | copy-done | bytes 491544
  36.5 2.3 %share.1 = (f32[8,32,480]{2,1,0:T(8,128)}, f32[480,32]{1,0:T(8,128)}, f32[480,32]{1,0:T(8,128)}) custom-call(s32[1]{0:T(128)} %bitcast.index_ref, f32[8,32,480]{2,1,0:T(8,128)} %copy-done.1, s32[3840,32]{1,0:T(8,128)} %copy.9.counts_ref), custom_call_target="tpu_custom_call" | custom-call | tf_op jit(solution)/shard_map/share/pallas_call | solution.py:180
  38.7 0.0 copy-start.5
  38.7 0.0 copy-start.3
  38.7 0.0 copy-start.2
  38.8 3.8 %all-to-all-start.1 = ((f32[8,32,480]{2,1,0:T(8,128)}), f32[8,32,480]{2,1,0:T(8,128)S(1)}, u32[]{:S(2)}, u32[]{:S(2)}) async-start(f32[8,32,480]{2,1,0:T(8,128)} %get-tuple-element.17), calls=%async_computation.1 | async-start | bytes 1048576 | tf_op jit(solution)/shard_map/all_to_all | solution.py:203
  42.5 0.0 copy-done.6
  42.5 0.1 collective-permute-start
  42.6 1.2 %collective-permute-done = f32[32,256]{1,0:T(8,128)S(1)} collective-permute-done((f32[32,256]{1,0:T(8,128)S(1)}, f32[32,256]{1,0:T(8,128)S(1)}, u32[]{:S(2)}, u32[]{:S(2)}) %collective-permute-start) | collective-permute-done | bytes 32800 | tf_op jit(solution)/shard_map/ppermute | solution.py:137
  43.8 13.4 %all-to-all-done.1.q_ref = f32[8,32,480]{2,1,0:T(8,128)S(1)} async-done(((f32[8,32,480]{2,1,0:T(8,128)}), f32[8,32,480]{2,1,0:T(8,128)S(1)}, u32[]{:S(2)}, u32[]{:S(2)}) %all-to-all-start.1) | async-done | bytes 491552 | tf_op jit(solution)/shard_map/all_to_all | solution.py:203
  57.2 0.0 copy-start
  57.2 0.8 %copy-done = f32[8,32,480]{2,1,0:T(8,128)} copy-done((f32[8,32,480]{2,1,0:T(8,128)}, f32[8,32,480]{2,1,0:T(8,128)S(1)}, u32[]{:S(2)}) %copy-start) | copy-done | bytes 491544
  58.0 8.0 %second.1 = (f32[512,128]{1,0:T(8,128)}, f32[32,128]{1,0:T(8,128)}) custom-call(f32[8,32,480]{2,1,0:T(8,128)} %copy-done, bf16[3840,128]{1,0:T(8,128)(2,1)} %geno_ref.3, f32[8,16,480]{2,1,0:T(8,128)} %get-tuple-element.18.traits_ref, f32[32,128]{1,0:T(8,128)} %freqs_ref.3), custom_call_target="tpu_custom_call" | custom-call | tf_op jit(solution)/shard_map/second/pallas_call | solution.py:205
  66.0 0.0 collective-permute-start.2
  66.0 0.5 collective-permute-start.1
  66.5 0.0 copy-done.5
  66.5 0.6 slice_multiply_fusion
  67.1 0.0 copy-done.3
  67.1 0.7 %copy.12 = f32[480,32]{0,1:T(8,128)} copy(f32[480,32]{1,0:T(8,128)S(1)} %copy-done.3) | data formatting | bytes 122880
  67.9 0.0 copy-done.2
  67.9 0.7 %copy.13 = f32[480,32]{0,1:T(8,128)} copy(f32[480,32]{1,0:T(8,128)S(1)} %copy-done.2) | data formatting | bytes 122880
  68.6 0.0 collective-permute-done.2
  68.6 0.7 %add_sqrt_fusion = f32[32,128]{1,0:T(8,128)S(1)} fusion(f32[32,128]{1,0:T(8,128)} %get-tuple-element.20, f32[32,128]{1,0:T(8,128)S(1)} %collective-permute-done.2), kind=kLoop, calls=%fused_computation.2 | loop fusion | flops 8192 | bytes 49152 | tf_op jit(solution)/shard_map/sqrt | solution.py:224
  69.4 0.0 collective-permute-done.1
  69.4 1.0 %add.24 = f32[512,128]{1,0:T(8,128)S(1)} add(f32[512,128]{1,0:T(8,128)} %get-tuple-element.19, f32[512,128]{1,0:T(8,128)S(1)} %collective-permute-done.1) | non-fusion elementwise | flops 65536 | bytes 786432 | tf_op jit(solution)/shard_map/add | solution.py:137
  70.3 0.7 %broadcast_divide_fusion = f32[32,16,128]{2,1,0:T(8,128)} fusion(f32[32,16,128]{2,1,0:T(8,128)S(1)} %bitcast.2, f32[32,128]{1,0:T(8,128)S(1)} %add_sqrt_fusion), kind=kLoop, calls=%fused_computation | loop fusion | flops 65536 | bytes 540672 | tf_op jit(solution)/shard_map/div | solution.py:224
  (1 shorter events, 0.0 us)
Async XLA Ops:
  0.6 3.0 %copy-start.4 = (s32[3840,16]{0,1:T(8,128)S(1)}, s32[3840,16]{0,1:T(8,128)}, u32[]{:S(2)}) copy-start(s32[3840,16]{0,1:T(8,128)} %param.6) | copy-start | bytes 737284
  13.9 21.8 %all-to-all-start = ((f32[8,32,480]{2,1,0:T(8,128)}), f32[8,32,480]{2,1,0:T(8,128)S(1)}, u32[]{:S(2)}, u32[]{:S(2)}) async-start(f32[8,32,480]{2,1,0:T(8,128)} %get-tuple-element.13), calls=%async_computation | async-start | bytes 1048576 | tf_op jit(solution)/shard_map/all_to_all | solution.py:172
  21.2 21.4 %copy-start.6 = (f32[32,256]{1,0:T(8,128)S(1)}, f32[32,256]{1,0:T(8,128)}, u32[]{:S(2)}) copy-start(f32[32,256]{1,0:T(8,128)} %get-tuple-element.16) | copy-start | bytes 98308
  35.7 0.8 %copy-start.1 = (f32[8,32,480]{2,1,0:T(8,128)}, f32[8,32,480]{2,1,0:T(8,128)S(1)}, u32[]{:S(2)}) copy-start(f32[8,32,480]{2,1,0:T(8,128)S(1)} %all-to-all-done.parts_ref) | copy-start | bytes 1474564
  38.7 27.8 %copy-start.5 = (f32[32,128]{1,0:T(8,128)S(1)}, f32[32,128]{1,0:T(8,128)}, u32[]{:S(2)}) copy-start(f32[32,128]{1,0:T(8,128)} %freqs_ref.3) | copy-start | bytes 49156
  38.7 28.4 %copy-start.3 = (f32[480,32]{1,0:T(8,128)S(1)}, f32[480,32]{1,0:T(8,128)}, u32[]{:S(2)}) copy-start(f32[480,32]{1,0:T(8,128)} %get-tuple-element.21) | copy-start | bytes 184324
  38.7 29.1 %copy-start.2 = (f32[480,32]{1,0:T(8,128)S(1)}, f32[480,32]{1,0:T(8,128)}, u32[]{:S(2)}) copy-start(f32[480,32]{1,0:T(8,128)} %get-tuple-element.22) | copy-start | bytes 184324
  38.8 18.4 %all-to-all-start.1 = ((f32[8,32,480]{2,1,0:T(8,128)}), f32[8,32,480]{2,1,0:T(8,128)S(1)}, u32[]{:S(2)}, u32[]{:S(2)}) async-start(f32[8,32,480]{2,1,0:T(8,128)} %get-tuple-element.17), calls=%async_computation.1 | async-start | bytes 1048576 | tf_op jit(solution)/shard_map/all_to_all | solution.py:203
  42.5 1.3 %collective-permute-start = (f32[32,256]{1,0:T(8,128)S(1)}, f32[32,256]{1,0:T(8,128)S(1)}, u32[]{:S(2)}, u32[]{:S(2)}) collective-permute-start(f32[32,256]{1,0:T(8,128)S(1)} %copy-done.6), channel_id=1, source_target_pairs={{0,1},{1,0},{2,3},{3,2},{4,5},{5,4},{6,7},{7,6},{8,9},{9,8},{10,11... | collective-permute-start | bytes 98312 | tf_op jit(solution)/shard_map/ppermute | solution.py:137
  57.2 0.8 %copy-start = (f32[8,32,480]{2,1,0:T(8,128)}, f32[8,32,480]{2,1,0:T(8,128)S(1)}, u32[]{:S(2)}) copy-start(f32[8,32,480]{2,1,0:T(8,128)S(1)} %all-to-all-done.1.q_ref) | copy-start | bytes 1474564
  66.0 2.6 %collective-permute-start.2 = (f32[32,128]{1,0:T(8,128)}, f32[32,128]{1,0:T(8,128)S(1)}, u32[]{:S(2)}, u32[]{:S(2)}) collective-permute-start(f32[32,128]{1,0:T(8,128)} %get-tuple-element.20), channel_id=1, source_target_pairs={{0,1},{1,0},{2,3},{3,2},{4,5},{5,4},{6,7},{7,6},{8,9},{9,8},{10,11... | collective-permute-start | bytes 49160 | tf_op jit(solution)/shard_map/ppermute | solution.py:137
  66.0 3.4 %collective-permute-start.1 = (f32[512,128]{1,0:T(8,128)}, f32[512,128]{1,0:T(8,128)S(1)}, u32[]{:S(2)}, u32[]{:S(2)}) collective-permute-start(f32[512,128]{1,0:T(8,128)} %get-tuple-element.19), channel_id=1, source_target_pairs={{0,1},{1,0},{2,3},{3,2},{4,5},{5,4},{6,7},{7,6},{8,9},{9,8},{10,11... | collective-permute-start | bytes 786440 | tf_op jit(solution)/shard_map/ppermute | solution.py:137

commit v2 on v0

v2 whole, which is shorter than its diff:
```python
import functools
import math

import jax
import jax.numpy as jnp
from jax import lax
from jax.experimental import pallas as pl
from jax.experimental.pallas import tpu as pltpu
from jax.sharding import PartitionSpec as P

F32 = jnp.float32
BF16 = jnp.bfloat16
LANES = 128
NN = ((1,), (0,))
NT = ((1,), (1,))
TN = ((0,), (0,))


def split(x):
    high = x.astype(BF16)
    return high, (x - high.astype(F32)).astype(BF16)


def dot(a, b, dims):
    return lax.dot_general(a, b, (dims, ((), ())), preferred_element_type=F32)


def count_table(freqs):
    high, low = split(freqs)
    ones = jnp.ones_like(high)
    return jnp.concatenate(
        [
            jnp.concatenate([high, ones], axis=1),
            jnp.concatenate([low, jnp.zeros_like(ones)], axis=1),
        ],
        axis=0,
    )


def ratio_parts(counts, dosage, table):
    width = dosage.shape[1]
    both = dot(jnp.concatenate([counts, counts], axis=0), table, TN)
    recon, total = both[:, :width], both[:, width:]
    rest = total - recon
    inverse = 1.0 / (recon * rest)
    part_b = (2.0 - dosage) * recon * inverse
    part = dosage * rest * inverse - part_b
    return part, part_b, total


def gradient_kernel(shares, place_ref, geno_ref, counts_ref, freqs_ref, grad_ref, excess_ref):
    half_rows = excess_ref.shape[0]
    width = freqs_ref.shape[1]
    anc = freqs_ref.shape[0]
    start = place_ref[0] * half_rows
    freqs = freqs_ref[...]
    table = count_table(freqs)
    for row in range(0, half_rows, LANES):
        first = pl.multiple_of(start + row, LANES)
        counts = counts_ref[:, pl.ds(first, LANES)].astype(F32).astype(BF16)
        dosage = geno_ref[pl.ds(first, LANES), :].astype(F32)
        part, _, total = ratio_parts(counts, dosage, table)
        high, low = split(part * total)
        excess_ref[pl.ds(row, LANES), :width] = high
        excess_ref[pl.ds(row, LANES), width:] = low
    left = jnp.concatenate(split(freqs), axis=0)
    grads = dot(jnp.concatenate([left, left], axis=1), excess_ref[...], NT)
    grads = grads[:anc] + grads[anc:]
    share = half_rows // shares
    for c in range(shares):
        grad_ref[c ^ place_ref[1]] = grads[:, c * share : (c + 1) * share]


def sums_kernel(geno_ref, counts_ref, freqs_ref, resid_ref, sums_ref, traits_ref, own_ref, parts_ref):
    rows, width = geno_ref.shape
    table = count_table(freqs_ref[...])
    for row in range(0, rows, LANES):
        counts = counts_ref[:, pl.ds(row, LANES)].astype(F32).astype(BF16)
        dosage = geno_ref[pl.ds(row, LANES), :].astype(F32)
        part, part_b, _ = ratio_parts(counts, dosage, table)
        for at, value in enumerate((part, part_b)):
            high, low = split(value)
            parts_ref[pl.ds(row, LANES), pl.ds(at * width, width)] = high
            parts_ref[pl.ds(rows + row, LANES), pl.ds(at * width, width)] = low
    counts = counts_ref[...].astype(F32)
    left = counts.astype(BF16)
    sums_ref[...] = dot(jnp.concatenate([left, left], axis=1), parts_ref[...], NN)
    residual = resid_ref[...].astype(F32) / 1000.0
    share = traits_ref.shape[2]
    for c in range(rows // share):
        traits_ref[c] = residual[:, c * share : (c + 1) * share]
        own_ref[c] = counts[:, c * share : (c + 1) * share]


def share_kernel(variants, n_parts, own_ref, counts_ref, *refs):
    parts, (q_ref, grad_ref) = refs[:n_parts], refs[n_parts:]
    gradient = parts[0][...]
    for part in parts[1:]:
        gradient = gradient + part[...]
    counts = counts_ref[own_ref[0]]
    fractions = counts / jnp.sum(counts, axis=0, keepdims=True)
    second = 2.0 * variants - jnp.sum(fractions * gradient, axis=0, keepdims=True)
    weighted = fractions * (gradient + second)
    q_ref[...] = weighted / jnp.sum(weighted, axis=0, keepdims=True)
    grad_ref[...] = gradient / math.sqrt(variants)


def score_kernel(n_shares, fresh, own_ref, *refs):
    q_refs, refs = refs[:n_shares], refs[n_shares:]
    geno_ref, traits_ref, freqs_ref = refs[:3]
    total_ref = None if fresh else refs[3]
    out_ref = refs[-1]
    freq_high, freq_low = split(freqs_ref[...])
    f_three = jnp.concatenate([freq_high, freq_high, freq_low], axis=0)
    anc, width = freqs_ref.shape
    traits = traits_ref.shape[1]
    score, info = None, None
    for c in range(n_shares):
        q_new = q_refs[c][...]
        rows = q_new.shape[1]
        owner = own_ref[c]
        q_high, q_low = split(q_new)
        recon = dot(jnp.concatenate([q_high, q_low, q_high], axis=0), f_three, TN)
        dosage = geno_ref[pl.ds(pl.multiple_of(owner * rows, 16), rows), :].astype(F32)
        ratio = dosage / recon
        ratio_high, ratio_low = split(ratio)
        right = jnp.concatenate([ratio_high, ratio_low], axis=1)
        square_high, square_low = split(ratio * ratio)
        q2_high, q2_low = split(q_new * q_new)
        residual = traits_ref[owner]
        products = (q_new[:, None, :] * residual[None, :, :]).reshape(anc * traits, rows)
        high, low = split(products)
        wide = dot(high, right, NN)
        part = wide[:, :width] + wide[:, width:] + dot(low, ratio_high, NN)
        wide2 = dot(
            jnp.concatenate([q2_high, q2_low], axis=0),
            jnp.concatenate([square_high, square_low], axis=1),
            NN,
        )
        part2 = wide2[:anc, :width] + wide2[:anc, width:] + wide2[anc:, :width]
        score = part if score is None else score + part
        info = part2 if info is None else info + part2
    if not fresh:
        score = score + total_ref[: anc * traits]
        info = info + total_ref[anc * traits :]
    out_ref[: anc * traits] = score
    out_ref[anc * traits :] = info


def final_kernel(mine_ref, other_ref, out_ref):
    anc, traits, width = out_ref.shape
    total = mine_ref[...] + other_ref[...]
    scale = jnp.sqrt(total[anc * traits :] + 1e-06)
    out_ref[...] = total[: anc * traits].reshape(anc, traits, width) / scale[:, None, :]


def update_freqs(freqs, excess_sum, second_sum, sample_count):
    allele_sum = excess_sum + second_sum
    freq_next = freqs * allele_sum / (freqs * allele_sum + (1.0 - freqs) * second_sum)
    freq_gradient = excess_sum * freqs.shape[0] / math.sqrt(sample_count)
    return (freq_next, freq_gradient)


VMEM = pltpu.VMEM
SCALARS = pl.BlockSpec(memory_space=pltpu.SMEM)
IN_VMEM = pl.BlockSpec(memory_space=pltpu.VMEM)


def call(kernel, name, n_scalars, args, outs, scratch=(), cost=2000, aliases=None):
    args = args[:n_scalars] + tuple(pltpu.with_memory_space_constraint(x, VMEM) for x in args[n_scalars:])
    return pl.pallas_call(
        kernel,
        in_specs=[SCALARS] * n_scalars + [IN_VMEM] * (len(args) - n_scalars),
        out_specs=[IN_VMEM] * len(outs),
        out_shape=[VMEM(s, F32) for s in outs],
        scratch_shapes=list(scratch),
        input_output_aliases=aliases or {},
        cost_estimate=pl.CostEstimate(flops=cost * 400_000, bytes_accessed=0, transcendentals=0),
        name=name,
    )(*args)


def shards(genotypes, ancestry_counts, residuals, freqs):
    var_count = lax.axis_size("var")
    rows, width = genotypes.shape
    share = rows // var_count
    half = var_count // 2
    anc = freqs.shape[0]
    traits = residuals.shape[1]
    sample_count = rows * lax.axis_size("smp")
    variants = width * var_count
    place = lax.axis_index("var").astype(jnp.int32)

    def move(x, m):
        return lax.ppermute(x, "var", [(i, i ^ m) for i in range(var_count)])

    def swap(x):
        return lax.ppermute(x, "smp", [(0, 1), (1, 0)])

    geno = pltpu.with_memory_space_constraint(genotypes, VMEM)
    counts = pltpu.with_memory_space_constraint(ancestry_counts.T, VMEM)
    resid = residuals.T

    def gradients(which, name):
        scalars = jnp.stack([which, place % half])
        (grads,) = call(
            functools.partial(gradient_kernel, half),
            name,
            1,
            (scalars, geno, counts, freqs),
            [(half, anc, share)],
            [VMEM((rows // 2, 2 * width), BF16)],
        )
        return grads

    far = gradients(1 - place // half, "grad_far")
    far_even = far.reshape(half // 2, 2, anc, share)
    got = move(far_even[:, 1], 1)
    near = gradients(place // half, "grad_near")
    arrived = [near[0]] + [move(near[m], m) for m in range(1, half)]
    combined = far_even[:, 0] + got
    arrived += [move(combined[m], half + 2 * m) for m in range(half // 2)]

    sums, trait_parts, count_parts = call(
        sums_kernel,
        "sums",
        0,
        (geno, counts, freqs, resid),
        [(anc, 2 * width), (var_count, traits, share), (var_count, anc, share)],
        [VMEM((2 * rows, 2 * width), BF16)],
    )
    sums_all = sums + swap(sums)
    freq_next, freq_gradient = update_freqs(
        freqs, sums_all[:, :width], sums_all[:, width:], sample_count
    )

    own = place.reshape(1)
    q_new, own_gradient = call(
        functools.partial(share_kernel, variants, len(arrived)),
        "share",
        1,
        (own, count_parts, *arrived),
        [(anc, share), (anc, share)],
        cost=500,
    )

    shares = {m: move(q_new, m) for m in range(2, var_count, 2)}
    shares[1] = move(q_new, 1)
    for m in range(3, half, 2):
        shares[m] = move(q_new, m)
    for m in range(half + 1, var_count, 2):
        shares[m] = move(shares[m - 1], 1)
    shares[0] = q_new

    def scores(ms, total):
        owners = jnp.stack([place ^ m for m in ms])
        inputs = (geno, trait_parts, freqs) + (() if total is None else (total,))
        (out,) = call(
            functools.partial(score_kernel, len(ms), total is None),
            "score",
            1,
            (owners, *[shares[m] for m in ms], *inputs),
            [((anc * traits + anc), width)],
            cost=700 * len(ms),
            aliases=None if total is None else {len(ms) + 4: 0},
        )
        return out

    order = [0, 1] + list(range(2, half)) + list(range(half, var_count, 2)) + list(range(half + 1, var_count, 2))
    total = None
    for at in range(0, var_count, 2):
        total = scores(order[at : at + 2], total)
    (z_score,) = call(final_kernel, "final", 0, (total, swap(total)), [(anc, traits, width)], cost=300)
    return (q_new.T, own_gradient.T, freq_next, freq_gradient, z_score)


def plain_shards(genotypes, ancestry_counts, residuals, freqs):
    highest = lax.Precision.HIGHEST
    var_count = lax.axis_size("var")
    rows, width = genotypes.shape
    share = rows // var_count
    anc = freqs.shape[0]
    traits = residuals.shape[1]
    counts = ancestry_counts.astype(F32)
    fractions = counts / jnp.sum(counts, axis=1, keepdims=True)
    dosage = genotypes.astype(F32)
    recon = jnp.dot(fractions, freqs, precision=highest)
    ratio_a = dosage / recon
    ratio_b = (2.0 - dosage) / (1.0 - recon)
    excess = ratio_a - ratio_b
    gradient, second = lax.psum(
        (jnp.dot(excess, freqs.T, precision=highest), jnp.sum(ratio_b, axis=1)), "var"
    )
    excess_sum, second_sum = lax.psum(
        (
            jnp.dot(fractions.T, excess, precision=highest),
            jnp.dot(fractions.T, ratio_b, precision=highest),
        ),
        "smp",
    )
    freq_next, freq_gradient = update_freqs(
        freqs, excess_sum, second_sum, rows * lax.axis_size("smp")
    )
    weighted = fractions * (gradient + second[:, None])
    q_new = weighted / jnp.sum(weighted, axis=1, keepdims=True)
    first_row = lax.axis_index("var") * share
    own_next = lax.dynamic_slice_in_dim(q_new, first_row, share, 0)
    own_gradient = lax.dynamic_slice_in_dim(gradient, first_row, share, 0)
    ratio = dosage / jnp.dot(q_new, freqs, precision=highest)
    residual = residuals.astype(F32) / 1000.0
    products = (q_new[:, :, None] * residual[:, None, :]).reshape(rows, anc * traits)
    score, info = lax.psum(
        (
            jnp.dot(products.T, ratio, precision=highest),
            jnp.dot((q_new * q_new).T, ratio * ratio, precision=highest),
        ),
        "smp",
    )
    tiles = score.reshape(anc, traits, width)
    z_score = tiles / jnp.sqrt(info + 1e-06)[:, None, :]
    return (own_next, own_gradient / math.sqrt(width * var_count), freq_next, freq_gradient, z_score)


def solution(mesh):
    sizes = dict(mesh.shape)

    def step(genotypes, ancestry_counts, residuals, freqs):
        rows = genotypes.shape[0] // (sizes["grp"] * sizes["smp"])
        power = sizes["var"] & (sizes["var"] - 1) == 0 and sizes["var"] >= 4
        tiled = rows % (16 * sizes["var"]) == 0 and rows % (2 * LANES) == 0
        in_specs = (
            P(("grp", "smp"), "var"),
            P(("grp", "smp"), None),
            P(("grp", "smp"), None),
            P("grp", "var"),
        )
        out_specs = (
            P(("grp", "smp", "var"), None),
            P(("grp", "smp", "var"), None),
            P("grp", "var"),
            P("grp", "var"),
            P("grp", None, "var"),
        )
        return jax.shard_map(
            shards if power and tiled and sizes["smp"] == 2 else plain_shards,
            mesh=mesh,
            in_specs=in_specs,
            out_specs=out_specs,
            check_vma=False,
        )(genotypes, ancestry_counts, residuals, freqs)

    return step
```

time: 132 us -> 49.6 us (0.38)
  blocking collectives: 42.4 us -> 0 us
  waiting for transfers between devices: 41.2 us -> 8.32 us
  matrix products: 21.7 us -> 0 us
  starting transfers between devices: 0.08 us -> 19.1 us
  between operations: 14.2 us -> 0.82 us
  Pallas kernels: 0 us -> 13 us
  other arithmetic: 9.86 us -> 3.68 us
  local copies, waits for them, and re-layouts: 2.3 us -> 4.33 us
    psum x2 -> x0, blocking collectives: 42.4 us -> none  [the longest x1 38.9 us: shards(): gradient_all, second_all = lax.psum((gradient_part, second_part), 'var')]
    psum x2 -> x0, waiting for transfers between devices: 41.1 us -> none  [the longest x1 29.5 us: shards(): gradient_all, second_all = lax.psum((gradient_part, second_part), 'var')]
    dot_general x7 -> x0, matrix products: 21.7 us -> none  [the longest x1 6.95 us: shards(): score_part = jnp.dot(trait_rows.T, ratio_next, precision=highest)]
    ppermute x0 -> x15, starting transfers between devices: none -> 19.1 us  [the longest x13 18.5 us: move(): return lax.ppermute(x, 'var', [(i, i ^ m) for i in range(var_count)])]
    pallas_call x0 -> x9, Pallas kernels: none -> 13 us  [call(): pl.pallas_call(kernel, in_specs=[SCALARS] * n_scalars + [IN_VMEM] * (len(...]
    ppermute x0 -> x15, waiting for transfers between devices: none -> 8.32 us  [the longest x13 7.22 us: move(): return lax.ppermute(x, 'var', [(i, i ^ m) for i in range(var_count)])]
    div x4 -> x0, other arithmetic: 6.08 us -> none  [the longest x1 1.68 us: shards(): z_score = score_tiles / jnp.sqrt(info_sum + 1e-06)[:, None, :]]
    another operation x0 -> x5, other arithmetic: none -> 3.03 us  [the longest x4 2.43 us: scores(): owners = jnp.stack([place ^ m for m in ms])]
  transfers between devices with their start and end apart: 2 -> 15, of which waited for: 2 -> 4; matrix products, arithmetic and copies ran while one was open for 7% -> 9% of each run, Pallas kernels for 0% -> 19%
where the time goes in v2:
time: 49.6 us; the launch traced here: 49.3 us
  starting transfers between devices  19.1 us (39%)
  Pallas kernels  13 us (26%)
  waiting for transfers between devices  8.32 us (17%)
  local copies, waits for them, and re-layouts  4.33 us (9%)
  other arithmetic  3.68 us (7%)
  between operations  0.82 us (2%)
    ppermute x13, starting transfers between devices, move(): return lax.ppermute(x, 'var', [(i, i ^ m) for i in range(var_count)])  18.5 us
    pallas_call x9, Pallas kernels, call(): pl.pallas_call(kernel, in_specs=[SCALARS] * n_scalars + [IN_VMEM] * (len(...  13 us
    ppermute x13, waiting for transfers between devices, move(): return lax.ppermute(x, 'var', [(i, i ^ m) for i in range(var_count)])  7.22 us
    unnamed x11, local copies, waits for them, and re-layouts  4.29 us
    another operation x4, other arithmetic, scores(): owners = jnp.stack([place ^ m for m in ms])  2.43 us
    ppermute x2, waiting for transfers between devices, swap(): return lax.ppermute(x, 'smp', [(0, 1), (1, 0)])  1.1 us
  transfers between devices with their start and end apart: 15, of which 4 were waited for; matrix products, arithmetic and copies ran while one was open for 9% of the time, Pallas kernels for 19%

profile of v2, /device:TPU:0, one launch (start us, length us, event | category | flops | bytes accessed | tf_op | source)
XLA Modules:
  0.0 49.3 jit_solution(10670532645603789752)
XLA Ops:
  0.6 0.0 copy-start
  0.7 0.6 %pad_add_fusion = (s32[2]{0:T(128)}, s32[2]{0:T(128)}) fusion(s32[1]{0:T(128)} %bitcast.3, s32[1]{0:T(128)} %bitcast.4, s32[1]{0:T(128)} %bitcast.9), kind=kLoop, calls=%fused_computation.11 | loop fusion | flops 4 | bytes 28 | tf_op jit(solution)/shard_map/stack | solution.py:205
  1.3 0.1 copy-done
  1.4 0.0 copy-start.1
  1.4 1.2 %copy-done.1 = bf16[3840,128]{1,0:T(8,128)(2,1)S(1)} copy-done((bf16[3840,128]{1,0:T(8,128)(2,1)S(1)}, bf16[3840,128]{1,0:T(8,128)(2,1)}, u32[]{:S(2)}) %copy-start.1) | copy-done | bytes 983064
  2.6 0.0 copy-start.2
  2.6 1.0 %copy-done.2 = s32[3840,32]{0,1:T(8,128)S(1)} copy-done((s32[3840,32]{0,1:T(8,128)S(1)}, s32[3840,32]{0,1:T(8,128)}, u32[]{:S(2)}) %copy-start.2) | copy-done | bytes 491544
  3.6 1.6 %grad_far.1 = f32[4,32,480]{2,1,0:T(8,128)S(1)} custom-call(s32[2]{0:T(128)} %get-tuple-element.24.place_ref, bf16[3840,128]{1,0:T(8,128)(2,1)S(1)} %copy-done.1, s32[32,3840]{1,0:T(8,128)S(1)} %bitcast.42, f32[32,128]{1,0:T(8,128)S(1)} %copy-done), custom_call_target="tpu_custom_call" | custom-call | flops 800000000 | tf_op jit(solution)/shard_map/grad_far/pallas_call | solution.py:171
  5.3 3.0 %collective-permute-start.3 = (f32[2,32,480]{2,1,0:T(8,128)S(1)}, f32[2,32,480]{2,1,0:T(8,128)S(1)}, u32[]{:S(2)}, u32[]{:S(2)}) collective-permute-start(f32[2,32,480]{2,1,0:T(8,128)S(1)} %slice_bitcast_fusion), channel_id=1, source_target_pairs={{0,2},{2,0},{4,6},{6,4},{8,10},{10,8},{12,14},{14,12},{1,3},{3,1},... | collective-permute-start | bytes 368648 | tf_op jit(solution)/shard_map/ppermute | solution.py:195
  8.3 1.6 %grad_near.1 = f32[4,32,480]{2,1,0:T(8,128)S(1)} custom-call(s32[2]{0:T(128)} %get-tuple-element.23.place_ref, bf16[3840,128]{1,0:T(8,128)(2,1)S(1)} %copy-done.1, s32[32,3840]{1,0:T(8,128)S(1)} %bitcast.43, f32[32,128]{1,0:T(8,128)S(1)} %copy-done), custom_call_target="tpu_custom_call" | custom-call | flops 800000000 | tf_op jit(solution)/shard_map/grad_near/pallas_call | solution.py:171
  10.0 0.1 collective-permute-start
  10.1 2.1 %collective-permute-start.1 = (f32[32,480]{1,0:T(8,128)S(1)}, f32[32,480]{1,0:T(8,128)S(1)}, u32[]{:S(2)}, u32[]{:S(2)}) collective-permute-start(f32[32,480]{1,0:T(8,128)S(1)} %get-tuple-element.16), channel_id=1, source_target_pairs={{0,4},{2,6},{4,0},{6,2},{8,12},{10,14},{12,8},{14,10},{1,5},{3,7},... | collective-permute-start | bytes 184328 | tf_op jit(solution)/shard_map/ppermute | solution.py:195
  12.1 1.4 %collective-permute-start.2 = (f32[32,480]{1,0:T(8,128)S(1)}, f32[32,480]{1,0:T(8,128)S(1)}, u32[]{:S(2)}, u32[]{:S(2)}) collective-permute-start(f32[32,480]{1,0:T(8,128)S(1)} %get-tuple-element.15), channel_id=1, source_target_pairs={{0,6},{2,4},{4,2},{6,0},{8,14},{10,12},{12,10},{14,8},{1,7},{3,5},... | collective-permute-start | bytes 184328 | tf_op jit(solution)/shard_map/ppermute | solution.py:195
  13.5 0.6 %pad_add_fusion.5.own_ref = s32[2]{0:T(128)} fusion(s32[1]{0:T(128)} %bitcast.23, s32[1]{0:T(128)} %bitcast.own_ref), kind=kLoop, calls=%fused_computation.16 | loop fusion | flops 2 | bytes 16 | tf_op jit(solution)/shard_map/stack | solution.py:256
  14.1 0.7 %pad_add_fusion.4.own_ref = s32[2]{0:T(128)} fusion(s32[1]{0:T(128)} %bitcast.22, s32[1]{0:T(128)} %bitcast.21), kind=kLoop, calls=%fused_computation.15 | loop fusion | flops 2 | bytes 16 | tf_op jit(solution)/shard_map/stack | solution.py:256
  14.8 0.6 %pad_add_fusion.3.own_ref = s32[2]{0:T(128)} fusion(s32[1]{0:T(128)} %bitcast.20, s32[1]{0:T(128)} %bitcast.19), kind=kLoop, calls=%fused_computation.14 | loop fusion | flops 2 | bytes 16 | tf_op jit(solution)/shard_map/stack | solution.py:256
  15.4 0.0 copy-start.3
  15.4 0.0 collective-permute-done.3
  15.4 2.7 %collective-permute-start.4 = (f32[32,480]{1,0:T(8,128)S(1)}, f32[32,480]{1,0:T(8,128)S(1)}, u32[]{:S(2)}, u32[]{:S(2)}) collective-permute-start(f32[32,480]{1,0:T(8,128)S(1)} %get-tuple-element.20), channel_id=1, source_target_pairs={{0,8},{2,10},{4,12},{6,14},{8,0},{10,2},{12,4},{14,6},{1,9},{3,11}... | collective-permute-start | bytes 184328 | tf_op jit(solution)/shard_map/ppermute | solution.py:195
  18.1 1.3 %collective-permute-start.5 = (f32[32,480]{1,0:T(8,128)S(1)}, f32[32,480]{1,0:T(8,128)S(1)}, u32[]{:S(2)}, u32[]{:S(2)}) collective-permute-start(f32[32,480]{1,0:T(8,128)S(1)} %get-tuple-element.19), channel_id=1, source_target_pairs={{0,12},{2,14},{4,8},{6,10},{8,4},{10,6},{12,0},{14,2},{1,13},{3,15... | collective-permute-start | bytes 184328 | tf_op jit(solution)/shard_map/ppermute | solution.py:195
  19.4 0.0 copy-done.3
  19.4 2.4 %sums.1 = (f32[32,256]{1,0:T(8,128)S(1)}, f32[8,16,480]{2,1,0:T(8,128)S(1)}, f32[8,32,480]{2,1,0:T(8,128)S(1)}) custom-call(bf16[3840,128]{1,0:T(8,128)(2,1)S(1)} %copy-done.1, s32[32,3840]{1,0:T(8,128)S(1)} %bitcast.44, f32[32,128]{1,0:T(8,128)S(1)} %copy-done, s32[16,3840]{1,0:T(8,128)S(1)} %bitcast.45), custom_call_target="tpu_custom_call" | custom-call | flops 800000000 | tf_op jit(solution)/shard_map/sums/pallas_call | solution.py:171
  21.8 0.0 collective-permute-done.refs_1_
  21.8 0.0 collective-permute-done.1.refs_2_
  21.8 0.0 collective-permute-done.2.refs_3_
  21.8 0.9 %collective-permute-done.4.refs_4_ = f32[32,480]{1,0:T(8,128)S(1)} collective-permute-done((f32[32,480]{1,0:T(8,128)S(1)}, f32[32,480]{1,0:T(8,128)S(1)}, u32[]{:S(2)}, u32[]{:S(2)}) %collective-permute-start.4) | collective-permute-done | bytes 61472 | tf_op jit(solution)/shard_map/ppermute | solution.py:195
  22.7 1.5 %collective-permute-done.5.refs_5_ = f32[32,480]{1,0:T(8,128)S(1)} collective-permute-done((f32[32,480]{1,0:T(8,128)S(1)}, f32[32,480]{1,0:T(8,128)S(1)}, u32[]{:S(2)}, u32[]{:S(2)}) %collective-permute-start.5) | collective-permute-done | bytes 61472 | tf_op jit(solution)/shard_map/ppermute | solution.py:195
  24.2 0.1 share.1
  24.3 0.5 %collective-permute-start.13 = (f32[32,480]{1,0:T(8,128)S(1)}, f32[32,480]{1,0:T(8,128)S(1)}, u32[]{:S(2)}, u32[]{:S(2)}) collective-permute-start(f32[32,480]{1,0:T(8,128)S(1)} %get-tuple-element.11.refs_0_), channel_id=1, source_target_pairs={{0,2},{2,0},{4,6},{6,4},{8,10},{10,8},{12,14},{14,12},{1,3},{3,1},... | collective-permute-start | bytes 184328 | tf_op jit(solution)/shard_map/ppermute | solution.py:195
  24.8 0.0 collective-permute-start.11
  24.8 3.1 %collective-permute-start.12 = (f32[32,480]{1,0:T(8,128)S(1)}, f32[32,480]{1,0:T(8,128)S(1)}, u32[]{:S(2)}, u32[]{:S(2)}) collective-permute-start(f32[32,480]{1,0:T(8,128)S(1)} %get-tuple-element.11.refs_0_), channel_id=1, source_target_pairs={{0,6},{2,4},{4,2},{6,0},{8,14},{10,12},{12,10},{14,8},{1,7},{3,5},... | collective-permute-start | bytes 184328 | tf_op jit(solution)/shard_map/ppermute | solution.py:195
  27.9 1.7 %collective-permute-start.7 = (f32[32,480]{1,0:T(8,128)S(1)}, f32[32,480]{1,0:T(8,128)S(1)}, u32[]{:S(2)}, u32[]{:S(2)}) collective-permute-start(f32[32,480]{1,0:T(8,128)S(1)} %get-tuple-element.11.refs_0_), channel_id=1, source_target_pairs={{0,8},{2,10},{4,12},{6,14},{8,0},{10,2},{12,4},{14,6},{1,9},{3,11}... | collective-permute-start | bytes 184328 | tf_op jit(solution)/shard_map/ppermute | solution.py:195
  29.5 0.7 %collective-permute-start.9 = (f32[32,480]{1,0:T(8,128)S(1)}, f32[32,480]{1,0:T(8,128)S(1)}, u32[]{:S(2)}, u32[]{:S(2)}) collective-permute-start(f32[32,480]{1,0:T(8,128)S(1)} %get-tuple-element.11.refs_0_), channel_id=1, source_target_pairs={{0,12},{2,14},{4,8},{6,10},{8,4},{10,6},{12,0},{14,2},{1,13},{3,15... | collective-permute-start | bytes 184328 | tf_op jit(solution)/shard_map/ppermute | solution.py:195
  30.2 0.6 %pad_add_fusion.2.own_ref = s32[2]{0:T(128)} fusion(s32[1]{0:T(128)} %bitcast.18, s32[1]{0:T(128)} %bitcast.17), kind=kLoop, calls=%fused_computation.13 | loop fusion | flops 2 | bytes 16 | tf_op jit(solution)/shard_map/stack | solution.py:256
  30.8 4.8 %collective-permute-done.9.refs_1_ = f32[32,480]{1,0:T(8,128)S(1)} collective-permute-done((f32[32,480]{1,0:T(8,128)S(1)}, f32[32,480]{1,0:T(8,128)S(1)}, u32[]{:S(2)}, u32[]{:S(2)}) %collective-permute-start.9) | collective-permute-done | bytes 61472 | tf_op jit(solution)/shard_map/ppermute | solution.py:195
  35.6 0.5 %collective-permute-start.10 = (f32[32,480]{1,0:T(8,128)S(1)}, f32[32,480]{1,0:T(8,128)S(1)}, u32[]{:S(2)}, u32[]{:S(2)}) collective-permute-start(f32[32,480]{1,0:T(8,128)S(1)} %collective-permute-done.9.refs_1_), channel_id=1, source_target_pairs={{0,2},{2,0},{4,6},{6,4},{8,10},{10,8},{12,14},{14,12},{1,3},{3,1},... | collective-permute-start | bytes 184328 | tf_op jit(solution)/shard_map/ppermute | solution.py:195
  36.1 0.0 collective-permute-done.7.refs_0_
  36.1 1.5 %collective-permute-start.8 = (f32[32,480]{1,0:T(8,128)S(1)}, f32[32,480]{1,0:T(8,128)S(1)}, u32[]{:S(2)}, u32[]{:S(2)}) collective-permute-start(f32[32,480]{1,0:T(8,128)S(1)} %collective-permute-done.7.refs_0_), channel_id=1, source_target_pairs={{0,2},{2,0},{4,6},{6,4},{8,10},{10,8},{12,14},{14,12},{1,3},{3,1},... | collective-permute-start | bytes 184328 | tf_op jit(solution)/shard_map/ppermute | solution.py:195
  37.6 0.0 collective-permute-done.13.refs_1_
  37.6 1.8 %score.4.refs_5_ = f32[544,128]{1,0:T(8,128)S(1)} custom-call(s32[2]{0:T(128)} %pad_add_fusion.5.own_ref, f32[32,480]{1,0:T(8,128)S(1)} %get-tuple-element.11.refs_0_, f32[32,480]{1,0:T(8,128)S(1)} %collective-permute-done.13.refs_1_, bf16[3840,128]{1,0:T(8,128)(2,1)S(1)} %copy-done.1, f32[8,16,480]{2,1,0:T(8,128)S(1)} %get-tuple-element.14.refs_3_, ...), custom_call_target="tpu_custom_call" | custom-call | flops 560000000 | tf_op jit(solution)/shard_map/score/pallas_call | solution.py:171
  39.4 0.0 collective-permute-done.11.refs_0_
  39.5 0.0 collective-permute-done.12.refs_1_
  39.5 1.8 %score.5.refs_5_ = f32[544,128]{1,0:T(8,128)S(1)} custom-call(s32[2]{0:T(128)} %pad_add_fusion.4.own_ref, f32[32,480]{1,0:T(8,128)S(1)} %collective-permute-done.11.refs_0_, f32[32,480]{1,0:T(8,128)S(1)} %collective-permute-done.12.refs_1_, bf16[3840,128]{1,0:T(8,128)(2,1)S(1)} %copy-done.1, ...), custom_call_target="tpu_custom_call", output_to_operand_aliasing={{}: (6, {})} | custom-call | flops 560000000 | tf_op jit(solution)/shard_map/score/pallas_call | solution.py:171
  41.3 1.8 %score.6.refs_5_ = f32[544,128]{1,0:T(8,128)S(1)} custom-call(s32[2]{0:T(128)} %pad_add_fusion.3.own_ref, f32[32,480]{1,0:T(8,128)S(1)} %collective-permute-done.7.refs_0_, f32[32,480]{1,0:T(8,128)S(1)} %collective-permute-done.9.refs_1_, bf16[3840,128]{1,0:T(8,128)(2,1)S(1)} %copy-done.1, ...), custom_call_target="tpu_custom_call", output_to_operand_aliasing={{}: (6, {})} | custom-call | flops 560000000 | tf_op jit(solution)/shard_map/score/pallas_call | solution.py:171
  43.1 0.0 collective-permute-done.10.refs_1_
  43.1 0.0 collective-permute-done.8.refs_0_
  43.1 1.8 %score.7.mine_ref = f32[544,128]{1,0:T(8,128)S(1)} custom-call(s32[2]{0:T(128)} %pad_add_fusion.2.own_ref, f32[32,480]{1,0:T(8,128)S(1)} %collective-permute-done.8.refs_0_, f32[32,480]{1,0:T(8,128)S(1)} %collective-permute-done.10.refs_1_, bf16[3840,128]{1,0:T(8,128)(2,1)S(1)} %copy-done.1, ...), custom_call_target="tpu_custom_call", output_to_operand_aliasing={{}: (6, {})} | custom-call | flops 560000000 | tf_op jit(solution)/shard_map/score/pallas_call | solution.py:171
  45.0 0.1 collective-permute-start.14
  45.0 0.5 %collective-permute-start.6 = (f32[32,256]{1,0:T(8,128)S(1)}, f32[32,256]{1,0:T(8,128)S(1)}, u32[]{:S(2)}, u32[]{:S(2)}) collective-permute-start(f32[32,256]{1,0:T(8,128)S(1)} %get-tuple-element.13), channel_id=1, source_target_pairs={{0,1},{1,0},{2,3},{3,2},{4,5},{5,4},{6,7},{7,6},{8,9},{9,8},{10,11... | collective-permute-start | bytes 98312 | tf_op jit(solution)/shard_map/ppermute | solution.py:198
  45.5 1.1 %collective-permute-done.6 = f32[32,256]{1,0:T(8,128)S(1)} collective-permute-done((f32[32,256]{1,0:T(8,128)S(1)}, f32[32,256]{1,0:T(8,128)S(1)}, u32[]{:S(2)}, u32[]{:S(2)}) %collective-permute-start.6) | collective-permute-done | bytes 32800 | tf_op jit(solution)/shard_map/ppermute | solution.py:198
  46.6 0.6 %slice_multiply_fusion = (f32[32,128]{1,0:T(8,128)}, f32[32,128]{1,0:T(8,128)}) fusion(f32[32,256]{1,0:T(8,128)S(1)} %add.20, f32[32,128]{1,0:T(8,128)S(1)} %copy-done), kind=kLoop, calls=%fused_computation.10 | loop fusion | flops 28672 | bytes 81920 | tf_op jit(solution)/shard_map/div | solution.py:160
  47.3 0.6 %copy.19 = f32[480,32]{0,1:T(8,128)} copy(f32[480,32]{0,1:T(8,128)S(1)} %bitcast.39) | data formatting | bytes 122880
  47.9 0.6 %copy.20 = f32[480,32]{0,1:T(8,128)} copy(f32[480,32]{0,1:T(8,128)S(1)} %bitcast.38) | data formatting | bytes 122880
  48.5 0.0 collective-permute-done.14.other_ref
  48.5 0.1 final.1
  48.6 0.7 %copy.21 = f32[32,16,128]{2,1,0:T(8,128)} copy(f32[32,16,128]{2,1,0:T(8,128)S(1)} %final.1) | data formatting | bytes 524288
  (5 shorter events, 0.1 us)
Async XLA Ops:
  0.6 0.7 %copy-start = (f32[32,128]{1,0:T(8,128)S(1)}, f32[32,128]{1,0:T(8,128)}, u32[]{:S(2)}) copy-start(f32[32,128]{1,0:T(8,128)} %refs_4_.7) | copy-start | bytes 49156
  1.4 1.2 %copy-start.1 = (bf16[3840,128]{1,0:T(8,128)(2,1)S(1)}, bf16[3840,128]{1,0:T(8,128)(2,1)}, u32[]{:S(2)}) copy-start(bf16[3840,128]{1,0:T(8,128)(2,1)} %refs_2_.7) | copy-start | bytes 2949124
  2.6 1.0 %copy-start.2 = (s32[3840,32]{0,1:T(8,128)S(1)}, s32[3840,32]{0,1:T(8,128)}, u32[]{:S(2)}) copy-start(s32[3840,32]{0,1:T(8,128)} %param.5) | copy-start | bytes 1474564
  5.3 10.1 %collective-permute-start.3 = (f32[2,32,480]{2,1,0:T(8,128)S(1)}, f32[2,32,480]{2,1,0:T(8,128)S(1)}, u32[]{:S(2)}, u32[]{:S(2)}) collective-permute-start(f32[2,32,480]{2,1,0:T(8,128)S(1)} %slice_bitcast_fusion), channel_id=1, source_target_pairs={{0,2},{2,0},{4,6},{6,4},{8,10},{10,8},{12,14},{14,12},{1,3},{3,1},... | collective-permute-start | bytes 368648 | tf_op jit(solution)/shard_map/ppermute | solution.py:195
  10.0 11.8 %collective-permute-start = (f32[32,480]{1,0:T(8,128)S(1)}, f32[32,480]{1,0:T(8,128)S(1)}, u32[]{:S(2)}, u32[]{:S(2)}) collective-permute-start(f32[32,480]{1,0:T(8,128)S(1)} %get-tuple-element.17), channel_id=1, source_target_pairs={{0,2},{2,0},{4,6},{6,4},{8,10},{10,8},{12,14},{14,12},{1,3},{3,1},... | collective-permute-start | bytes 184328 | tf_op jit(solution)/shard_map/ppermute | solution.py:195
  10.1 11.7 %collective-permute-start.1 = (f32[32,480]{1,0:T(8,128)S(1)}, f32[32,480]{1,0:T(8,128)S(1)}, u32[]{:S(2)}, u32[]{:S(2)}) collective-permute-start(f32[32,480]{1,0:T(8,128)S(1)} %get-tuple-element.16), channel_id=1, source_target_pairs={{0,4},{2,6},{4,0},{6,2},{8,12},{10,14},{12,8},{14,10},{1,5},{3,7},... | collective-permute-start | bytes 184328 | tf_op jit(solution)/shard_map/ppermute | solution.py:195
  12.1 9.7 %collective-permute-start.2 = (f32[32,480]{1,0:T(8,128)S(1)}, f32[32,480]{1,0:T(8,128)S(1)}, u32[]{:S(2)}, u32[]{:S(2)}) collective-permute-start(f32[32,480]{1,0:T(8,128)S(1)} %get-tuple-element.15), channel_id=1, source_target_pairs={{0,6},{2,4},{4,2},{6,0},{8,14},{10,12},{12,10},{14,8},{1,7},{3,5},... | collective-permute-start | bytes 184328 | tf_op jit(solution)/shard_map/ppermute | solution.py:195
  15.4 4.1 %copy-start.3 = (s32[3840,16]{0,1:T(8,128)S(1)}, s32[3840,16]{0,1:T(8,128)}, u32[]{:S(2)}) copy-start(s32[3840,16]{0,1:T(8,128)} %param.6) | copy-start | bytes 737284
  15.4 7.3 %collective-permute-start.4 = (f32[32,480]{1,0:T(8,128)S(1)}, f32[32,480]{1,0:T(8,128)S(1)}, u32[]{:S(2)}, u32[]{:S(2)}) collective-permute-start(f32[32,480]{1,0:T(8,128)S(1)} %get-tuple-element.20), channel_id=1, source_target_pairs={{0,8},{2,10},{4,12},{6,14},{8,0},{10,2},{12,4},{14,6},{1,9},{3,11}... | collective-permute-start | bytes 184328 | tf_op jit(solution)/shard_map/ppermute | solution.py:195
  18.1 6.2 %collective-permute-start.5 = (f32[32,480]{1,0:T(8,128)S(1)}, f32[32,480]{1,0:T(8,128)S(1)}, u32[]{:S(2)}, u32[]{:S(2)}) collective-permute-start(f32[32,480]{1,0:T(8,128)S(1)} %get-tuple-element.19), channel_id=1, source_target_pairs={{0,12},{2,14},{4,8},{6,10},{8,4},{10,6},{12,0},{14,2},{1,13},{3,15... | collective-permute-start | bytes 184328 | tf_op jit(solution)/shard_map/ppermute | solution.py:195
  24.3 13.3 %collective-permute-start.13 = (f32[32,480]{1,0:T(8,128)S(1)}, f32[32,480]{1,0:T(8,128)S(1)}, u32[]{:S(2)}, u32[]{:S(2)}) collective-permute-start(f32[32,480]{1,0:T(8,128)S(1)} %get-tuple-element.11.refs_0_), channel_id=1, source_target_pairs={{0,2},{2,0},{4,6},{6,4},{8,10},{10,8},{12,14},{14,12},{1,3},{3,1},... | collective-permute-start | bytes 184328 | tf_op jit(solution)/shard_map/ppermute | solution.py:195
  24.8 14.6 %collective-permute-start.11 = (f32[32,480]{1,0:T(8,128)S(1)}, f32[32,480]{1,0:T(8,128)S(1)}, u32[]{:S(2)}, u32[]{:S(2)}) collective-permute-start(f32[32,480]{1,0:T(8,128)S(1)} %get-tuple-element.11.refs_0_), channel_id=1, source_target_pairs={{0,4},{2,6},{4,0},{6,2},{8,12},{10,14},{12,8},{14,10},{1,5},{3,7},... | collective-permute-start | bytes 184328 | tf_op jit(solution)/shard_map/ppermute | solution.py:195
  24.8 14.6 %collective-permute-start.12 = (f32[32,480]{1,0:T(8,128)S(1)}, f32[32,480]{1,0:T(8,128)S(1)}, u32[]{:S(2)}, u32[]{:S(2)}) collective-permute-start(f32[32,480]{1,0:T(8,128)S(1)} %get-tuple-element.11.refs_0_), channel_id=1, source_target_pairs={{0,6},{2,4},{4,2},{6,0},{8,14},{10,12},{12,10},{14,8},{1,7},{3,5},... | collective-permute-start | bytes 184328 | tf_op jit(solution)/shard_map/ppermute | solution.py:195
  27.9 8.3 %collective-permute-start.7 = (f32[32,480]{1,0:T(8,128)S(1)}, f32[32,480]{1,0:T(8,128)S(1)}, u32[]{:S(2)}, u32[]{:S(2)}) collective-permute-start(f32[32,480]{1,0:T(8,128)S(1)} %get-tuple-element.11.refs_0_), channel_id=1, source_target_pairs={{0,8},{2,10},{4,12},{6,14},{8,0},{10,2},{12,4},{14,6},{1,9},{3,11}... | collective-permute-start | bytes 184328 | tf_op jit(solution)/shard_map/ppermute | solution.py:195
  29.5 6.1 %collective-permute-start.9 = (f32[32,480]{1,0:T(8,128)S(1)}, f32[32,480]{1,0:T(8,128)S(1)}, u32[]{:S(2)}, u32[]{:S(2)}) collective-permute-start(f32[32,480]{1,0:T(8,128)S(1)} %get-tuple-element.11.refs_0_), channel_id=1, source_target_pairs={{0,12},{2,14},{4,8},{6,10},{8,4},{10,6},{12,0},{14,2},{1,13},{3,15... | collective-permute-start | bytes 184328 | tf_op jit(solution)/shard_map/ppermute | solution.py:195
  35.6 7.5 %collective-permute-start.10 = (f32[32,480]{1,0:T(8,128)S(1)}, f32[32,480]{1,0:T(8,128)S(1)}, u32[]{:S(2)}, u32[]{:S(2)}) collective-permute-start(f32[32,480]{1,0:T(8,128)S(1)} %collective-permute-done.9.refs_1_), channel_id=1, source_target_pairs={{0,2},{2,0},{4,6},{6,4},{8,10},{10,8},{12,14},{14,12},{1,3},{3,1},... | collective-permute-start | bytes 184328 | tf_op jit(solution)/shard_map/ppermute | solution.py:195
  36.1 7.0 %collective-permute-start.8 = (f32[32,480]{1,0:T(8,128)S(1)}, f32[32,480]{1,0:T(8,128)S(1)}, u32[]{:S(2)}, u32[]{:S(2)}) collective-permute-start(f32[32,480]{1,0:T(8,128)S(1)} %collective-permute-done.7.refs_0_), channel_id=1, source_target_pairs={{0,2},{2,0},{4,6},{6,4},{8,10},{10,8},{12,14},{14,12},{1,3},{3,1},... | collective-permute-start | bytes 184328 | tf_op jit(solution)/shard_map/ppermute | solution.py:195
  45.0 3.6 %collective-permute-start.14 = (f32[544,128]{1,0:T(8,128)S(1)}, f32[544,128]{1,0:T(8,128)S(1)}, u32[]{:S(2)}, u32[]{:S(2)}) collective-permute-start(f32[544,128]{1,0:T(8,128)S(1)} %score.7.mine_ref), channel_id=1, source_target_pairs={{0,1},{1,0},{2,3},{3,2},{4,5},{5,4},{6,7},{7,6},{8,9},{9,8},{10,11... | collective-permute-start | bytes 835592 | tf_op jit(solution)/shard_map/ppermute | solution.py:198
  45.0 1.6 %collective-permute-start.6 = (f32[32,256]{1,0:T(8,128)S(1)}, f32[32,256]{1,0:T(8,128)S(1)}, u32[]{:S(2)}, u32[]{:S(2)}) collective-permute-start(f32[32,256]{1,0:T(8,128)S(1)} %get-tuple-element.13), channel_id=1, source_target_pairs={{0,1},{1,0},{2,3},{3,2},{4,5},{5,4},{6,7},{7,6},{8,9},{9,8},{10,11... | collective-permute-start | bytes 98312 | tf_op jit(solution)/shard_map/ppermute | solution.py:198

commit v3 on v2

--- a/solution.py
+++ b/solution.py
@@ -48,18 +48,46 @@
     return part, part_b, total
 
 
-def gradient_kernel(shares, place_ref, geno_ref, counts_ref, freqs_ref, grad_ref, excess_ref):
+def gradient_kernel(shares, far, place_ref, geno_ref, counts_ref, freqs_ref, grad_ref, excess_ref, *copies):
     half_rows = excess_ref.shape[0]
     width = freqs_ref.shape[1]
     anc = freqs_ref.shape[0]
-    start = place_ref[0] * half_rows
+    own_half = place_ref[0] // shares
+    start = (1 - own_half if far else own_half) * half_rows
+    if far:
+        geno_buf, counts_buf, sems = copies
+        pieces = sems.shape[1]
+        size = half_rows // pieces
+        moves = []
+        for i in range(pieces):
+            first = pl.multiple_of(start + i * size, LANES)
+            rows = pl.ds(i * size, size)
+            moves.append(
+                (
+                    pltpu.make_async_copy(
+                        counts_ref.at[:, pl.ds(first, size)], counts_buf.at[:, rows], sems.at[0, i]
+                    ),
+                    pltpu.make_async_copy(
+                        geno_ref.at[pl.ds(first, size), :], geno_buf.at[rows, :], sems.at[1, i]
+                    ),
+                )
+            )
+            for copy in moves[-1]:
+                copy.start()
     freqs = freqs_ref[...]
     table = count_table(freqs)
     for row in range(0, half_rows, LANES):
-        first = pl.multiple_of(start + row, LANES)
-        counts = counts_ref[:, pl.ds(first, LANES)].astype(F32).astype(BF16)
-        dosage = geno_ref[pl.ds(first, LANES), :].astype(F32)
-        part, _, total = ratio_parts(counts, dosage, table)
+        if far:
+            if row % size == 0:
+                for copy in moves[row // size]:
+                    copy.wait()
+            counts = counts_buf[:, pl.ds(row, LANES)]
+            dosage = geno_buf[pl.ds(row, LANES), :]
+        else:
+            first = pl.multiple_of(start + row, LANES)
+            counts = counts_ref[:, pl.ds(first, LANES)]
+            dosage = geno_ref[pl.ds(first, LANES), :]
+        part, _, total = ratio_parts(counts.astype(F32).astype(BF16), dosage.astype(F32), table)
         high, low = split(part * total)
         excess_ref[pl.ds(row, LANES), :width] = high
         excess_ref[pl.ds(row, LANES), width:] = low
@@ -68,10 +96,10 @@
     grads = grads[:anc] + grads[anc:]
     share = half_rows // shares
     for c in range(shares):
-        grad_ref[c ^ place_ref[1]] = grads[:, c * share : (c + 1) * share]
-
-
-def sums_kernel(geno_ref, counts_ref, freqs_ref, resid_ref, sums_ref, traits_ref, own_ref, parts_ref):
+        grad_ref[c ^ (place_ref[0] % shares)] = grads[:, c * share : (c + 1) * share]
+
+
+def sums_kernel(place_ref, geno_ref, counts_ref, freqs_ref, resid_ref, sums_ref, traits_ref, own_ref, parts_ref):
     rows, width = geno_ref.shape
     table = count_table(freqs_ref[...])
     for row in range(0, rows, LANES):
@@ -92,11 +120,8 @@
         own_ref[c] = counts[:, c * share : (c + 1) * share]
 
 
-def share_kernel(variants, n_parts, own_ref, counts_ref, *refs):
-    parts, (q_ref, grad_ref) = refs[:n_parts], refs[n_parts:]
-    gradient = parts[0][...]
-    for part in parts[1:]:
-        gradient = gradient + part[...]
+def share_kernel(variants, own_ref, counts_ref, total_ref, q_ref, grad_ref):
+    gradient = total_ref[...]
     counts = counts_ref[own_ref[0]]
     fractions = counts / jnp.sum(counts, axis=0, keepdims=True)
     second = 2.0 * variants - jnp.sum(fractions * gradient, axis=0, keepdims=True)
@@ -105,8 +130,8 @@
     grad_ref[...] = gradient / math.sqrt(variants)
 
 
-def score_kernel(n_shares, fresh, own_ref, *refs):
-    q_refs, refs = refs[:n_shares], refs[n_shares:]
+def score_kernel(shares, fresh, own_ref, *refs):
+    q_refs, refs = refs[: len(shares)], refs[len(shares) :]
     geno_ref, traits_ref, freqs_ref = refs[:3]
     total_ref = None if fresh else refs[3]
     out_ref = refs[-1]
@@ -115,10 +140,10 @@
     anc, width = freqs_ref.shape
     traits = traits_ref.shape[1]
     score, info = None, None
-    for c in range(n_shares):
-        q_new = q_refs[c][...]
+    for m, q_ref in zip(shares, q_refs):
+        q_new = q_ref[...]
         rows = q_new.shape[1]
-        owner = own_ref[c]
+        owner = own_ref[0] ^ m
         q_high, q_low = split(q_new)
         recon = dot(jnp.concatenate([q_high, q_low, q_high], axis=0), f_three, TN)
         dosage = geno_ref[pl.ds(pl.multiple_of(owner * rows, 16), rows), :].astype(F32)
@@ -147,7 +172,7 @@
     out_ref[anc * traits :] = info
 
 
-def final_kernel(mine_ref, other_ref, out_ref):
+def final_kernel(place_ref, mine_ref, other_ref, out_ref):
     anc, traits, width = out_ref.shape
     total = mine_ref[...] + other_ref[...]
     scale = jnp.sqrt(total[anc * traits :] + 1e-06)
@@ -166,18 +191,22 @@
 IN_VMEM = pl.BlockSpec(memory_space=pltpu.VMEM)
 
 
-def call(kernel, name, n_scalars, args, outs, scratch=(), cost=2000, aliases=None):
-    args = args[:n_scalars] + tuple(pltpu.with_memory_space_constraint(x, VMEM) for x in args[n_scalars:])
+def call(kernel, name, args, outs, scratch=(), cost=2000, aliases=None, raw=()):
+    specs = [SCALARS]
+    held = [args[0]]
+    for at, x in enumerate(args[1:], 1):
+        specs.append(pl.BlockSpec(memory_space=pl.ANY) if at in raw else IN_VMEM)
+        held.append(x if at in raw else pltpu.with_memory_space_constraint(x, VMEM))
     return pl.pallas_call(
         kernel,
-        in_specs=[SCALARS] * n_scalars + [IN_VMEM] * (len(args) - n_scalars),
+        in_specs=specs,
         out_specs=[IN_VMEM] * len(outs),
         out_shape=[VMEM(s, F32) for s in outs],
         scratch_shapes=list(scratch),
         input_output_aliases=aliases or {},
         cost_estimate=pl.CostEstimate(flops=cost * 400_000, bytes_accessed=0, transcendentals=0),
         name=name,
-    )(*args)
+    )(*held)
 
 
 def shards(genotypes, ancestry_counts, residuals, freqs):
@@ -189,88 +218,94 @@
     traits = residuals.shape[1]
     sample_count = rows * lax.axis_size("smp")
     variants = width * var_count
-    place = lax.axis_index("var").astype(jnp.int32)
-
-    def move(x, m):
-        return lax.ppermute(x, "var", [(i, i ^ m) for i in range(var_count)])
-
-    def swap(x):
-        return lax.ppermute(x, "smp", [(0, 1), (1, 0)])
-
-    geno = pltpu.with_memory_space_constraint(genotypes, VMEM)
-    counts = pltpu.with_memory_space_constraint(ancestry_counts.T, VMEM)
+    place = lax.axis_index("var").astype(jnp.int32).reshape(1)
+
+    def move(x, m, name):
+        with jax.named_scope(name):
+            return lax.ppermute(x, "var", [(i, i ^ m) for i in range(var_count)])
+
+    def swap(x, name):
+        with jax.named_scope(name):
+            return lax.ppermute(x, "smp", [(0, 1), (1, 0)])
+
+    counts = ancestry_counts.T
     resid = residuals.T
-
-    def gradients(which, name):
-        scalars = jnp.stack([which, place % half])
-        (grads,) = call(
-            functools.partial(gradient_kernel, half),
-            name,
-            1,
-            (scalars, geno, counts, freqs),
-            [(half, anc, share)],
-            [VMEM((rows // 2, 2 * width), BF16)],
-        )
-        return grads
-
-    far = gradients(1 - place // half, "grad_far")
-    far_even = far.reshape(half // 2, 2, anc, share)
-    got = move(far_even[:, 1], 1)
-    near = gradients(place // half, "grad_near")
-    arrived = [near[0]] + [move(near[m], m) for m in range(1, half)]
-    combined = far_even[:, 0] + got
-    arrived += [move(combined[m], half + 2 * m) for m in range(half // 2)]
+    half_rows = rows // 2
+    excess = VMEM((half_rows, 2 * width), BF16)
+    pieces = 3 if half_rows % (3 * LANES) == 0 else 1
+
+    (far,) = call(
+        functools.partial(gradient_kernel, half, True),
+        "grad_far",
+        (place, genotypes, counts, freqs),
+        [(half, anc, share)],
+        [
+            excess,
+            VMEM((half_rows, width), BF16),
+            VMEM((anc, half_rows), jnp.int32),
+            pltpu.SemaphoreType.DMA((2, pieces)),
+        ],
+        raw=(1, 2),
+    )
+    (near,) = call(
+        functools.partial(gradient_kernel, half, False),
+        "grad_near",
+        (place, genotypes, counts, freqs),
+        [(half, anc, share)],
+        [excess],
+    )
+    slots = {half + c: far[c] for c in range(half)} | {c: near[c] for c in range(half)}
+    bit = 1
+    while bit < var_count:
+        for m in reversed(range(bit, var_count, 2 * bit)):
+            slots[m ^ bit] = slots[m ^ bit] + move(slots[m], bit, f"rs{m}")
+        bit *= 2
 
     sums, trait_parts, count_parts = call(
         sums_kernel,
         "sums",
-        0,
-        (geno, counts, freqs, resid),
+        (place, genotypes, counts, freqs, resid),
         [(anc, 2 * width), (var_count, traits, share), (var_count, anc, share)],
         [VMEM((2 * rows, 2 * width), BF16)],
     )
-    sums_all = sums + swap(sums)
+    sums_all = sums + swap(sums, "swap_sums")
     freq_next, freq_gradient = update_freqs(
         freqs, sums_all[:, :width], sums_all[:, width:], sample_count
     )
 
-    own = place.reshape(1)
     q_new, own_gradient = call(
-        functools.partial(share_kernel, variants, len(arrived)),
+        functools.partial(share_kernel, variants),
         "share",
-        1,
-        (own, count_parts, *arrived),
+        (place, count_parts, slots[0]),
         [(anc, share), (anc, share)],
         cost=500,
     )
 
-    shares = {m: move(q_new, m) for m in range(2, var_count, 2)}
-    shares[1] = move(q_new, 1)
-    for m in range(3, half, 2):
-        shares[m] = move(q_new, m)
-    for m in range(half + 1, var_count, 2):
-        shares[m] = move(shares[m - 1], 1)
-    shares[0] = q_new
+    shares = {0: q_new}
+    bit = half
+    while bit:
+        for m in range(bit, var_count, 2 * bit):
+            shares[m] = move(shares[m ^ bit], bit, f"ag{m}")
+        bit //= 2
 
     def scores(ms, total):
-        owners = jnp.stack([place ^ m for m in ms])
-        inputs = (geno, trait_parts, freqs) + (() if total is None else (total,))
+        inputs = (genotypes, trait_parts, freqs) + (() if total is None else (total,))
         (out,) = call(
-            functools.partial(score_kernel, len(ms), total is None),
+            functools.partial(score_kernel, ms, total is None),
             "score",
-            1,
-            (owners, *[shares[m] for m in ms], *inputs),
+            (place, *[shares[m] for m in ms], *inputs),
             [((anc * traits + anc), width)],
             cost=700 * len(ms),
             aliases=None if total is None else {len(ms) + 4: 0},
         )
         return out
 
-    order = [0, 1] + list(range(2, half)) + list(range(half, var_count, 2)) + list(range(half + 1, var_count, 2))
     total = None
-    for at in range(0, var_count, 2):
-        total = scores(order[at : at + 2], total)
-    (z_score,) = call(final_kernel, "final", 0, (total, swap(total)), [(anc, traits, width)], cost=300)
+    for ms in ([0], [2], [1], [3], [4], [6], [5], [7]) if var_count == 8 else [[m] for m in range(var_count)]:
+        total = scores(tuple(ms), total)
+    (z_score,) = call(
+        final_kernel, "final", (place, total, swap(total, "swap_score")), [(anc, traits, width)], cost=300
+    )
     return (q_new.T, own_gradient.T, freq_next, freq_gradient, z_score)
 
 

time: 49.6 us -> 42.3 us (0.85)
  waiting for transfers between devices: 8.32 us -> 3.29 us
  starting transfers between devices: 19.1 us -> 23.1 us
  other arithmetic: 3.68 us -> 0.68 us
  local copies, waits for them, and re-layouts: 4.33 us -> 2.72 us
  Pallas kernels: 13 us -> 11.4 us
    ppermute x13 -> x14, waiting for transfers between devices: 7.22 us -> 2.19 us  [move(): return lax.ppermute(x, 'var', [(i, i ^ m) for i in range(var_count)])]
    ppermute x13 -> x14, starting transfers between devices: 18.5 us -> 22.6 us  [move(): return lax.ppermute(x, 'var', [(i, i ^ m) for i in range(var_count)])]
    another operation x5 -> x0, other arithmetic: 3.03 us -> none  [the longest x4 2.43 us: scores(): owners = jnp.stack([place ^ m for m in ms])]
    pallas_call x9 -> x13, Pallas kernels: 13 us -> 11.4 us  [call(): pl.pallas_call(kernel, in_specs=specs, out_specs=[IN_VMEM] * len(outs), o...]
    unnamed x11 -> x13, local copies, waits for them, and re-layouts: 4.29 us -> 2.7 us
  transfers between devices with their start and end apart: 15 -> 16, of which waited for: 4 -> 5; matrix products, arithmetic and copies ran while one was open for 9% -> 5% of each run, Pallas kernels for 19% -> 19%
where the time goes in v3:
time: 42.3 us; the launch traced here: 42.1 us
  starting transfers between devices  23.1 us (55%)
  Pallas kernels  11.4 us (27%)
  waiting for transfers between devices  3.29 us (8%)
  local copies, waits for them, and re-layouts  2.72 us (6%)
  between operations  0.84 us (2%)
  other arithmetic  0.68 us (2%)
    ppermute x14, starting transfers between devices, move(): return lax.ppermute(x, 'var', [(i, i ^ m) for i in range(var_count)])  22.6 us
    pallas_call x13, Pallas kernels, call(): pl.pallas_call(kernel, in_specs=specs, out_specs=[IN_VMEM] * len(outs), o...  11.4 us
    unnamed x13, local copies, waits for them, and re-layouts  2.7 us
    ppermute x14, waiting for transfers between devices, move(): return lax.ppermute(x, 'var', [(i, i ^ m) for i in range(var_count)])  2.19 us
    ppermute x2, waiting for transfers between devices, swap(): return lax.ppermute(x, 'smp', [(0, 1), (1, 0)])  1.1 us
  transfers between devices with their start and end apart: 16, of which 5 were waited for; matrix products, arithmetic and copies ran while one was open for 5% of the time, Pallas kernels for 19%

profile of v3, /device:TPU:0, one launch (start us, length us, event | category | flops | bytes accessed | tf_op | source)
XLA Modules:
  0.0 42.1 jit_solution(10546381917264747817)
XLA Ops:
  0.6 0.0 copy-start.1
  0.6 0.7 %copy-done.1 = f32[32,128]{1,0:T(8,128)S(1)} copy-done((f32[32,128]{1,0:T(8,128)S(1)}, f32[32,128]{1,0:T(8,128)}, u32[]{:S(2)}) %copy-start.1) | copy-done | bytes 16408
  1.4 0.0 copy-start
  1.4 0.0 copy-start.3
  1.4 2.5 %grad_far.1 = f32[4,32,480]{2,1,0:T(8,128)S(1)} custom-call(s32[1]{0:T(128)} %bitcast.place_ref.own_ref, bf16[3840,128]{1,0:T(8,128)(2,1)} %refs_1_.15, s32[32,3840]{1,0:T(8,128)} %bitcast.37, f32[32,128]{1,0:T(8,128)S(1)} %copy-done.1), custom_call_target="tpu_custom_call" | custom-call | flops 800000000 | tf_op jit(solution)/shard_map/grad_far/pallas_call | solution.py:200
  3.9 3.0 %collective-permute-start.4 = (f32[32,480]{1,0:T(8,128)S(1)}, f32[32,480]{1,0:T(8,128)S(1)}, u32[]{:S(2)}, u32[]{:S(2)}) collective-permute-start(f32[32,480]{1,0:T(8,128)S(1)} %get-tuple-element.18), channel_id=1, source_target_pairs={{0,2},{2,0},{4,6},{6,4},{8,10},{10,8},{12,14},{14,12},{1,3},{3,1},... | collective-permute-start | bytes 184328 | tf_op jit(solution)/shard_map/rs7/ppermute | solution.py:225
  6.9 0.1 collective-permute-start.3
  7.0 0.0 copy-done
  7.0 0.0 copy-done.3
  7.0 1.0 %grad_near.1 = f32[4,32,480]{2,1,0:T(8,128)S(1)} custom-call(s32[1]{0:T(128)} %bitcast.place_ref.own_ref, bf16[3840,128]{1,0:T(8,128)(2,1)S(1)} %copy-done, s32[32,3840]{1,0:T(8,128)S(1)} %bitcast.38, f32[32,128]{1,0:T(8,128)S(1)} %copy-done.1), custom_call_target="tpu_custom_call" | custom-call | flops 800000000 | tf_op jit(solution)/shard_map/grad_near/pallas_call | solution.py:200
  8.0 2.0 %collective-permute-start.1 = (f32[32,480]{1,0:T(8,128)S(1)}, f32[32,480]{1,0:T(8,128)S(1)}, u32[]{:S(2)}, u32[]{:S(2)}) collective-permute-start(f32[32,480]{1,0:T(8,128)S(1)} %get-tuple-element.16), channel_id=1, source_target_pairs={{0,2},{2,0},{4,6},{6,4},{8,10},{10,8},{12,14},{14,12},{1,3},{3,1},... | collective-permute-start | bytes 184328 | tf_op jit(solution)/shard_map/rs3/ppermute | solution.py:225
  10.0 0.1 collective-permute-start
  10.1 0.0 collective-permute-done.4
  10.1 0.0 copy-start.4
  10.1 2.1 %collective-permute-start.5 = (f32[32,480]{1,0:T(8,128)S(1)}, f32[32,480]{1,0:T(8,128)S(1)}, u32[]{:S(2)}, u32[]{:S(2)}) collective-permute-start(f32[32,480]{1,0:T(8,128)S(1)} %fusion), channel_id=1, source_target_pairs={{0,4},{2,6},{4,0},{6,2},{8,12},{10,14},{12,8},{14,10},{1,5},{3,7},... | collective-permute-start | bytes 184328 | tf_op jit(solution)/shard_map/rs6/ppermute | solution.py:225
  12.2 0.8 %collective-permute-done.1 = f32[32,480]{1,0:T(8,128)S(1)} collective-permute-done((f32[32,480]{1,0:T(8,128)S(1)}, f32[32,480]{1,0:T(8,128)S(1)}, u32[]{:S(2)}, u32[]{:S(2)}) %collective-permute-start.1) | collective-permute-done | bytes 61472 | tf_op jit(solution)/shard_map/rs3/ppermute | solution.py:225
  13.0 1.8 %collective-permute-start.2 = (f32[32,480]{1,0:T(8,128)S(1)}, f32[32,480]{1,0:T(8,128)S(1)}, u32[]{:S(2)}, u32[]{:S(2)}) collective-permute-start(f32[32,480]{1,0:T(8,128)S(1)} %fusion.3), channel_id=1, source_target_pairs={{0,4},{2,6},{4,0},{6,2},{8,12},{10,14},{12,8},{14,10},{1,5},{3,7},... | collective-permute-start | bytes 184328 | tf_op jit(solution)/shard_map/rs2/ppermute | solution.py:225
  14.8 0.0 collective-permute-done.3
  14.8 0.0 collective-permute-done.5
  14.9 3.1 %collective-permute-start.6 = (f32[32,480]{1,0:T(8,128)S(1)}, f32[32,480]{1,0:T(8,128)S(1)}, u32[]{:S(2)}, u32[]{:S(2)}) collective-permute-start(f32[32,480]{1,0:T(8,128)S(1)} %fusion.2), channel_id=1, source_target_pairs={{0,8},{2,10},{4,12},{6,14},{8,0},{10,2},{12,4},{14,6},{1,9},{3,11}... | collective-permute-start | bytes 184328 | tf_op jit(solution)/shard_map/rs4/ppermute | solution.py:225
  18.0 0.0 copy-done.4
  18.0 2.4 %sums.1 = (f32[32,256]{1,0:T(8,128)S(1)}, f32[8,16,480]{2,1,0:T(8,128)S(1)}, f32[8,32,480]{2,1,0:T(8,128)S(1)}) custom-call(s32[1]{0:T(128)} %bitcast.place_ref.own_ref, bf16[3840,128]{1,0:T(8,128)(2,1)S(1)} %copy-done, s32[32,3840]{1,0:T(8,128)S(1)} %bitcast.39, f32[32,128]{1,0:T(8,128)S(1)} %copy-done.1, s32[16,3840]{1,0:T(8,128)S(1)} %bitcast.40), custom_call_target="tpu_custom_call" | custom-call | flops 800000000 | tf_op jit(solution)/shard_map/sums/pallas_call | solution.py:200
  20.3 0.0 collective-permute-done
  20.3 0.0 collective-permute-done.2
  20.4 0.0 collective-permute-done.6
  20.4 0.0 copy-start.2
  20.4 0.1 share.1
  20.5 1.8 %collective-permute-start.12 = (f32[32,480]{1,0:T(8,128)S(1)}, f32[32,480]{1,0:T(8,128)S(1)}, u32[]{:S(2)}, u32[]{:S(2)}) collective-permute-start(f32[32,480]{1,0:T(8,128)S(1)} %get-tuple-element.11.refs_0_), channel_id=1, source_target_pairs={{0,4},{2,6},{4,0},{6,2},{8,12},{10,14},{12,8},{14,10},{1,5},{3,7},... | collective-permute-start | bytes 184328 | tf_op jit(solution)/shard_map/ag2/ppermute | solution.py:225
  22.3 3.3 %collective-permute-start.8 = (f32[32,480]{1,0:T(8,128)S(1)}, f32[32,480]{1,0:T(8,128)S(1)}, u32[]{:S(2)}, u32[]{:S(2)}) collective-permute-start(f32[32,480]{1,0:T(8,128)S(1)} %get-tuple-element.11.refs_0_), channel_id=1, source_target_pairs={{0,8},{2,10},{4,12},{6,14},{8,0},{10,2},{12,4},{14,6},{1,9},{3,11}... | collective-permute-start | bytes 184328 | tf_op jit(solution)/shard_map/ag4/ppermute | solution.py:225
  25.6 1.4 %collective-permute-start.14 = (f32[32,480]{1,0:T(8,128)S(1)}, f32[32,480]{1,0:T(8,128)S(1)}, u32[]{:S(2)}, u32[]{:S(2)}) collective-permute-start(f32[32,480]{1,0:T(8,128)S(1)} %get-tuple-element.11.refs_0_), channel_id=1, source_target_pairs={{0,2},{2,0},{4,6},{6,4},{8,10},{10,8},{12,14},{14,12},{1,3},{3,1},... | collective-permute-start | bytes 184328 | tf_op jit(solution)/shard_map/ag1/ppermute | solution.py:225
  27.0 0.0 collective-permute-done.12.refs_0_
  27.0 0.6 %collective-permute-start.13 = (f32[32,480]{1,0:T(8,128)S(1)}, f32[32,480]{1,0:T(8,128)S(1)}, u32[]{:S(2)}, u32[]{:S(2)}) collective-permute-start(f32[32,480]{1,0:T(8,128)S(1)} %collective-permute-done.12.refs_0_), channel_id=1, source_target_pairs={{0,2},{2,0},{4,6},{6,4},{8,10},{10,8},{12,14},{14,12},{1,3},{3,1},... | collective-permute-start | bytes 184328 | tf_op jit(solution)/shard_map/ag3/ppermute | solution.py:225
  27.6 0.9 %collective-permute-done.8.refs_0_ = f32[32,480]{1,0:T(8,128)S(1)} collective-permute-done((f32[32,480]{1,0:T(8,128)S(1)}, f32[32,480]{1,0:T(8,128)S(1)}, u32[]{:S(2)}, u32[]{:S(2)}) %collective-permute-start.8) | collective-permute-done | bytes 61472 | tf_op jit(solution)/shard_map/ag4/ppermute | solution.py:225
  28.5 0.4 collective-permute-start.9
  28.9 0.0 copy-done.2
  28.9 0.7 %score.8.refs_4_ = f32[544,128]{1,0:T(8,128)S(1)} custom-call(s32[1]{0:T(128)} %bitcast.place_ref.own_ref, f32[32,480]{1,0:T(8,128)S(1)} %get-tuple-element.11.refs_0_, bf16[3840,128]{1,0:T(8,128)(2,1)S(1)} %copy-done, f32[8,16,480]{2,1,0:T(8,128)S(1)} %get-tuple-element.14.refs_2_, f32[32,128]{1,0:T(8,128)S(1)} %copy-done.2), custom_call_target="tpu_custom_call" | custom-call | flops 280000000 | tf_op jit(solution)/shard_map/score/pallas_call | solution.py:200
  29.6 1.4 %collective-permute-start.11 = (f32[32,480]{1,0:T(8,128)S(1)}, f32[32,480]{1,0:T(8,128)S(1)}, u32[]{:S(2)}, u32[]{:S(2)}) collective-permute-start(f32[32,480]{1,0:T(8,128)S(1)} %collective-permute-done.8.refs_0_), channel_id=1, source_target_pairs={{0,2},{2,0},{4,6},{6,4},{8,10},{10,8},{12,14},{14,12},{1,3},{3,1},... | collective-permute-start | bytes 184328 | tf_op jit(solution)/shard_map/ag5/ppermute | solution.py:225
  31.0 0.7 %score.9.refs_4_ = f32[544,128]{1,0:T(8,128)S(1)} custom-call(s32[1]{0:T(128)} %bitcast.place_ref.own_ref, f32[32,480]{1,0:T(8,128)S(1)} %collective-permute-done.12.refs_0_, bf16[3840,128]{1,0:T(8,128)(2,1)S(1)} %copy-done, f32[8,16,480]{2,1,0:T(8,128)S(1)} %get-tuple-element.14.refs_2_, f32[32,128]{1,0:T(8,128)S(1)} %copy-done.2, ...), custom_call_target="tpu_custom_call", output_to_operand_aliasing={{}: (5, {})} | custom-call | flops 280000000 | tf_op jit(solution)/shard_map/score/pallas_call | solution.py:200
  31.7 0.0 collective-permute-done.14.refs_0_
  31.7 0.7 %score.10.refs_4_ = f32[544,128]{1,0:T(8,128)S(1)} custom-call(s32[1]{0:T(128)} %bitcast.place_ref.own_ref, f32[32,480]{1,0:T(8,128)S(1)} %collective-permute-done.14.refs_0_, bf16[3840,128]{1,0:T(8,128)(2,1)S(1)} %copy-done, f32[8,16,480]{2,1,0:T(8,128)S(1)} %get-tuple-element.14.refs_2_, f32[32,128]{1,0:T(8,128)S(1)} %copy-done.2, ...), custom_call_target="tpu_custom_call", output_to_operand_aliasing={{}: (5, {})} | custom-call | flops 280000000 | tf_op jit(solution)/shard_map/score/pallas_call | solution.py:200
  32.4 0.4 collective-permute-done.9.refs_0_
  32.8 1.4 %collective-permute-start.10 = (f32[32,480]{1,0:T(8,128)S(1)}, f32[32,480]{1,0:T(8,128)S(1)}, u32[]{:S(2)}, u32[]{:S(2)}) collective-permute-start(f32[32,480]{1,0:T(8,128)S(1)} %collective-permute-done.9.refs_0_), channel_id=1, source_target_pairs={{0,2},{2,0},{4,6},{6,4},{8,10},{10,8},{12,14},{14,12},{1,3},{3,1},... | collective-permute-start | bytes 184328 | tf_op jit(solution)/shard_map/ag7/ppermute | solution.py:225
  34.2 0.0 collective-permute-done.13.refs_0_
  34.2 0.7 %score.11.refs_4_ = f32[544,128]{1,0:T(8,128)S(1)} custom-call(s32[1]{0:T(128)} %bitcast.place_ref.own_ref, f32[32,480]{1,0:T(8,128)S(1)} %collective-permute-done.13.refs_0_, bf16[3840,128]{1,0:T(8,128)(2,1)S(1)} %copy-done, f32[8,16,480]{2,1,0:T(8,128)S(1)} %get-tuple-element.14.refs_2_, f32[32,128]{1,0:T(8,128)S(1)} %copy-done.2, ...), custom_call_target="tpu_custom_call", output_to_operand_aliasing={{}: (5, {})} | custom-call | flops 280000000 | tf_op jit(solution)/shard_map/score/pallas_call | solution.py:200
  34.9 0.7 %score.12.refs_4_ = f32[544,128]{1,0:T(8,128)S(1)} custom-call(s32[1]{0:T(128)} %bitcast.place_ref.own_ref, f32[32,480]{1,0:T(8,128)S(1)} %collective-permute-done.8.refs_0_, bf16[3840,128]{1,0:T(8,128)(2,1)S(1)} %copy-done, f32[8,16,480]{2,1,0:T(8,128)S(1)} %get-tuple-element.14.refs_2_, f32[32,128]{1,0:T(8,128)S(1)} %copy-done.2, ...), custom_call_target="tpu_custom_call", output_to_operand_aliasing={{}: (5, {})} | custom-call | flops 280000000 | tf_op jit(solution)/shard_map/score/pallas_call | solution.py:200
  35.6 0.7 %score.13.refs_4_ = f32[544,128]{1,0:T(8,128)S(1)} custom-call(s32[1]{0:T(128)} %bitcast.place_ref.own_ref, f32[32,480]{1,0:T(8,128)S(1)} %collective-permute-done.9.refs_0_, bf16[3840,128]{1,0:T(8,128)(2,1)S(1)} %copy-done, f32[8,16,480]{2,1,0:T(8,128)S(1)} %get-tuple-element.14.refs_2_, f32[32,128]{1,0:T(8,128)S(1)} %copy-done.2, ...), custom_call_target="tpu_custom_call", output_to_operand_aliasing={{}: (5, {})} | custom-call | flops 280000000 | tf_op jit(solution)/shard_map/score/pallas_call | solution.py:200
  36.3 0.0 collective-permute-done.11.refs_0_
  36.3 0.7 %score.14.refs_4_ = f32[544,128]{1,0:T(8,128)S(1)} custom-call(s32[1]{0:T(128)} %bitcast.place_ref.own_ref, f32[32,480]{1,0:T(8,128)S(1)} %collective-permute-done.11.refs_0_, bf16[3840,128]{1,0:T(8,128)(2,1)S(1)} %copy-done, f32[8,16,480]{2,1,0:T(8,128)S(1)} %get-tuple-element.14.refs_2_, f32[32,128]{1,0:T(8,128)S(1)} %copy-done.2, ...), custom_call_target="tpu_custom_call", output_to_operand_aliasing={{}: (5, {})} | custom-call | flops 280000000 | tf_op jit(solution)/shard_map/score/pallas_call | solution.py:200
  37.0 0.1 collective-permute-done.10.refs_0_
  37.1 0.7 %score.15.mine_ref = f32[544,128]{1,0:T(8,128)S(1)} custom-call(s32[1]{0:T(128)} %bitcast.place_ref.own_ref, f32[32,480]{1,0:T(8,128)S(1)} %collective-permute-done.10.refs_0_, bf16[3840,128]{1,0:T(8,128)(2,1)S(1)} %copy-done, f32[8,16,480]{2,1,0:T(8,128)S(1)} %get-tuple-element.14.refs_2_, f32[32,128]{1,0:T(8,128)S(1)} %copy-done.2, ...), custom_call_target="tpu_custom_call", output_to_operand_aliasing={{}: (5, {})} | custom-call | flops 280000000 | tf_op jit(solution)/shard_map/score/pallas_call | solution.py:200
  37.7 0.1 collective-permute-start.15
  37.8 0.5 %collective-permute-start.7 = (f32[32,256]{1,0:T(8,128)S(1)}, f32[32,256]{1,0:T(8,128)S(1)}, u32[]{:S(2)}, u32[]{:S(2)}) collective-permute-start(f32[32,256]{1,0:T(8,128)S(1)} %get-tuple-element.13), channel_id=1, source_target_pairs={{0,1},{1,0},{2,3},{3,2},{4,5},{5,4},{6,7},{7,6},{8,9},{9,8},{10,11... | collective-permute-start | bytes 98312 | tf_op jit(solution)/shard_map/swap_sums/ppermute | solution.py:229
  38.3 1.1 %collective-permute-done.7 = f32[32,256]{1,0:T(8,128)S(1)} collective-permute-done((f32[32,256]{1,0:T(8,128)S(1)}, f32[32,256]{1,0:T(8,128)S(1)}, u32[]{:S(2)}, u32[]{:S(2)}) %collective-permute-start.7) | collective-permute-done | bytes 32800 | tf_op jit(solution)/shard_map/swap_sums/ppermute | solution.py:229
  39.4 0.6 %slice_multiply_fusion = (f32[32,128]{1,0:T(8,128)}, f32[32,128]{1,0:T(8,128)}) fusion(f32[32,256]{1,0:T(8,128)S(1)} %add.37, f32[32,128]{1,0:T(8,128)S(1)} %copy-done.2), kind=kLoop, calls=%fused_computation.16 | loop fusion | flops 28672 | bytes 81920 | tf_op jit(solution)/shard_map/div | solution.py:185
  40.0 0.6 %copy.23 = f32[480,32]{0,1:T(8,128)} copy(f32[480,32]{0,1:T(8,128)S(1)} %bitcast.35) | data formatting | bytes 122880
  40.7 0.6 %copy.24 = f32[480,32]{0,1:T(8,128)} copy(f32[480,32]{0,1:T(8,128)S(1)} %bitcast.36) | data formatting | bytes 122880
  41.3 0.0 collective-permute-done.15.other_ref
  41.3 0.1 final.1
  41.4 0.7 %copy.25 = f32[32,16,128]{2,1,0:T(8,128)} copy(f32[32,16,128]{2,1,0:T(8,128)S(1)} %final.1) | data formatting | bytes 524288
  (7 shorter events, 0.1 us)
Async XLA Ops:
  0.6 0.7 %copy-start.1 = (f32[32,128]{1,0:T(8,128)S(1)}, f32[32,128]{1,0:T(8,128)}, u32[]{:S(2)}) copy-start(f32[32,128]{1,0:T(8,128)} %refs_3_.15) | copy-start | bytes 49156
  1.4 5.6 %copy-start = (bf16[3840,128]{1,0:T(8,128)(2,1)S(1)}, bf16[3840,128]{1,0:T(8,128)(2,1)}, u32[]{:S(2)}) copy-start(bf16[3840,128]{1,0:T(8,128)(2,1)} %refs_1_.15) | copy-start | bytes 2949124
  1.4 5.6 %copy-start.3 = (s32[3840,32]{0,1:T(8,128)S(1)}, s32[3840,32]{0,1:T(8,128)}, u32[]{:S(2)}) copy-start(s32[3840,32]{0,1:T(8,128)} %param.5) | copy-start | bytes 1474564
  3.9 6.2 %collective-permute-start.4 = (f32[32,480]{1,0:T(8,128)S(1)}, f32[32,480]{1,0:T(8,128)S(1)}, u32[]{:S(2)}, u32[]{:S(2)}) collective-permute-start(f32[32,480]{1,0:T(8,128)S(1)} %get-tuple-element.18), channel_id=1, source_target_pairs={{0,2},{2,0},{4,6},{6,4},{8,10},{10,8},{12,14},{14,12},{1,3},{3,1},... | collective-permute-start | bytes 184328 | tf_op jit(solution)/shard_map/rs7/ppermute | solution.py:225
  6.9 8.0 %collective-permute-start.3 = (f32[32,480]{1,0:T(8,128)S(1)}, f32[32,480]{1,0:T(8,128)S(1)}, u32[]{:S(2)}, u32[]{:S(2)}) collective-permute-start(f32[32,480]{1,0:T(8,128)S(1)} %get-tuple-element.17), channel_id=1, source_target_pairs={{0,2},{2,0},{4,6},{6,4},{8,10},{10,8},{12,14},{14,12},{1,3},{3,1},... | collective-permute-start | bytes 184328 | tf_op jit(solution)/shard_map/rs5/ppermute | solution.py:225
  8.0 5.0 %collective-permute-start.1 = (f32[32,480]{1,0:T(8,128)S(1)}, f32[32,480]{1,0:T(8,128)S(1)}, u32[]{:S(2)}, u32[]{:S(2)}) collective-permute-start(f32[32,480]{1,0:T(8,128)S(1)} %get-tuple-element.16), channel_id=1, source_target_pairs={{0,2},{2,0},{4,6},{6,4},{8,10},{10,8},{12,14},{14,12},{1,3},{3,1},... | collective-permute-start | bytes 184328 | tf_op jit(solution)/shard_map/rs3/ppermute | solution.py:225
  10.0 10.4 %collective-permute-start = (f32[32,480]{1,0:T(8,128)S(1)}, f32[32,480]{1,0:T(8,128)S(1)}, u32[]{:S(2)}, u32[]{:S(2)}) collective-permute-start(f32[32,480]{1,0:T(8,128)S(1)} %get-tuple-element.15), channel_id=1, source_target_pairs={{0,2},{2,0},{4,6},{6,4},{8,10},{10,8},{12,14},{14,12},{1,3},{3,1},... | collective-permute-start | bytes 184328 | tf_op jit(solution)/shard_map/rs1/ppermute | solution.py:225
  10.1 7.9 %copy-start.4 = (s32[3840,16]{0,1:T(8,128)S(1)}, s32[3840,16]{0,1:T(8,128)}, u32[]{:S(2)}) copy-start(s32[3840,16]{0,1:T(8,128)} %param.6) | copy-start | bytes 737284
  10.1 4.7 %collective-permute-start.5 = (f32[32,480]{1,0:T(8,128)S(1)}, f32[32,480]{1,0:T(8,128)S(1)}, u32[]{:S(2)}, u32[]{:S(2)}) collective-permute-start(f32[32,480]{1,0:T(8,128)S(1)} %fusion), channel_id=1, source_target_pairs={{0,4},{2,6},{4,0},{6,2},{8,12},{10,14},{12,8},{14,10},{1,5},{3,7},... | collective-permute-start | bytes 184328 | tf_op jit(solution)/shard_map/rs6/ppermute | solution.py:225
  13.0 7.3 %collective-permute-start.2 = (f32[32,480]{1,0:T(8,128)S(1)}, f32[32,480]{1,0:T(8,128)S(1)}, u32[]{:S(2)}, u32[]{:S(2)}) collective-permute-start(f32[32,480]{1,0:T(8,128)S(1)} %fusion.3), channel_id=1, source_target_pairs={{0,4},{2,6},{4,0},{6,2},{8,12},{10,14},{12,8},{14,10},{1,5},{3,7},... | collective-permute-start | bytes 184328 | tf_op jit(solution)/shard_map/rs2/ppermute | solution.py:225
  14.9 5.5 %collective-permute-start.6 = (f32[32,480]{1,0:T(8,128)S(1)}, f32[32,480]{1,0:T(8,128)S(1)}, u32[]{:S(2)}, u32[]{:S(2)}) collective-permute-start(f32[32,480]{1,0:T(8,128)S(1)} %fusion.2), channel_id=1, source_target_pairs={{0,8},{2,10},{4,12},{6,14},{8,0},{10,2},{12,4},{14,6},{1,9},{3,11}... | collective-permute-start | bytes 184328 | tf_op jit(solution)/shard_map/rs4/ppermute | solution.py:225
  20.4 8.5 %copy-start.2 = (f32[32,128]{1,0:T(8,128)S(1)}, f32[32,128]{1,0:T(8,128)}, u32[]{:S(2)}) copy-start(f32[32,128]{1,0:T(8,128)} %refs_3_.15) | copy-start | bytes 49156
  20.5 6.5 %collective-permute-start.12 = (f32[32,480]{1,0:T(8,128)S(1)}, f32[32,480]{1,0:T(8,128)S(1)}, u32[]{:S(2)}, u32[]{:S(2)}) collective-permute-start(f32[32,480]{1,0:T(8,128)S(1)} %get-tuple-element.11.refs_0_), channel_id=1, source_target_pairs={{0,4},{2,6},{4,0},{6,2},{8,12},{10,14},{12,8},{14,10},{1,5},{3,7},... | collective-permute-start | bytes 184328 | tf_op jit(solution)/shard_map/ag2/ppermute | solution.py:225
  22.3 6.2 %collective-permute-start.8 = (f32[32,480]{1,0:T(8,128)S(1)}, f32[32,480]{1,0:T(8,128)S(1)}, u32[]{:S(2)}, u32[]{:S(2)}) collective-permute-start(f32[32,480]{1,0:T(8,128)S(1)} %get-tuple-element.11.refs_0_), channel_id=1, source_target_pairs={{0,8},{2,10},{4,12},{6,14},{8,0},{10,2},{12,4},{14,6},{1,9},{3,11}... | collective-permute-start | bytes 184328 | tf_op jit(solution)/shard_map/ag4/ppermute | solution.py:225
  25.6 6.1 %collective-permute-start.14 = (f32[32,480]{1,0:T(8,128)S(1)}, f32[32,480]{1,0:T(8,128)S(1)}, u32[]{:S(2)}, u32[]{:S(2)}) collective-permute-start(f32[32,480]{1,0:T(8,128)S(1)} %get-tuple-element.11.refs_0_), channel_id=1, source_target_pairs={{0,2},{2,0},{4,6},{6,4},{8,10},{10,8},{12,14},{14,12},{1,3},{3,1},... | collective-permute-start | bytes 184328 | tf_op jit(solution)/shard_map/ag1/ppermute | solution.py:225
  27.0 7.2 %collective-permute-start.13 = (f32[32,480]{1,0:T(8,128)S(1)}, f32[32,480]{1,0:T(8,128)S(1)}, u32[]{:S(2)}, u32[]{:S(2)}) collective-permute-start(f32[32,480]{1,0:T(8,128)S(1)} %collective-permute-done.12.refs_0_), channel_id=1, source_target_pairs={{0,2},{2,0},{4,6},{6,4},{8,10},{10,8},{12,14},{14,12},{1,3},{3,1},... | collective-permute-start | bytes 184328 | tf_op jit(solution)/shard_map/ag3/ppermute | solution.py:225
  28.5 4.3 %collective-permute-start.9 = (f32[32,480]{1,0:T(8,128)S(1)}, f32[32,480]{1,0:T(8,128)S(1)}, u32[]{:S(2)}, u32[]{:S(2)}) collective-permute-start(f32[32,480]{1,0:T(8,128)S(1)} %collective-permute-done.8.refs_0_), channel_id=1, source_target_pairs={{0,4},{2,6},{4,0},{6,2},{8,12},{10,14},{12,8},{14,10},{1,5},{3,7},... | collective-permute-start | bytes 184328 | tf_op jit(solution)/shard_map/ag6/ppermute | solution.py:225
  29.6 6.7 %collective-permute-start.11 = (f32[32,480]{1,0:T(8,128)S(1)}, f32[32,480]{1,0:T(8,128)S(1)}, u32[]{:S(2)}, u32[]{:S(2)}) collective-permute-start(f32[32,480]{1,0:T(8,128)S(1)} %collective-permute-done.8.refs_0_), channel_id=1, source_target_pairs={{0,2},{2,0},{4,6},{6,4},{8,10},{10,8},{12,14},{14,12},{1,3},{3,1},... | collective-permute-start | bytes 184328 | tf_op jit(solution)/shard_map/ag5/ppermute | solution.py:225
  32.8 4.3 %collective-permute-start.10 = (f32[32,480]{1,0:T(8,128)S(1)}, f32[32,480]{1,0:T(8,128)S(1)}, u32[]{:S(2)}, u32[]{:S(2)}) collective-permute-start(f32[32,480]{1,0:T(8,128)S(1)} %collective-permute-done.9.refs_0_), channel_id=1, source_target_pairs={{0,2},{2,0},{4,6},{6,4},{8,10},{10,8},{12,14},{14,12},{1,3},{3,1},... | collective-permute-start | bytes 184328 | tf_op jit(solution)/shard_map/ag7/ppermute | solution.py:225
  37.7 3.6 %collective-permute-start.15 = (f32[544,128]{1,0:T(8,128)S(1)}, f32[544,128]{1,0:T(8,128)S(1)}, u32[]{:S(2)}, u32[]{:S(2)}) collective-permute-start(f32[544,128]{1,0:T(8,128)S(1)} %score.15.mine_ref), channel_id=1, source_target_pairs={{0,1},{1,0},{2,3},{3,2},{4,5},{5,4},{6,7},{7,6},{8,9},{9,8},{10,11... | collective-permute-start | bytes 835592 | tf_op jit(solution)/shard_map/swap_score/ppermute | solution.py:229
  37.8 1.6 %collective-permute-start.7 = (f32[32,256]{1,0:T(8,128)S(1)}, f32[32,256]{1,0:T(8,128)S(1)}, u32[]{:S(2)}, u32[]{:S(2)}) collective-permute-start(f32[32,256]{1,0:T(8,128)S(1)} %get-tuple-element.13), channel_id=1, source_target_pairs={{0,1},{1,0},{2,3},{3,2},{4,5},{5,4},{6,7},{7,6},{8,9},{9,8},{10,11... | collective-permute-start | bytes 98312 | tf_op jit(solution)/shard_map/swap_sums/ppermute | solution.py:229

commit v4 on v3

--- a/solution.py
+++ b/solution.py
@@ -7,6 +7,7 @@
 from jax.experimental import pallas as pl
 from jax.experimental.pallas import tpu as pltpu
 from jax.sharding import PartitionSpec as P
+
 
 F32 = jnp.float32
 BF16 = jnp.bfloat16
@@ -48,46 +49,16 @@
     return part, part_b, total
 
 
-def gradient_kernel(shares, far, place_ref, geno_ref, counts_ref, freqs_ref, grad_ref, excess_ref, *copies):
+def half_gradient(shares, place, start, geno_ref, counts_ref, freqs, grad_ref, excess_ref, before):
     half_rows = excess_ref.shape[0]
-    width = freqs_ref.shape[1]
-    anc = freqs_ref.shape[0]
-    own_half = place_ref[0] // shares
-    start = (1 - own_half if far else own_half) * half_rows
-    if far:
-        geno_buf, counts_buf, sems = copies
-        pieces = sems.shape[1]
-        size = half_rows // pieces
-        moves = []
-        for i in range(pieces):
-            first = pl.multiple_of(start + i * size, LANES)
-            rows = pl.ds(i * size, size)
-            moves.append(
-                (
-                    pltpu.make_async_copy(
-                        counts_ref.at[:, pl.ds(first, size)], counts_buf.at[:, rows], sems.at[0, i]
-                    ),
-                    pltpu.make_async_copy(
-                        geno_ref.at[pl.ds(first, size), :], geno_buf.at[rows, :], sems.at[1, i]
-                    ),
-                )
-            )
-            for copy in moves[-1]:
-                copy.start()
-    freqs = freqs_ref[...]
+    anc, width = freqs.shape
     table = count_table(freqs)
     for row in range(0, half_rows, LANES):
-        if far:
-            if row % size == 0:
-                for copy in moves[row // size]:
-                    copy.wait()
-            counts = counts_buf[:, pl.ds(row, LANES)]
-            dosage = geno_buf[pl.ds(row, LANES), :]
-        else:
-            first = pl.multiple_of(start + row, LANES)
-            counts = counts_ref[:, pl.ds(first, LANES)]
-            dosage = geno_ref[pl.ds(first, LANES), :]
-        part, _, total = ratio_parts(counts.astype(F32).astype(BF16), dosage.astype(F32), table)
+        before(row)
+        first = pl.multiple_of(start + row, LANES)
+        counts = counts_ref[:, pl.ds(first, LANES)].astype(F32).astype(BF16)
+        dosage = geno_ref[pl.ds(first, LANES), :].astype(F32)
+        part, _, total = ratio_parts(counts, dosage, table)
         high, low = split(part * total)
         excess_ref[pl.ds(row, LANES), :width] = high
         excess_ref[pl.ds(row, LANES), width:] = low
@@ -96,7 +67,52 @@
     grads = grads[:anc] + grads[anc:]
     share = half_rows // shares
     for c in range(shares):
-        grad_ref[c ^ (place_ref[0] % shares)] = grads[:, c * share : (c + 1) * share]
+        grad_ref[c ^ (place % shares)] = grads[:, c * share : (c + 1) * share]
+
+
+def far_kernel(
+    shares, place_ref, geno_hbm, counts_hbm, freqs_hbm, grad_ref, geno_ref, counts_ref, excess_ref, freqs_ref, sems
+):
+    half_rows = excess_ref.shape[0]
+    pieces = sems.shape[1] - 1
+    size = half_rows // pieces
+    place = place_ref[0]
+    own_half = place // shares
+    far = (1 - own_half) * half_rows
+    near = own_half * half_rows
+
+    def pair(first, count, at):
+        rows = pl.ds(pl.multiple_of(first, LANES), count)
+        return (
+            pltpu.make_async_copy(counts_hbm.at[:, rows], counts_ref.at[:, rows], sems.at[0, at]),
+            pltpu.make_async_copy(geno_hbm.at[rows, :], geno_ref.at[rows, :], sems.at[1, at]),
+        )
+
+    freqs_copy = pltpu.make_async_copy(freqs_hbm, freqs_ref, sems.at[2, 0])
+    freqs_copy.start()
+    moves = [pair(far + i * size, size, i) for i in range(pieces)]
+    moves.append(pair(near, half_rows, pieces))
+    for move in moves:
+        for copy in move:
+            copy.start()
+    freqs_copy.wait()
+
+    def before(row):
+        if row % size == 0:
+            for copy in moves[row // size]:
+                copy.wait()
+
+    half_gradient(shares, place, far, geno_ref, counts_ref, freqs_ref[...], grad_ref, excess_ref, before)
+    for copy in moves[pieces]:
+        copy.wait()
+
+
+def near_kernel(shares, place_ref, geno_ref, counts_ref, freqs_ref, grad_ref, excess_ref):
+    place = place_ref[0]
+    start = (place // shares) * excess_ref.shape[0]
+    half_gradient(
+        shares, place, start, geno_ref, counts_ref, freqs_ref[...], grad_ref, excess_ref, lambda row: None
+    )
 
 
 def sums_kernel(place_ref, geno_ref, counts_ref, freqs_ref, resid_ref, sums_ref, traits_ref, own_ref, parts_ref):
@@ -172,11 +188,46 @@
     out_ref[anc * traits :] = info
 
 
-def final_kernel(place_ref, mine_ref, other_ref, out_ref):
+def emit_kernel(
+    sample_count, place_ref, q_ref, grad_ref, sums_ref, other_ref, freqs_ref, q_out, grad_out, next_out, slope_out, next_ref, slope_ref, sems
+):
+    _, width = freqs_ref.shape
+    copies = [
+        pltpu.make_async_copy(q_ref, q_out, sems.at[0]),
+        pltpu.make_async_copy(grad_ref, grad_out, sems.at[1]),
+    ]
+    for copy in copies:
+        copy.start()
+    sums = sums_ref[...] + other_ref[...]
+    next_ref[...], slope_ref[...] = update_freqs(
+        freqs_ref[...], sums[:, :width], sums[:, width:], sample_count
+    )
+    copies += [
+        pltpu.make_async_copy(next_ref, next_out, sems.at[2]),
+        pltpu.make_async_copy(slope_ref, slope_out, sems.at[3]),
+    ]
+    for copy in copies[2:]:
+        copy.start()
+    for copy in copies:
+        copy.wait()
+
+
+def final_kernel(place_ref, mine_ref, other_ref, out_hbm, out_ref, sems):
     anc, traits, width = out_ref.shape
-    total = mine_ref[...] + other_ref[...]
-    scale = jnp.sqrt(total[anc * traits :] + 1e-06)
-    out_ref[...] = total[: anc * traits].reshape(anc, traits, width) / scale[:, None, :]
+    rows = pl.ds(anc * traits, anc)
+    scale = jnp.sqrt(mine_ref[rows] + other_ref[rows] + 1e-06)
+    pieces = sems.shape[0]
+    size = anc // pieces
+    copies = []
+    for i in range(pieces):
+        rows = pl.ds(i * size * traits, size * traits)
+        total = mine_ref[rows] + other_ref[rows]
+        at = pl.ds(i * size, size)
+        out_ref[at] = total.reshape(size, traits, width) / scale[i * size : (i + 1) * size, None, :]
+        copies.append(pltpu.make_async_copy(out_ref.at[at], out_hbm.at[at], sems.at[i]))
+        copies[-1].start()
+    for copy in copies:
+        copy.wait()
 
 
 def update_freqs(freqs, excess_sum, second_sum, sample_count):
@@ -191,21 +242,28 @@
 IN_VMEM = pl.BlockSpec(memory_space=pltpu.VMEM)
 
 
-def call(kernel, name, args, outs, scratch=(), cost=2000, aliases=None, raw=()):
+def call(kernel, args, outs, scratch=(), cost=2000, aliases=None, raw=()):
     specs = [SCALARS]
     held = [args[0]]
     for at, x in enumerate(args[1:], 1):
         specs.append(pl.BlockSpec(memory_space=pl.ANY) if at in raw else IN_VMEM)
         held.append(x if at in raw else pltpu.with_memory_space_constraint(x, VMEM))
+    out_specs, out_shape = [], []
+    for out in outs:
+        if isinstance(out, jax.ShapeDtypeStruct):
+            out_specs.append(pl.BlockSpec(memory_space=pltpu.HBM))
+            out_shape.append(out)
+        else:
+            out_specs.append(IN_VMEM)
+            out_shape.append(VMEM(out, F32) if isinstance(out, tuple) else out)
     return pl.pallas_call(
         kernel,
         in_specs=specs,
-        out_specs=[IN_VMEM] * len(outs),
-        out_shape=[VMEM(s, F32) for s in outs],
+        out_specs=out_specs,
+        out_shape=out_shape,
         scratch_shapes=list(scratch),
         input_output_aliases=aliases or {},
         cost_estimate=pl.CostEstimate(flops=cost * 400_000, bytes_accessed=0, transcendentals=0),
-        name=name,
     )(*held)
 
 
@@ -219,63 +277,54 @@
     sample_count = rows * lax.axis_size("smp")
     variants = width * var_count
     place = lax.axis_index("var").astype(jnp.int32).reshape(1)
-
-    def move(x, m, name):
-        with jax.named_scope(name):
-            return lax.ppermute(x, "var", [(i, i ^ m) for i in range(var_count)])
-
-    def swap(x, name):
-        with jax.named_scope(name):
-            return lax.ppermute(x, "smp", [(0, 1), (1, 0)])
-
-    counts = ancestry_counts.T
-    resid = residuals.T
+    dma = pltpu.SemaphoreType.DMA
+
+    def move(x, m):
+        return lax.ppermute(x, "var", [(i, i ^ m) for i in range(var_count)])
+
+    def swap(x):
+        return lax.ppermute(x, "smp", [(0, 1), (1, 0)])
+
     half_rows = rows // 2
+    tiles = half_rows // LANES
+    pieces = next(p for p in (5, 4, 3, 2, 1) if tiles % p == 0)
     excess = VMEM((half_rows, 2 * width), BF16)
-    pieces = 3 if half_rows % (3 * LANES) == 0 else 1
-
-    (far,) = call(
-        functools.partial(gradient_kernel, half, True),
-        "grad_far",
-        (place, genotypes, counts, freqs),
-        [(half, anc, share)],
-        [
-            excess,
-            VMEM((half_rows, width), BF16),
-            VMEM((anc, half_rows), jnp.int32),
-            pltpu.SemaphoreType.DMA((2, pieces)),
-        ],
-        raw=(1, 2),
+
+    far, geno, counts = call(
+        functools.partial(far_kernel, half),
+        (place, genotypes, ancestry_counts.T, freqs),
+        [(half, anc, share), VMEM(genotypes.shape, genotypes.dtype), VMEM((anc, rows), jnp.int32)],
+        [excess, VMEM(freqs.shape, F32), dma((3, pieces + 1))],
+        raw=(1, 2, 3),
     )
     (near,) = call(
-        functools.partial(gradient_kernel, half, False),
-        "grad_near",
-        (place, genotypes, counts, freqs),
+        functools.partial(near_kernel, half),
+        (place, geno, counts, freqs),
         [(half, anc, share)],
         [excess],
     )
-    slots = {half + c: far[c] for c in range(half)} | {c: near[c] for c in range(half)}
-    bit = 1
+    slots = {half + c: far[c] for c in range(half)}
+    for m in reversed(range(half + 1, var_count, 2)):
+        slots[m ^ 1] = slots[m ^ 1] + move(slots[m], 1)
+    pairs = near.reshape(half // 2, 2, anc, share)
+    pairs = pairs[:, 0] + move(pairs[:, 1], 1)
+    slots |= {2 * c: pairs[c] for c in range(half // 2)}
+    bit = 2
     while bit < var_count:
         for m in reversed(range(bit, var_count, 2 * bit)):
-            slots[m ^ bit] = slots[m ^ bit] + move(slots[m], bit, f"rs{m}")
+            slots[m ^ bit] = slots[m ^ bit] + move(slots[m], bit)
         bit *= 2
 
     sums, trait_parts, count_parts = call(
         sums_kernel,
-        "sums",
-        (place, genotypes, counts, freqs, resid),
+        (place, geno, counts, freqs, residuals.T),
         [(anc, 2 * width), (var_count, traits, share), (var_count, anc, share)],
         [VMEM((2 * rows, 2 * width), BF16)],
     )
-    sums_all = sums + swap(sums, "swap_sums")
-    freq_next, freq_gradient = update_freqs(
-        freqs, sums_all[:, :width], sums_all[:, width:], sample_count
-    )
+    sums_other = swap(sums)
 
     q_new, own_gradient = call(
         functools.partial(share_kernel, variants),
-        "share",
         (place, count_parts, slots[0]),
         [(anc, share), (anc, share)],
         cost=500,
@@ -285,28 +334,36 @@
     bit = half
     while bit:
         for m in range(bit, var_count, 2 * bit):
-            shares[m] = move(shares[m ^ bit], bit, f"ag{m}")
+            shares[m] = move(shares[m ^ bit], bit)
         bit //= 2
 
-    def scores(ms, total):
-        inputs = (genotypes, trait_parts, freqs) + (() if total is None else (total,))
-        (out,) = call(
-            functools.partial(score_kernel, ms, total is None),
-            "score",
-            (place, *[shares[m] for m in ms], *inputs),
+    total = None
+    for m in (0, 4, 2, 1, 3, 6, 5, 7) if var_count == 8 else range(var_count):
+        inputs = (geno, trait_parts, freqs) + (() if total is None else (total,))
+        (total,) = call(
+            functools.partial(score_kernel, (m,), total is None),
+            (place, shares[m], *inputs),
             [((anc * traits + anc), width)],
-            cost=700 * len(ms),
-            aliases=None if total is None else {len(ms) + 4: 0},
-        )
-        return out
-
-    total = None
-    for ms in ([0], [2], [1], [3], [4], [6], [5], [7]) if var_count == 8 else [[m] for m in range(var_count)]:
-        total = scores(tuple(ms), total)
+            cost=700,
+            aliases=None if total is None else {5: 0},
+        )
+    total_other = swap(total)
+    out = jax.ShapeDtypeStruct
+    q_out, grad_out, freq_next, freq_gradient = call(
+        functools.partial(emit_kernel, sample_count),
+        (place, q_new, own_gradient, sums, sums_other, freqs),
+        [out((anc, share), F32)] * 2 + [out((anc, width), F32)] * 2,
+        [VMEM((anc, width), F32)] * 2 + [dma((4,))],
+        cost=600,
+    )
     (z_score,) = call(
-        final_kernel, "final", (place, total, swap(total, "swap_score")), [(anc, traits, width)], cost=300
-    )
-    return (q_new.T, own_gradient.T, freq_next, freq_gradient, z_score)
+        final_kernel,
+        (place, total, total_other),
+        [out((anc, traits, width), F32)],
+        [VMEM((anc, traits, width), F32), dma((4 if anc % 4 == 0 else 1,))],
+        cost=300,
+    )
+    return (q_out.T, grad_out.T, freq_next, freq_gradient, z_score)
 
 
 def plain_shards(genotypes, ancestry_counts, residuals, freqs):
@@ -376,12 +433,18 @@
             P("grp", "var"),
             P("grp", None, "var"),
         )
-        return jax.shard_map(
-            shards if power and tiled and sizes["smp"] == 2 else plain_shards,
+        fits = power and tiled and sizes["smp"] == 2
+
+        def body(*args):
+            return (shards if fits else plain_shards)(*args)
+
+        mapped = jax.shard_map(
+            body,
             mesh=mesh,
             in_specs=in_specs,
             out_specs=out_specs,
             check_vma=False,
-        )(genotypes, ancestry_counts, residuals, freqs)
+        )
+        return mapped(genotypes, ancestry_counts, residuals, freqs)
 
     return step

time: 42.3 us -> 39.7 us (0.939)
  starting transfers between devices: 23.1 us -> 18.3 us
  waiting for transfers between devices: 3.29 us -> 7.02 us
  local copies, waits for them, and re-layouts: 2.72 us -> 0.04 us
  Pallas kernels: 11.4 us -> 13.2 us
  other arithmetic: 0.68 us -> 0.06 us
    ppermute x14 -> x13, starting transfers between devices: 22.6 us -> 17.7 us  [move(): return lax.ppermute(x, 'var', [(i, i ^ m) for i in range(var_count)])]
    ppermute x14 -> x13, waiting for transfers between devices: 2.19 us -> 5.92 us  [move(): return lax.ppermute(x, 'var', [(i, i ^ m) for i in range(var_count)])]
    unnamed x13 -> x4, local copies, waits for them, and re-layouts: 2.7 us -> 0.01 us
    pallas_call x13 -> x14, Pallas kernels: 11.4 us -> 13.2 us  [call(): pl.pallas_call(kernel, in_specs=specs, out_specs=out_specs, out_shape=out...]
    div x1 -> x0, other arithmetic: 0.62 us -> none  [update_freqs(): freq_gradient = excess_sum * freqs.shape[0] / math.sqrt(sample_count)]
  transfers between devices with their start and end apart: 16 -> 15, of which waited for: 5 -> 7; matrix products, arithmetic and copies ran while one was open for 5% -> 0% of each run, Pallas kernels for 19% -> 22%
where the time goes in v4:
time: 39.7 us; the launch traced here: 39.4 us
  starting transfers between devices  18.3 us (46%)
  Pallas kernels  13.2 us (33%)
  waiting for transfers between devices  7.02 us (18%)
  between operations  0.83 us (2%)
    ppermute x13, starting transfers between devices, move(): return lax.ppermute(x, 'var', [(i, i ^ m) for i in range(var_count)])  17.7 us
    pallas_call x14, Pallas kernels, call(): pl.pallas_call(kernel, in_specs=specs, out_specs=out_specs, out_shape=out...  13.2 us
    ppermute x13, waiting for transfers between devices, move(): return lax.ppermute(x, 'var', [(i, i ^ m) for i in range(var_count)])  5.92 us
    ppermute x2, waiting for transfers between devices, swap(): return lax.ppermute(x, 'smp', [(0, 1), (1, 0)])  1.1 us
  transfers between devices with their start and end apart: 15, of which 7 were waited for; matrix products, arithmetic and copies ran while one was open for 0% of the time, Pallas kernels for 22%

profile of v4, /device:TPU:0, one launch (start us, length us, event | category | flops | bytes accessed | tf_op | source)
XLA Modules:
  0.0 39.4 jit_solution(16202906274480163697)
XLA Ops:
  0.6 2.9 %shard_map.83 = (f32[4,32,480]{2,1,0:T(8,128)S(1)}, bf16[3840,128]{1,0:T(8,128)(2,1)S(1)}, s32[32,3840]{1,0:T(8,128)S(1)}) custom-call(s32[1]{0:T(128)} %bitcast.place_ref.own_ref, bf16[3840,128]{1,0:T(8,128)(2,1)} %geno_hbm.1, s32[32,3840]{1,0:T(8,128)} %bitcast.37, f32[32,128]{1,0:T(8,128)} %refs_3_.15), custom_call_target="tpu_custom_call" | custom-call | flops 800000000 | tf_op jit(solution)/shard_map/pallas_call | solution.py:259
  3.5 0.0 copy-start
  3.5 3.0 %collective-permute-start.3 = (f32[32,480]{1,0:T(8,128)S(1)}, f32[32,480]{1,0:T(8,128)S(1)}, u32[]{:S(2)}, u32[]{:S(2)}) collective-permute-start(f32[32,480]{1,0:T(8,128)S(1)} %get-tuple-element.30), channel_id=1, source_target_pairs={{0,2},{2,0},{4,6},{6,4},{8,10},{10,8},{12,14},{14,12},{1,3},{3,1},... | collective-permute-start | bytes 184328 | tf_op jit(solution)/shard_map/ppermute | solution.py:283
  6.6 0.0 copy-done
  6.6 1.0 %shard_map.85 = f32[4,32,480]{2,1,0:T(8,128)S(1)} custom-call(s32[1]{0:T(128)} %bitcast.place_ref.own_ref, bf16[3840,128]{1,0:T(8,128)(2,1)S(1)} %get-tuple-element.17.geno_ref.refs_1_, s32[32,3840]{1,0:T(8,128)S(1)} %get-tuple-element.18.counts_ref, f32[32,128]{1,0:T(8,128)S(1)} %copy-done), custom_call_target="tpu_custom_call" | custom-call | flops 800000000 | tf_op jit(solution)/shard_map/pallas_call | solution.py:259
  7.6 0.7 %collective-permute-start = (f32[2,32,480]{2,1,0:T(8,128)S(1)}, f32[2,32,480]{2,1,0:T(8,128)S(1)}, u32[]{:S(2)}, u32[]{:S(2)}) collective-permute-start(f32[2,32,480]{2,1,0:T(8,128)S(1)} %slice_bitcast_fusion), channel_id=1, source_target_pairs={{0,2},{2,0},{4,6},{6,4},{8,10},{10,8},{12,14},{14,12},{1,3},{3,1},... | collective-permute-start | bytes 368648 | tf_op jit(solution)/shard_map/ppermute | solution.py:283
  8.3 1.4 %collective-permute-start.2 = (f32[32,480]{1,0:T(8,128)S(1)}, f32[32,480]{1,0:T(8,128)S(1)}, u32[]{:S(2)}, u32[]{:S(2)}) collective-permute-start(f32[32,480]{1,0:T(8,128)S(1)} %get-tuple-element.29), channel_id=1, source_target_pairs={{0,2},{2,0},{4,6},{6,4},{8,10},{10,8},{12,14},{14,12},{1,3},{3,1},... | collective-permute-start | bytes 184328 | tf_op jit(solution)/shard_map/ppermute | solution.py:283
  9.7 0.0 collective-permute-done.3
  9.7 1.6 %collective-permute-start.4 = (f32[32,480]{1,0:T(8,128)S(1)}, f32[32,480]{1,0:T(8,128)S(1)}, u32[]{:S(2)}, u32[]{:S(2)}) collective-permute-start(f32[32,480]{1,0:T(8,128)S(1)} %bitcast_add_fusion), channel_id=1, source_target_pairs={{0,4},{2,6},{4,0},{6,2},{8,12},{10,14},{12,8},{14,10},{1,5},{3,7},... | collective-permute-start | bytes 184328 | tf_op jit(solution)/shard_map/ppermute | solution.py:283
  11.3 2.0 %collective-permute-done = f32[2,32,480]{2,1,0:T(8,128)S(1)} collective-permute-done((f32[2,32,480]{2,1,0:T(8,128)S(1)}, f32[2,32,480]{2,1,0:T(8,128)S(1)}, u32[]{:S(2)}, u32[]{:S(2)}) %collective-permute-start) | collective-permute-done | bytes 122912 | tf_op jit(solution)/shard_map/ppermute | solution.py:283
  13.3 0.0 copy-start.1
  13.3 1.6 %collective-permute-start.1 = (f32[32,480]{1,0:T(8,128)S(1)}, f32[32,480]{1,0:T(8,128)S(1)}, u32[]{:S(2)}, u32[]{:S(2)}) collective-permute-start(f32[32,480]{1,0:T(8,128)S(1)} %slice_bitcast_fusion.2), channel_id=1, source_target_pairs={{0,4},{2,6},{4,0},{6,2},{8,12},{10,14},{12,8},{14,10},{1,5},{3,7},... | collective-permute-start | bytes 184328 | tf_op jit(solution)/shard_map/ppermute | solution.py:283
  15.0 0.0 collective-permute-done.2
  15.0 0.0 collective-permute-done.4
  15.0 2.7 %collective-permute-start.5 = (f32[32,480]{1,0:T(8,128)S(1)}, f32[32,480]{1,0:T(8,128)S(1)}, u32[]{:S(2)}, u32[]{:S(2)}) collective-permute-start(f32[32,480]{1,0:T(8,128)S(1)} %fusion.3), channel_id=1, source_target_pairs={{0,8},{2,10},{4,12},{6,14},{8,0},{10,2},{12,4},{14,6},{1,9},{3,11}... | collective-permute-start | bytes 184328 | tf_op jit(solution)/shard_map/ppermute | solution.py:283
  17.7 0.0 copy-done.1
  17.7 2.4 %shard_map.84 = (f32[32,256]{1,0:T(8,128)S(1)}, f32[8,16,480]{2,1,0:T(8,128)S(1)}, f32[8,32,480]{2,1,0:T(8,128)S(1)}) custom-call(s32[1]{0:T(128)} %bitcast.place_ref.own_ref, bf16[3840,128]{1,0:T(8,128)(2,1)S(1)} %get-tuple-element.17.geno_ref.refs_1_, s32[32,3840]{1,0:T(8,128)S(1)} %get-tuple-element.18.counts_ref, f32[32,128]{1,0:T(8,128)S(1)} %copy-done, ...), custom_call_target="tpu_custom_call" | custom-call | flops 800000000 | tf_op jit(solution)/shard_map/pallas_call | solution.py:259
  20.0 0.0 collective-permute-done.1
  20.0 0.9 %collective-permute-done.5 = f32[32,480]{1,0:T(8,128)S(1)} collective-permute-done((f32[32,480]{1,0:T(8,128)S(1)}, f32[32,480]{1,0:T(8,128)S(1)}, u32[]{:S(2)}, u32[]{:S(2)}) %collective-permute-start.5) | collective-permute-done | bytes 61472 | tf_op jit(solution)/shard_map/ppermute | solution.py:283
  21.0 0.1 shard_map.86
  21.0 2.1 %collective-permute-start.7 = (f32[32,480]{1,0:T(8,128)S(1)}, f32[32,480]{1,0:T(8,128)S(1)}, u32[]{:S(2)}, u32[]{:S(2)}) collective-permute-start(f32[32,480]{1,0:T(8,128)S(1)} %get-tuple-element.21.q_ref.refs_0_), channel_id=1, source_target_pairs={{0,8},{2,10},{4,12},{6,14},{8,0},{10,2},{12,4},{14,6},{1,9},{3,11}... | collective-permute-start | bytes 184328 | tf_op jit(solution)/shard_map/ppermute | solution.py:283
  23.1 1.5 %collective-permute-start.11 = (f32[32,480]{1,0:T(8,128)S(1)}, f32[32,480]{1,0:T(8,128)S(1)}, u32[]{:S(2)}, u32[]{:S(2)}) collective-permute-start(f32[32,480]{1,0:T(8,128)S(1)} %get-tuple-element.21.q_ref.refs_0_), channel_id=1, source_target_pairs={{0,4},{2,6},{4,0},{6,2},{8,12},{10,14},{12,8},{14,10},{1,5},{3,7},... | collective-permute-start | bytes 184328 | tf_op jit(solution)/shard_map/ppermute | solution.py:283
  24.6 0.3 collective-permute-start.13
  24.9 0.7 %shard_map.88.refs_4_ = f32[544,128]{1,0:T(8,128)S(1)} custom-call(s32[1]{0:T(128)} %bitcast.place_ref.own_ref, f32[32,480]{1,0:T(8,128)S(1)} %get-tuple-element.21.q_ref.refs_0_, bf16[3840,128]{1,0:T(8,128)(2,1)S(1)} %get-tuple-element.17.geno_ref.refs_1_, f32[8,16,480]{2,1,0:T(8,128)S(1)} %get-tuple-element.28.refs_2_, f32[32,128]{1,0:T(8,128)S(1)} %copy-done), custom_call_target="tpu_custom_call" | custom-call | flops 280000000 | tf_op jit(solution)/shard_map/pallas_call | solution.py:259
  25.6 1.5 %collective-permute-done.7.refs_0_ = f32[32,480]{1,0:T(8,128)S(1)} collective-permute-done((f32[32,480]{1,0:T(8,128)S(1)}, f32[32,480]{1,0:T(8,128)S(1)}, u32[]{:S(2)}, u32[]{:S(2)}) %collective-permute-start.7) | collective-permute-done | bytes 61472 | tf_op jit(solution)/shard_map/ppermute | solution.py:283
  27.1 0.0 collective-permute-start.8
  27.1 0.8 %collective-permute-start.10 = (f32[32,480]{1,0:T(8,128)S(1)}, f32[32,480]{1,0:T(8,128)S(1)}, u32[]{:S(2)}, u32[]{:S(2)}) collective-permute-start(f32[32,480]{1,0:T(8,128)S(1)} %collective-permute-done.7.refs_0_), channel_id=1, source_target_pairs={{0,2},{2,0},{4,6},{6,4},{8,10},{10,8},{12,14},{14,12},{1,3},{3,1},... | collective-permute-start | bytes 184328 | tf_op jit(solution)/shard_map/ppermute | solution.py:283
  27.9 0.0 collective-permute-done.11.refs_0_
  27.9 1.2 %collective-permute-start.12 = (f32[32,480]{1,0:T(8,128)S(1)}, f32[32,480]{1,0:T(8,128)S(1)}, u32[]{:S(2)}, u32[]{:S(2)}) collective-permute-start(f32[32,480]{1,0:T(8,128)S(1)} %collective-permute-done.11.refs_0_), channel_id=1, source_target_pairs={{0,2},{2,0},{4,6},{6,4},{8,10},{10,8},{12,14},{14,12},{1,3},{3,1},... | collective-permute-start | bytes 184328 | tf_op jit(solution)/shard_map/ppermute | solution.py:283
  29.1 0.7 %shard_map.89.refs_4_ = f32[544,128]{1,0:T(8,128)S(1)} custom-call(s32[1]{0:T(128)} %bitcast.place_ref.own_ref, f32[32,480]{1,0:T(8,128)S(1)} %collective-permute-done.7.refs_0_, bf16[3840,128]{1,0:T(8,128)(2,1)S(1)} %get-tuple-element.17.geno_ref.refs_1_, f32[8,16,480]{2,1,0:T(8,128)S(1)} %get-tuple-element.28.refs_2_, ...), custom_call_target="tpu_custom_call", output_to_operand_aliasing={{}: (5, {})} | custom-call | flops 280000000 | tf_op jit(solution)/shard_map/pallas_call | solution.py:259
  29.8 0.7 %shard_map.90.refs_4_ = f32[544,128]{1,0:T(8,128)S(1)} custom-call(s32[1]{0:T(128)} %bitcast.place_ref.own_ref, f32[32,480]{1,0:T(8,128)S(1)} %collective-permute-done.11.refs_0_, bf16[3840,128]{1,0:T(8,128)(2,1)S(1)} %get-tuple-element.17.geno_ref.refs_1_, f32[8,16,480]{2,1,0:T(8,128)S(1)} %get-tuple-element.28.refs_2_, ...), custom_call_target="tpu_custom_call", output_to_operand_aliasing={{}: (5, {})} | custom-call | flops 280000000 | tf_op jit(solution)/shard_map/pallas_call | solution.py:259
  30.5 0.0 collective-permute-done.13.refs_0_
  30.5 0.7 %shard_map.91.refs_4_ = f32[544,128]{1,0:T(8,128)S(1)} custom-call(s32[1]{0:T(128)} %bitcast.place_ref.own_ref, f32[32,480]{1,0:T(8,128)S(1)} %collective-permute-done.13.refs_0_, bf16[3840,128]{1,0:T(8,128)(2,1)S(1)} %get-tuple-element.17.geno_ref.refs_1_, f32[8,16,480]{2,1,0:T(8,128)S(1)} %get-tuple-element.28.refs_2_, ...), custom_call_target="tpu_custom_call", output_to_operand_aliasing={{}: (5, {})} | custom-call | flops 280000000 | tf_op jit(solution)/shard_map/pallas_call | solution.py:259
  31.2 0.1 collective-permute-done.8.refs_0_
  31.3 0.8 %collective-permute-start.9 = (f32[32,480]{1,0:T(8,128)S(1)}, f32[32,480]{1,0:T(8,128)S(1)}, u32[]{:S(2)}, u32[]{:S(2)}) collective-permute-start(f32[32,480]{1,0:T(8,128)S(1)} %collective-permute-done.8.refs_0_), channel_id=1, source_target_pairs={{0,2},{2,0},{4,6},{6,4},{8,10},{10,8},{12,14},{14,12},{1,3},{3,1},... | collective-permute-start | bytes 184328 | tf_op jit(solution)/shard_map/ppermute | solution.py:283
  32.1 0.1 collective-permute-done.12.refs_0_
  32.2 0.7 %shard_map.92.refs_4_ = f32[544,128]{1,0:T(8,128)S(1)} custom-call(s32[1]{0:T(128)} %bitcast.place_ref.own_ref, f32[32,480]{1,0:T(8,128)S(1)} %collective-permute-done.12.refs_0_, bf16[3840,128]{1,0:T(8,128)(2,1)S(1)} %get-tuple-element.17.geno_ref.refs_1_, f32[8,16,480]{2,1,0:T(8,128)S(1)} %get-tuple-element.28.refs_2_, ...), custom_call_target="tpu_custom_call", output_to_operand_aliasing={{}: (5, {})} | custom-call | flops 280000000 | tf_op jit(solution)/shard_map/pallas_call | solution.py:259
  32.9 0.7 %shard_map.93.refs_4_ = f32[544,128]{1,0:T(8,128)S(1)} custom-call(s32[1]{0:T(128)} %bitcast.place_ref.own_ref, f32[32,480]{1,0:T(8,128)S(1)} %collective-permute-done.8.refs_0_, bf16[3840,128]{1,0:T(8,128)(2,1)S(1)} %get-tuple-element.17.geno_ref.refs_1_, f32[8,16,480]{2,1,0:T(8,128)S(1)} %get-tuple-element.28.refs_2_, ...), custom_call_target="tpu_custom_call", output_to_operand_aliasing={{}: (5, {})} | custom-call | flops 280000000 | tf_op jit(solution)/shard_map/pallas_call | solution.py:259
  33.6 0.0 collective-permute-done.10.refs_0_
  33.6 0.7 %shard_map.94.refs_4_ = f32[544,128]{1,0:T(8,128)S(1)} custom-call(s32[1]{0:T(128)} %bitcast.place_ref.own_ref, f32[32,480]{1,0:T(8,128)S(1)} %collective-permute-done.10.refs_0_, bf16[3840,128]{1,0:T(8,128)(2,1)S(1)} %get-tuple-element.17.geno_ref.refs_1_, f32[8,16,480]{2,1,0:T(8,128)S(1)} %get-tuple-element.28.refs_2_, ...), custom_call_target="tpu_custom_call", output_to_operand_aliasing={{}: (5, {})} | custom-call | flops 280000000 | tf_op jit(solution)/shard_map/pallas_call | solution.py:259
  34.3 1.3 %collective-permute-done.9.refs_0_ = f32[32,480]{1,0:T(8,128)S(1)} collective-permute-done((f32[32,480]{1,0:T(8,128)S(1)}, f32[32,480]{1,0:T(8,128)S(1)}, u32[]{:S(2)}, u32[]{:S(2)}) %collective-permute-start.9) | collective-permute-done | bytes 61472 | tf_op jit(solution)/shard_map/ppermute | solution.py:283
  35.6 0.7 %shard_map.95.mine_ref = f32[544,128]{1,0:T(8,128)S(1)} custom-call(s32[1]{0:T(128)} %bitcast.place_ref.own_ref, f32[32,480]{1,0:T(8,128)S(1)} %collective-permute-done.9.refs_0_, bf16[3840,128]{1,0:T(8,128)(2,1)S(1)} %get-tuple-element.17.geno_ref.refs_1_, f32[8,16,480]{2,1,0:T(8,128)S(1)} %get-tuple-element.28.refs_2_, ...), custom_call_target="tpu_custom_call", output_to_operand_aliasing={{}: (5, {})} | custom-call | flops 280000000 | tf_op jit(solution)/shard_map/pallas_call | solution.py:259
  36.3 0.1 collective-permute-start.14
  36.4 0.5 %collective-permute-start.6 = (f32[32,256]{1,0:T(8,128)S(1)}, f32[32,256]{1,0:T(8,128)S(1)}, u32[]{:S(2)}, u32[]{:S(2)}) collective-permute-start(f32[32,256]{1,0:T(8,128)S(1)} %get-tuple-element.23.sums_ref), channel_id=1, source_target_pairs={{0,1},{1,0},{2,3},{3,2},{4,5},{5,4},{6,7},{7,6},{8,9},{9,8},{10,11... | collective-permute-start | bytes 98312 | tf_op jit(solution)/shard_map/ppermute | solution.py:286
  36.9 1.1 %collective-permute-done.6.other_ref = f32[32,256]{1,0:T(8,128)S(1)} collective-permute-done((f32[32,256]{1,0:T(8,128)S(1)}, f32[32,256]{1,0:T(8,128)S(1)}, u32[]{:S(2)}, u32[]{:S(2)}) %collective-permute-start.6) | collective-permute-done | bytes 32800 | tf_op jit(solution)/shard_map/ppermute | solution.py:286
  38.0 0.7 %shard_map.87 = (f32[32,480]{1,0:T(8,128)}, f32[32,480]{1,0:T(8,128)}, f32[32,128]{1,0:T(8,128)}, f32[32,128]{1,0:T(8,128)}) custom-call(s32[1]{0:T(128)} %bitcast.place_ref.own_ref, f32[32,480]{1,0:T(8,128)S(1)} %get-tuple-element.21.q_ref.refs_0_, f32[32,480]{1,0:T(8,128)S(1)} %get-tuple-element.22.grad_ref, f32[32,256]{1,0:T(8,128)S(1)} %get-tuple-element.23.sums_ref, ...), custom_call_target="tpu_custom_call" | custom-call | flops 240000000 | tf_op jit(solution)/shard_map/pallas_call | solution.py:259
  38.6 0.0 collective-permute-done.14.other_ref
  38.7 0.8 %shard_map.96 = f32[32,16,128]{2,1,0:T(8,128)} custom-call(s32[1]{0:T(128)} %bitcast.place_ref.own_ref, f32[544,128]{1,0:T(8,128)S(1)} %shard_map.95.mine_ref, f32[544,128]{1,0:T(8,128)S(1)} %collective-permute-done.14.other_ref), custom_call_target="tpu_custom_call" | custom-call | flops 120000000 | tf_op jit(solution)/shard_map/pallas_call | solution.py:259
  (7 shorter events, 0.1 us)
Async XLA Ops:
  3.5 3.1 %copy-start = (f32[32,128]{1,0:T(8,128)S(1)}, f32[32,128]{1,0:T(8,128)}, u32[]{:S(2)}) copy-start(f32[32,128]{1,0:T(8,128)} %refs_3_.15) | copy-start | bytes 49156
  3.5 6.1 %collective-permute-start.3 = (f32[32,480]{1,0:T(8,128)S(1)}, f32[32,480]{1,0:T(8,128)S(1)}, u32[]{:S(2)}, u32[]{:S(2)}) collective-permute-start(f32[32,480]{1,0:T(8,128)S(1)} %get-tuple-element.30), channel_id=1, source_target_pairs={{0,2},{2,0},{4,6},{6,4},{8,10},{10,8},{12,14},{14,12},{1,3},{3,1},... | collective-permute-start | bytes 184328 | tf_op jit(solution)/shard_map/ppermute | solution.py:283
  7.6 5.7 %collective-permute-start = (f32[2,32,480]{2,1,0:T(8,128)S(1)}, f32[2,32,480]{2,1,0:T(8,128)S(1)}, u32[]{:S(2)}, u32[]{:S(2)}) collective-permute-start(f32[2,32,480]{2,1,0:T(8,128)S(1)} %slice_bitcast_fusion), channel_id=1, source_target_pairs={{0,2},{2,0},{4,6},{6,4},{8,10},{10,8},{12,14},{14,12},{1,3},{3,1},... | collective-permute-start | bytes 368648 | tf_op jit(solution)/shard_map/ppermute | solution.py:283
  8.3 6.7 %collective-permute-start.2 = (f32[32,480]{1,0:T(8,128)S(1)}, f32[32,480]{1,0:T(8,128)S(1)}, u32[]{:S(2)}, u32[]{:S(2)}) collective-permute-start(f32[32,480]{1,0:T(8,128)S(1)} %get-tuple-element.29), channel_id=1, source_target_pairs={{0,2},{2,0},{4,6},{6,4},{8,10},{10,8},{12,14},{14,12},{1,3},{3,1},... | collective-permute-start | bytes 184328 | tf_op jit(solution)/shard_map/ppermute | solution.py:283
  9.7 5.3 %collective-permute-start.4 = (f32[32,480]{1,0:T(8,128)S(1)}, f32[32,480]{1,0:T(8,128)S(1)}, u32[]{:S(2)}, u32[]{:S(2)}) collective-permute-start(f32[32,480]{1,0:T(8,128)S(1)} %bitcast_add_fusion), channel_id=1, source_target_pairs={{0,4},{2,6},{4,0},{6,2},{8,12},{10,14},{12,8},{14,10},{1,5},{3,7},... | collective-permute-start | bytes 184328 | tf_op jit(solution)/shard_map/ppermute | solution.py:283
  13.3 4.4 %copy-start.1 = (s32[3840,16]{0,1:T(8,128)S(1)}, s32[3840,16]{0,1:T(8,128)}, u32[]{:S(2)}) copy-start(s32[3840,16]{0,1:T(8,128)} %param.6) | copy-start | bytes 737284
  13.3 6.7 %collective-permute-start.1 = (f32[32,480]{1,0:T(8,128)S(1)}, f32[32,480]{1,0:T(8,128)S(1)}, u32[]{:S(2)}, u32[]{:S(2)}) collective-permute-start(f32[32,480]{1,0:T(8,128)S(1)} %slice_bitcast_fusion.2), channel_id=1, source_target_pairs={{0,4},{2,6},{4,0},{6,2},{8,12},{10,14},{12,8},{14,10},{1,5},{3,7},... | collective-permute-start | bytes 184328 | tf_op jit(solution)/shard_map/ppermute | solution.py:283
  15.0 5.9 %collective-permute-start.5 = (f32[32,480]{1,0:T(8,128)S(1)}, f32[32,480]{1,0:T(8,128)S(1)}, u32[]{:S(2)}, u32[]{:S(2)}) collective-permute-start(f32[32,480]{1,0:T(8,128)S(1)} %fusion.3), channel_id=1, source_target_pairs={{0,8},{2,10},{4,12},{6,14},{8,0},{10,2},{12,4},{14,6},{1,9},{3,11}... | collective-permute-start | bytes 184328 | tf_op jit(solution)/shard_map/ppermute | solution.py:283
  21.0 6.0 %collective-permute-start.7 = (f32[32,480]{1,0:T(8,128)S(1)}, f32[32,480]{1,0:T(8,128)S(1)}, u32[]{:S(2)}, u32[]{:S(2)}) collective-permute-start(f32[32,480]{1,0:T(8,128)S(1)} %get-tuple-element.21.q_ref.refs_0_), channel_id=1, source_target_pairs={{0,8},{2,10},{4,12},{6,14},{8,0},{10,2},{12,4},{14,6},{1,9},{3,11}... | collective-permute-start | bytes 184328 | tf_op jit(solution)/shard_map/ppermute | solution.py:283
  23.1 4.8 %collective-permute-start.11 = (f32[32,480]{1,0:T(8,128)S(1)}, f32[32,480]{1,0:T(8,128)S(1)}, u32[]{:S(2)}, u32[]{:S(2)}) collective-permute-start(f32[32,480]{1,0:T(8,128)S(1)} %get-tuple-element.21.q_ref.refs_0_), channel_id=1, source_target_pairs={{0,4},{2,6},{4,0},{6,2},{8,12},{10,14},{12,8},{14,10},{1,5},{3,7},... | collective-permute-start | bytes 184328 | tf_op jit(solution)/shard_map/ppermute | solution.py:283
  24.6 5.9 %collective-permute-start.13 = (f32[32,480]{1,0:T(8,128)S(1)}, f32[32,480]{1,0:T(8,128)S(1)}, u32[]{:S(2)}, u32[]{:S(2)}) collective-permute-start(f32[32,480]{1,0:T(8,128)S(1)} %get-tuple-element.21.q_ref.refs_0_), channel_id=1, source_target_pairs={{0,2},{2,0},{4,6},{6,4},{8,10},{10,8},{12,14},{14,12},{1,3},{3,1},... | collective-permute-start | bytes 184328 | tf_op jit(solution)/shard_map/ppermute | solution.py:283
  27.1 4.3 %collective-permute-start.8 = (f32[32,480]{1,0:T(8,128)S(1)}, f32[32,480]{1,0:T(8,128)S(1)}, u32[]{:S(2)}, u32[]{:S(2)}) collective-permute-start(f32[32,480]{1,0:T(8,128)S(1)} %collective-permute-done.7.refs_0_), channel_id=1, source_target_pairs={{0,4},{2,6},{4,0},{6,2},{8,12},{10,14},{12,8},{14,10},{1,5},{3,7},... | collective-permute-start | bytes 184328 | tf_op jit(solution)/shard_map/ppermute | solution.py:283
  27.1 6.5 %collective-permute-start.10 = (f32[32,480]{1,0:T(8,128)S(1)}, f32[32,480]{1,0:T(8,128)S(1)}, u32[]{:S(2)}, u32[]{:S(2)}) collective-permute-start(f32[32,480]{1,0:T(8,128)S(1)} %collective-permute-done.7.refs_0_), channel_id=1, source_target_pairs={{0,2},{2,0},{4,6},{6,4},{8,10},{10,8},{12,14},{14,12},{1,3},{3,1},... | collective-permute-start | bytes 184328 | tf_op jit(solution)/shard_map/ppermute | solution.py:283
  27.9 4.3 %collective-permute-start.12 = (f32[32,480]{1,0:T(8,128)S(1)}, f32[32,480]{1,0:T(8,128)S(1)}, u32[]{:S(2)}, u32[]{:S(2)}) collective-permute-start(f32[32,480]{1,0:T(8,128)S(1)} %collective-permute-done.11.refs_0_), channel_id=1, source_target_pairs={{0,2},{2,0},{4,6},{6,4},{8,10},{10,8},{12,14},{14,12},{1,3},{3,1},... | collective-permute-start | bytes 184328 | tf_op jit(solution)/shard_map/ppermute | solution.py:283
  31.3 4.3 %collective-permute-start.9 = (f32[32,480]{1,0:T(8,128)S(1)}, f32[32,480]{1,0:T(8,128)S(1)}, u32[]{:S(2)}, u32[]{:S(2)}) collective-permute-start(f32[32,480]{1,0:T(8,128)S(1)} %collective-permute-done.8.refs_0_), channel_id=1, source_target_pairs={{0,2},{2,0},{4,6},{6,4},{8,10},{10,8},{12,14},{14,12},{1,3},{3,1},... | collective-permute-start | bytes 184328 | tf_op jit(solution)/shard_map/ppermute | solution.py:283
  36.3 2.4 %collective-permute-start.14 = (f32[544,128]{1,0:T(8,128)S(1)}, f32[544,128]{1,0:T(8,128)S(1)}, u32[]{:S(2)}, u32[]{:S(2)}) collective-permute-start(f32[544,128]{1,0:T(8,128)S(1)} %shard_map.95.mine_ref), channel_id=1, source_target_pairs={{0,1},{1,0},{2,3},{3,2},{4,5},{5,4},{6,7},{7,6},{8,9},{9,8},{10,11... | collective-permute-start | bytes 835592 | tf_op jit(solution)/shard_map/ppermute | solution.py:286
  36.4 1.6 %collective-permute-start.6 = (f32[32,256]{1,0:T(8,128)S(1)}, f32[32,256]{1,0:T(8,128)S(1)}, u32[]{:S(2)}, u32[]{:S(2)}) collective-permute-start(f32[32,256]{1,0:T(8,128)S(1)} %get-tuple-element.23.sums_ref), channel_id=1, source_target_pairs={{0,1},{1,0},{2,3},{3,2},{4,5},{5,4},{6,7},{7,6},{8,9},{9,8},{10,11... | collective-permute-start | bytes 98312 | tf_op jit(solution)/shard_map/ppermute | solution.py:286

commit v5 on v4

--- a/solution.py
+++ b/solution.py
@@ -136,8 +136,9 @@
         own_ref[c] = counts[:, c * share : (c + 1) * share]
 
 
-def share_kernel(variants, own_ref, counts_ref, total_ref, q_ref, grad_ref):
-    gradient = total_ref[...]
+def share_kernel(variants, own_ref, counts_ref, *refs):
+    q_ref, grad_ref = refs[-2:]
+    gradient = sum(part[...] for part in refs[1:-2]) + refs[0][...]
     counts = counts_ref[own_ref[0]]
     fractions = counts / jnp.sum(counts, axis=0, keepdims=True)
     second = 2.0 * variants - jnp.sum(fractions * gradient, axis=0, keepdims=True)
@@ -303,17 +304,10 @@
         [(half, anc, share)],
         [excess],
     )
-    slots = {half + c: far[c] for c in range(half)}
-    for m in reversed(range(half + 1, var_count, 2)):
-        slots[m ^ 1] = slots[m ^ 1] + move(slots[m], 1)
-    pairs = near.reshape(half // 2, 2, anc, share)
-    pairs = pairs[:, 0] + move(pairs[:, 1], 1)
-    slots |= {2 * c: pairs[c] for c in range(half // 2)}
-    bit = 2
-    while bit < var_count:
-        for m in reversed(range(bit, var_count, 2 * bit)):
-            slots[m ^ bit] = slots[m ^ bit] + move(slots[m], bit)
-        bit *= 2
+    pairs = far.reshape(half // 2, 2, anc, share)
+    joined = pairs[:, 0] + move(pairs[:, 1], 1)
+    arrived = [near[0]] + [move(near[m], m) for m in range(1, half)]
+    arrived += [move(joined[c], half + 2 * c) for c in range(half // 2)]
 
     sums, trait_parts, count_parts = call(
         sums_kernel,
@@ -325,20 +319,19 @@
 
     q_new, own_gradient = call(
         functools.partial(share_kernel, variants),
-        (place, count_parts, slots[0]),
+        (place, count_parts, *arrived),
         [(anc, share), (anc, share)],
         cost=500,
     )
 
     shares = {0: q_new}
-    bit = half
-    while bit:
-        for m in range(bit, var_count, 2 * bit):
-            shares[m] = move(shares[m ^ bit], bit)
-        bit //= 2
+    for m in (*range(half, var_count, 2), *range(1, half)):
+        shares[m] = move(q_new, m)
+    for m in range(half + 1, var_count, 2):
+        shares[m] = move(shares[m - 1], 1)
 
     total = None
-    for m in (0, 4, 2, 1, 3, 6, 5, 7) if var_count == 8 else range(var_count):
+    for m in (0, 2, 1, 4, 3, 6, 5, 7) if var_count == 8 else range(var_count):
         inputs = (geno, trait_parts, freqs) + (() if total is None else (total,))
         (total,) = call(
             functools.partial(score_kernel, (m,), total is None),

time: 39.7 us -> 37.7 us (0.950)
  waiting for transfers between devices: 7.02 us -> 4.8 us
    ppermute x13, waiting for transfers between devices: 5.92 us -> 3.7 us  [move(): return lax.ppermute(x, 'var', [(i, i ^ m) for i in range(var_count)])]
  transfers between devices with their start and end apart: 15 -> 15, of which waited for: 7 -> 4; matrix products, arithmetic and copies ran while one was open for 0% -> 0% of each run, Pallas kernels for 22% -> 23%
where the time goes in v5:
time: 37.7 us; the launch traced here: 37.5 us
  starting transfers between devices  18.6 us (49%)
  Pallas kernels  13.2 us (35%)
  waiting for transfers between devices  4.8 us (13%)
  between operations  0.84 us (2%)
    ppermute x13, starting transfers between devices, move(): return lax.ppermute(x, 'var', [(i, i ^ m) for i in range(var_count)])  18 us
    pallas_call x14, Pallas kernels, call(): pl.pallas_call(kernel, in_specs=specs, out_specs=out_specs, out_shape=out...  13.2 us
    ppermute x13, waiting for transfers between devices, move(): return lax.ppermute(x, 'var', [(i, i ^ m) for i in range(var_count)])  3.7 us
    ppermute x2, waiting for transfers between devices, swap(): return lax.ppermute(x, 'smp', [(0, 1), (1, 0)])  1.1 us
  transfers between devices with their start and end apart: 15, of which 4 were waited for; matrix products, arithmetic and copies ran while one was open for 0% of the time, Pallas kernels for 23%

profile of v5, /device:TPU:0, one launch (start us, length us, event | category | flops | bytes accessed | tf_op | source)
XLA Modules:
  0.0 37.5 jit_solution(15136059658577711005)
XLA Ops:
  0.6 2.9 %shard_map.83 = (f32[4,32,480]{2,1,0:T(8,128)S(1)}, bf16[3840,128]{1,0:T(8,128)(2,1)S(1)}, s32[32,3840]{1,0:T(8,128)S(1)}) custom-call(s32[1]{0:T(128)} %bitcast.place_ref.own_ref, bf16[3840,128]{1,0:T(8,128)(2,1)} %geno_hbm.1, s32[32,3840]{1,0:T(8,128)} %bitcast.31, f32[32,128]{1,0:T(8,128)} %refs_3_.15), custom_call_target="tpu_custom_call" | custom-call | flops 800000000 | tf_op jit(solution)/shard_map/pallas_call | solution.py:260
  3.5 0.0 copy-start
  3.5 3.0 %collective-permute-start.3 = (f32[2,32,480]{2,1,0:T(8,128)S(1)}, f32[2,32,480]{2,1,0:T(8,128)S(1)}, u32[]{:S(2)}, u32[]{:S(2)}) collective-permute-start(f32[2,32,480]{2,1,0:T(8,128)S(1)} %slice_bitcast_fusion), channel_id=1, source_target_pairs={{0,2},{2,0},{4,6},{6,4},{8,10},{10,8},{12,14},{14,12},{1,3},{3,1},... | collective-permute-start | bytes 368648 | tf_op jit(solution)/shard_map/ppermute | solution.py:284
  6.6 0.0 copy-done
  6.6 1.0 %shard_map.85 = f32[4,32,480]{2,1,0:T(8,128)S(1)} custom-call(s32[1]{0:T(128)} %bitcast.place_ref.own_ref, bf16[3840,128]{1,0:T(8,128)(2,1)S(1)} %get-tuple-element.17.geno_ref.refs_1_, s32[32,3840]{1,0:T(8,128)S(1)} %get-tuple-element.18.counts_ref, f32[32,128]{1,0:T(8,128)S(1)} %copy-done), custom_call_target="tpu_custom_call" | custom-call | flops 800000000 | tf_op jit(solution)/shard_map/pallas_call | solution.py:260
  7.6 1.7 %collective-permute-start.2 = (f32[32,480]{1,0:T(8,128)S(1)}, f32[32,480]{1,0:T(8,128)S(1)}, u32[]{:S(2)}, u32[]{:S(2)}) collective-permute-start(f32[32,480]{1,0:T(8,128)S(1)} %get-tuple-element.29), channel_id=1, source_target_pairs={{0,6},{2,4},{4,2},{6,0},{8,14},{10,12},{12,10},{14,8},{1,7},{3,5},... | collective-permute-start | bytes 184328 | tf_op jit(solution)/shard_map/ppermute | solution.py:284
  9.3 0.4 %collective-permute-start.1 = (f32[32,480]{1,0:T(8,128)S(1)}, f32[32,480]{1,0:T(8,128)S(1)}, u32[]{:S(2)}, u32[]{:S(2)}) collective-permute-start(f32[32,480]{1,0:T(8,128)S(1)} %get-tuple-element.30), channel_id=1, source_target_pairs={{0,4},{2,6},{4,0},{6,2},{8,12},{10,14},{12,8},{14,10},{1,5},{3,7},... | collective-permute-start | bytes 184328 | tf_op jit(solution)/shard_map/ppermute | solution.py:284
  9.7 0.0 copy-start.1
  9.7 1.4 %collective-permute-start = (f32[32,480]{1,0:T(8,128)S(1)}, f32[32,480]{1,0:T(8,128)S(1)}, u32[]{:S(2)}, u32[]{:S(2)}) collective-permute-start(f32[32,480]{1,0:T(8,128)S(1)} %get-tuple-element.31), channel_id=1, source_target_pairs={{0,2},{2,0},{4,6},{6,4},{8,10},{10,8},{12,14},{14,12},{1,3},{3,1},... | collective-permute-start | bytes 184328 | tf_op jit(solution)/shard_map/ppermute | solution.py:284
  11.1 0.0 collective-permute-done.3
  11.2 3.7 %collective-permute-start.5 = (f32[32,480]{1,0:T(8,128)S(1)}, f32[32,480]{1,0:T(8,128)S(1)}, u32[]{:S(2)}, u32[]{:S(2)}) collective-permute-start(f32[32,480]{1,0:T(8,128)S(1)} %get-tuple-element.33), channel_id=1, source_target_pairs={{0,12},{2,14},{4,8},{6,10},{8,4},{10,6},{12,0},{14,2},{1,13},{3,15... | collective-permute-start | bytes 184328 | tf_op jit(solution)/shard_map/ppermute | solution.py:284
  14.9 0.0 collective-permute-start.4
  14.9 0.0 copy-done.1
  14.9 2.4 %shard_map.84 = (f32[32,256]{1,0:T(8,128)S(1)}, f32[8,16,480]{2,1,0:T(8,128)S(1)}, f32[8,32,480]{2,1,0:T(8,128)S(1)}) custom-call(s32[1]{0:T(128)} %bitcast.place_ref.own_ref, bf16[3840,128]{1,0:T(8,128)(2,1)S(1)} %get-tuple-element.17.geno_ref.refs_1_, s32[32,3840]{1,0:T(8,128)S(1)} %get-tuple-element.18.counts_ref, f32[32,128]{1,0:T(8,128)S(1)} %copy-done, ...), custom_call_target="tpu_custom_call" | custom-call | flops 800000000 | tf_op jit(solution)/shard_map/pallas_call | solution.py:260
  17.2 0.0 collective-permute-done.2.refs_3_
  17.2 0.0 collective-permute-done.1.refs_2_
  17.2 0.0 collective-permute-done.refs_1_
  17.2 0.4 collective-permute-done.5.refs_5_
  17.6 2.5 %collective-permute-done.4.refs_4_ = f32[32,480]{1,0:T(8,128)S(1)} collective-permute-done((f32[32,480]{1,0:T(8,128)S(1)}, f32[32,480]{1,0:T(8,128)S(1)}, u32[]{:S(2)}, u32[]{:S(2)}) %collective-permute-start.4) | collective-permute-done | bytes 61472 | tf_op jit(solution)/shard_map/ppermute | solution.py:284
  20.1 0.1 shard_map.86
  20.2 0.8 %collective-permute-start.9 = (f32[32,480]{1,0:T(8,128)S(1)}, f32[32,480]{1,0:T(8,128)S(1)}, u32[]{:S(2)}, u32[]{:S(2)}) collective-permute-start(f32[32,480]{1,0:T(8,128)S(1)} %get-tuple-element.21.q_ref.refs_0_), channel_id=1, source_target_pairs={{0,8},{2,10},{4,12},{6,14},{8,0},{10,2},{12,4},{14,6},{1,9},{3,11}... | collective-permute-start | bytes 184328 | tf_op jit(solution)/shard_map/ppermute | solution.py:284
  21.0 1.4 %collective-permute-start.7 = (f32[32,480]{1,0:T(8,128)S(1)}, f32[32,480]{1,0:T(8,128)S(1)}, u32[]{:S(2)}, u32[]{:S(2)}) collective-permute-start(f32[32,480]{1,0:T(8,128)S(1)} %get-tuple-element.21.q_ref.refs_0_), channel_id=1, source_target_pairs={{0,12},{2,14},{4,8},{6,10},{8,4},{10,6},{12,0},{14,2},{1,13},{3,15... | collective-permute-start | bytes 184328 | tf_op jit(solution)/shard_map/ppermute | solution.py:284
  22.4 1.3 %collective-permute-start.13 = (f32[32,480]{1,0:T(8,128)S(1)}, f32[32,480]{1,0:T(8,128)S(1)}, u32[]{:S(2)}, u32[]{:S(2)}) collective-permute-start(f32[32,480]{1,0:T(8,128)S(1)} %get-tuple-element.21.q_ref.refs_0_), channel_id=1, source_target_pairs={{0,4},{2,6},{4,0},{6,2},{8,12},{10,14},{12,8},{14,10},{1,5},{3,7},... | collective-permute-start | bytes 184328 | tf_op jit(solution)/shard_map/ppermute | solution.py:284
  23.7 1.3 %collective-permute-start.12 = (f32[32,480]{1,0:T(8,128)S(1)}, f32[32,480]{1,0:T(8,128)S(1)}, u32[]{:S(2)}, u32[]{:S(2)}) collective-permute-start(f32[32,480]{1,0:T(8,128)S(1)} %get-tuple-element.21.q_ref.refs_0_), channel_id=1, source_target_pairs={{0,2},{2,0},{4,6},{6,4},{8,10},{10,8},{12,14},{14,12},{1,3},{3,1},... | collective-permute-start | bytes 184328 | tf_op jit(solution)/shard_map/ppermute | solution.py:284
  25.0 0.9 %collective-permute-start.11 = (f32[32,480]{1,0:T(8,128)S(1)}, f32[32,480]{1,0:T(8,128)S(1)}, u32[]{:S(2)}, u32[]{:S(2)}) collective-permute-start(f32[32,480]{1,0:T(8,128)S(1)} %get-tuple-element.21.q_ref.refs_0_), channel_id=1, source_target_pairs={{0,6},{2,4},{4,2},{6,0},{8,14},{10,12},{12,10},{14,8},{1,7},{3,5},... | collective-permute-start | bytes 184328 | tf_op jit(solution)/shard_map/ppermute | solution.py:284
  25.9 0.7 %shard_map.88.refs_4_ = f32[544,128]{1,0:T(8,128)S(1)} custom-call(s32[1]{0:T(128)} %bitcast.place_ref.own_ref, f32[32,480]{1,0:T(8,128)S(1)} %get-tuple-element.21.q_ref.refs_0_, bf16[3840,128]{1,0:T(8,128)(2,1)S(1)} %get-tuple-element.17.geno_ref.refs_1_, f32[8,16,480]{2,1,0:T(8,128)S(1)} %get-tuple-element.28.refs_2_, f32[32,128]{1,0:T(8,128)S(1)} %copy-done), custom_call_target="tpu_custom_call" | custom-call | flops 280000000 | tf_op jit(solution)/shard_map/pallas_call | solution.py:260
  26.6 0.8 %collective-permute-done.9.refs_0_ = f32[32,480]{1,0:T(8,128)S(1)} collective-permute-done((f32[32,480]{1,0:T(8,128)S(1)}, f32[32,480]{1,0:T(8,128)S(1)}, u32[]{:S(2)}, u32[]{:S(2)}) %collective-permute-start.9) | collective-permute-done | bytes 61472 | tf_op jit(solution)/shard_map/ppermute | solution.py:284
  27.4 0.4 collective-permute-start.10
  27.8 0.0 collective-permute-done.7.refs_0_
  27.8 1.7 %collective-permute-start.8 = (f32[32,480]{1,0:T(8,128)S(1)}, f32[32,480]{1,0:T(8,128)S(1)}, u32[]{:S(2)}, u32[]{:S(2)}) collective-permute-start(f32[32,480]{1,0:T(8,128)S(1)} %collective-permute-done.7.refs_0_), channel_id=1, source_target_pairs={{0,2},{2,0},{4,6},{6,4},{8,10},{10,8},{12,14},{14,12},{1,3},{3,1},... | collective-permute-start | bytes 184328 | tf_op jit(solution)/shard_map/ppermute | solution.py:284
  29.4 0.0 collective-permute-done.13.refs_0_
  29.4 0.7 %shard_map.89.refs_4_ = f32[544,128]{1,0:T(8,128)S(1)} custom-call(s32[1]{0:T(128)} %bitcast.place_ref.own_ref, f32[32,480]{1,0:T(8,128)S(1)} %collective-permute-done.13.refs_0_, bf16[3840,128]{1,0:T(8,128)(2,1)S(1)} %get-tuple-element.17.geno_ref.refs_1_, f32[8,16,480]{2,1,0:T(8,128)S(1)} %get-tuple-element.28.refs_2_, ...), custom_call_target="tpu_custom_call", output_to_operand_aliasing={{}: (5, {})} | custom-call | flops 280000000 | tf_op jit(solution)/shard_map/pallas_call | solution.py:260
  30.1 0.0 collective-permute-done.12.refs_0_
  30.1 0.7 %shard_map.90.refs_4_ = f32[544,128]{1,0:T(8,128)S(1)} custom-call(s32[1]{0:T(128)} %bitcast.place_ref.own_ref, f32[32,480]{1,0:T(8,128)S(1)} %collective-permute-done.12.refs_0_, bf16[3840,128]{1,0:T(8,128)(2,1)S(1)} %get-tuple-element.17.geno_ref.refs_1_, f32[8,16,480]{2,1,0:T(8,128)S(1)} %get-tuple-element.28.refs_2_, ...), custom_call_target="tpu_custom_call", output_to_operand_aliasing={{}: (5, {})} | custom-call | flops 280000000 | tf_op jit(solution)/shard_map/pallas_call | solution.py:260
  30.8 0.7 %shard_map.91.refs_4_ = f32[544,128]{1,0:T(8,128)S(1)} custom-call(s32[1]{0:T(128)} %bitcast.place_ref.own_ref, f32[32,480]{1,0:T(8,128)S(1)} %collective-permute-done.9.refs_0_, bf16[3840,128]{1,0:T(8,128)(2,1)S(1)} %get-tuple-element.17.geno_ref.refs_1_, f32[8,16,480]{2,1,0:T(8,128)S(1)} %get-tuple-element.28.refs_2_, ...), custom_call_target="tpu_custom_call", output_to_operand_aliasing={{}: (5, {})} | custom-call | flops 280000000 | tf_op jit(solution)/shard_map/pallas_call | solution.py:260
  31.5 0.0 collective-permute-done.11.refs_0_
  31.5 0.7 %shard_map.92.refs_4_ = f32[544,128]{1,0:T(8,128)S(1)} custom-call(s32[1]{0:T(128)} %bitcast.place_ref.own_ref, f32[32,480]{1,0:T(8,128)S(1)} %collective-permute-done.11.refs_0_, bf16[3840,128]{1,0:T(8,128)(2,1)S(1)} %get-tuple-element.17.geno_ref.refs_1_, f32[8,16,480]{2,1,0:T(8,128)S(1)} %get-tuple-element.28.refs_2_, ...), custom_call_target="tpu_custom_call", output_to_operand_aliasing={{}: (5, {})} | custom-call | flops 280000000 | tf_op jit(solution)/shard_map/pallas_call | solution.py:260
  32.2 0.7 %shard_map.93.refs_4_ = f32[544,128]{1,0:T(8,128)S(1)} custom-call(s32[1]{0:T(128)} %bitcast.place_ref.own_ref, f32[32,480]{1,0:T(8,128)S(1)} %collective-permute-done.7.refs_0_, bf16[3840,128]{1,0:T(8,128)(2,1)S(1)} %get-tuple-element.17.geno_ref.refs_1_, f32[8,16,480]{2,1,0:T(8,128)S(1)} %get-tuple-element.28.refs_2_, ...), custom_call_target="tpu_custom_call", output_to_operand_aliasing={{}: (5, {})} | custom-call | flops 280000000 | tf_op jit(solution)/shard_map/pallas_call | solution.py:260
  32.9 0.0 collective-permute-done.10.refs_0_
  32.9 0.7 %shard_map.94.refs_4_ = f32[544,128]{1,0:T(8,128)S(1)} custom-call(s32[1]{0:T(128)} %bitcast.place_ref.own_ref, f32[32,480]{1,0:T(8,128)S(1)} %collective-permute-done.10.refs_0_, bf16[3840,128]{1,0:T(8,128)(2,1)S(1)} %get-tuple-element.17.geno_ref.refs_1_, f32[8,16,480]{2,1,0:T(8,128)S(1)} %get-tuple-element.28.refs_2_, ...), custom_call_target="tpu_custom_call", output_to_operand_aliasing={{}: (5, {})} | custom-call | flops 280000000 | tf_op jit(solution)/shard_map/pallas_call | solution.py:260
  33.6 0.0 collective-permute-done.8.refs_0_
  33.6 0.7 %shard_map.95.mine_ref = f32[544,128]{1,0:T(8,128)S(1)} custom-call(s32[1]{0:T(128)} %bitcast.place_ref.own_ref, f32[32,480]{1,0:T(8,128)S(1)} %collective-permute-done.8.refs_0_, bf16[3840,128]{1,0:T(8,128)(2,1)S(1)} %get-tuple-element.17.geno_ref.refs_1_, f32[8,16,480]{2,1,0:T(8,128)S(1)} %get-tuple-element.28.refs_2_, ...), custom_call_target="tpu_custom_call", output_to_operand_aliasing={{}: (5, {})} | custom-call | flops 280000000 | tf_op jit(solution)/shard_map/pallas_call | solution.py:260
  34.3 0.1 collective-permute-start.14
  34.4 0.5 %collective-permute-start.6 = (f32[32,256]{1,0:T(8,128)S(1)}, f32[32,256]{1,0:T(8,128)S(1)}, u32[]{:S(2)}, u32[]{:S(2)}) collective-permute-start(f32[32,256]{1,0:T(8,128)S(1)} %get-tuple-element.23.sums_ref), channel_id=1, source_target_pairs={{0,1},{1,0},{2,3},{3,2},{4,5},{5,4},{6,7},{7,6},{8,9},{9,8},{10,11... | collective-permute-start | bytes 98312 | tf_op jit(solution)/shard_map/ppermute | solution.py:287
  34.9 1.1 %collective-permute-done.6.other_ref = f32[32,256]{1,0:T(8,128)S(1)} collective-permute-done((f32[32,256]{1,0:T(8,128)S(1)}, f32[32,256]{1,0:T(8,128)S(1)}, u32[]{:S(2)}, u32[]{:S(2)}) %collective-permute-start.6) | collective-permute-done | bytes 32800 | tf_op jit(solution)/shard_map/ppermute | solution.py:287
  36.0 0.7 %shard_map.87 = (f32[32,480]{1,0:T(8,128)}, f32[32,480]{1,0:T(8,128)}, f32[32,128]{1,0:T(8,128)}, f32[32,128]{1,0:T(8,128)}) custom-call(s32[1]{0:T(128)} %bitcast.place_ref.own_ref, f32[32,480]{1,0:T(8,128)S(1)} %get-tuple-element.21.q_ref.refs_0_, f32[32,480]{1,0:T(8,128)S(1)} %get-tuple-element.22.grad_ref, f32[32,256]{1,0:T(8,128)S(1)} %get-tuple-element.23.sums_ref, ...), custom_call_target="tpu_custom_call" | custom-call | flops 240000000 | tf_op jit(solution)/shard_map/pallas_call | solution.py:260
  36.7 0.0 collective-permute-done.14.other_ref
  36.7 0.8 %shard_map.96 = f32[32,16,128]{2,1,0:T(8,128)} custom-call(s32[1]{0:T(128)} %bitcast.place_ref.own_ref, f32[544,128]{1,0:T(8,128)S(1)} %shard_map.95.mine_ref, f32[544,128]{1,0:T(8,128)S(1)} %collective-permute-done.14.other_ref), custom_call_target="tpu_custom_call" | custom-call | flops 120000000 | tf_op jit(solution)/shard_map/pallas_call | solution.py:260
  (4 shorter events, 0.1 us)
Async XLA Ops:
  3.5 3.1 %copy-start = (f32[32,128]{1,0:T(8,128)S(1)}, f32[32,128]{1,0:T(8,128)}, u32[]{:S(2)}) copy-start(f32[32,128]{1,0:T(8,128)} %refs_3_.15) | copy-start | bytes 49156
  3.5 7.6 %collective-permute-start.3 = (f32[2,32,480]{2,1,0:T(8,128)S(1)}, f32[2,32,480]{2,1,0:T(8,128)S(1)}, u32[]{:S(2)}, u32[]{:S(2)}) collective-permute-start(f32[2,32,480]{2,1,0:T(8,128)S(1)} %slice_bitcast_fusion), channel_id=1, source_target_pairs={{0,2},{2,0},{4,6},{6,4},{8,10},{10,8},{12,14},{14,12},{1,3},{3,1},... | collective-permute-start | bytes 368648 | tf_op jit(solution)/shard_map/ppermute | solution.py:284
  7.6 9.6 %collective-permute-start.2 = (f32[32,480]{1,0:T(8,128)S(1)}, f32[32,480]{1,0:T(8,128)S(1)}, u32[]{:S(2)}, u32[]{:S(2)}) collective-permute-start(f32[32,480]{1,0:T(8,128)S(1)} %get-tuple-element.29), channel_id=1, source_target_pairs={{0,6},{2,4},{4,2},{6,0},{8,14},{10,12},{12,10},{14,8},{1,7},{3,5},... | collective-permute-start | bytes 184328 | tf_op jit(solution)/shard_map/ppermute | solution.py:284
  9.3 8.0 %collective-permute-start.1 = (f32[32,480]{1,0:T(8,128)S(1)}, f32[32,480]{1,0:T(8,128)S(1)}, u32[]{:S(2)}, u32[]{:S(2)}) collective-permute-start(f32[32,480]{1,0:T(8,128)S(1)} %get-tuple-element.30), channel_id=1, source_target_pairs={{0,4},{2,6},{4,0},{6,2},{8,12},{10,14},{12,8},{14,10},{1,5},{3,7},... | collective-permute-start | bytes 184328 | tf_op jit(solution)/shard_map/ppermute | solution.py:284
  9.7 5.1 %copy-start.1 = (s32[3840,16]{0,1:T(8,128)S(1)}, s32[3840,16]{0,1:T(8,128)}, u32[]{:S(2)}) copy-start(s32[3840,16]{0,1:T(8,128)} %param.6) | copy-start | bytes 737284
  9.7 7.5 %collective-permute-start = (f32[32,480]{1,0:T(8,128)S(1)}, f32[32,480]{1,0:T(8,128)S(1)}, u32[]{:S(2)}, u32[]{:S(2)}) collective-permute-start(f32[32,480]{1,0:T(8,128)S(1)} %get-tuple-element.31), channel_id=1, source_target_pairs={{0,2},{2,0},{4,6},{6,4},{8,10},{10,8},{12,14},{14,12},{1,3},{3,1},... | collective-permute-start | bytes 184328 | tf_op jit(solution)/shard_map/ppermute | solution.py:284
  11.2 6.4 %collective-permute-start.5 = (f32[32,480]{1,0:T(8,128)S(1)}, f32[32,480]{1,0:T(8,128)S(1)}, u32[]{:S(2)}, u32[]{:S(2)}) collective-permute-start(f32[32,480]{1,0:T(8,128)S(1)} %get-tuple-element.33), channel_id=1, source_target_pairs={{0,12},{2,14},{4,8},{6,10},{8,4},{10,6},{12,0},{14,2},{1,13},{3,15... | collective-permute-start | bytes 184328 | tf_op jit(solution)/shard_map/ppermute | solution.py:284
  14.9 5.2 %collective-permute-start.4 = (f32[32,480]{1,0:T(8,128)S(1)}, f32[32,480]{1,0:T(8,128)S(1)}, u32[]{:S(2)}, u32[]{:S(2)}) collective-permute-start(f32[32,480]{1,0:T(8,128)S(1)} %get-tuple-element.34), channel_id=1, source_target_pairs={{0,8},{2,10},{4,12},{6,14},{8,0},{10,2},{12,4},{14,6},{1,9},{3,11}... | collective-permute-start | bytes 184328 | tf_op jit(solution)/shard_map/ppermute | solution.py:284
  20.2 7.2 %collective-permute-start.9 = (f32[32,480]{1,0:T(8,128)S(1)}, f32[32,480]{1,0:T(8,128)S(1)}, u32[]{:S(2)}, u32[]{:S(2)}) collective-permute-start(f32[32,480]{1,0:T(8,128)S(1)} %get-tuple-element.21.q_ref.refs_0_), channel_id=1, source_target_pairs={{0,8},{2,10},{4,12},{6,14},{8,0},{10,2},{12,4},{14,6},{1,9},{3,11}... | collective-permute-start | bytes 184328 | tf_op jit(solution)/shard_map/ppermute | solution.py:284
  21.0 6.8 %collective-permute-start.7 = (f32[32,480]{1,0:T(8,128)S(1)}, f32[32,480]{1,0:T(8,128)S(1)}, u32[]{:S(2)}, u32[]{:S(2)}) collective-permute-start(f32[32,480]{1,0:T(8,128)S(1)} %get-tuple-element.21.q_ref.refs_0_), channel_id=1, source_target_pairs={{0,12},{2,14},{4,8},{6,10},{8,4},{10,6},{12,0},{14,2},{1,13},{3,15... | collective-permute-start | bytes 184328 | tf_op jit(solution)/shard_map/ppermute | solution.py:284
  22.4 7.0 %collective-permute-start.13 = (f32[32,480]{1,0:T(8,128)S(1)}, f32[32,480]{1,0:T(8,128)S(1)}, u32[]{:S(2)}, u32[]{:S(2)}) collective-permute-start(f32[32,480]{1,0:T(8,128)S(1)} %get-tuple-element.21.q_ref.refs_0_), channel_id=1, source_target_pairs={{0,4},{2,6},{4,0},{6,2},{8,12},{10,14},{12,8},{14,10},{1,5},{3,7},... | collective-permute-start | bytes 184328 | tf_op jit(solution)/shard_map/ppermute | solution.py:284
  23.7 6.4 %collective-permute-start.12 = (f32[32,480]{1,0:T(8,128)S(1)}, f32[32,480]{1,0:T(8,128)S(1)}, u32[]{:S(2)}, u32[]{:S(2)}) collective-permute-start(f32[32,480]{1,0:T(8,128)S(1)} %get-tuple-element.21.q_ref.refs_0_), channel_id=1, source_target_pairs={{0,2},{2,0},{4,6},{6,4},{8,10},{10,8},{12,14},{14,12},{1,3},{3,1},... | collective-permute-start | bytes 184328 | tf_op jit(solution)/shard_map/ppermute | solution.py:284
  25.0 6.5 %collective-permute-start.11 = (f32[32,480]{1,0:T(8,128)S(1)}, f32[32,480]{1,0:T(8,128)S(1)}, u32[]{:S(2)}, u32[]{:S(2)}) collective-permute-start(f32[32,480]{1,0:T(8,128)S(1)} %get-tuple-element.21.q_ref.refs_0_), channel_id=1, source_target_pairs={{0,6},{2,4},{4,2},{6,0},{8,14},{10,12},{12,10},{14,8},{1,7},{3,5},... | collective-permute-start | bytes 184328 | tf_op jit(solution)/shard_map/ppermute | solution.py:284
  27.4 5.5 %collective-permute-start.10 = (f32[32,480]{1,0:T(8,128)S(1)}, f32[32,480]{1,0:T(8,128)S(1)}, u32[]{:S(2)}, u32[]{:S(2)}) collective-permute-start(f32[32,480]{1,0:T(8,128)S(1)} %collective-permute-done.9.refs_0_), channel_id=1, source_target_pairs={{0,2},{2,0},{4,6},{6,4},{8,10},{10,8},{12,14},{14,12},{1,3},{3,1},... | collective-permute-start | bytes 184328 | tf_op jit(solution)/shard_map/ppermute | solution.py:284
  27.8 5.9 %collective-permute-start.8 = (f32[32,480]{1,0:T(8,128)S(1)}, f32[32,480]{1,0:T(8,128)S(1)}, u32[]{:S(2)}, u32[]{:S(2)}) collective-permute-start(f32[32,480]{1,0:T(8,128)S(1)} %collective-permute-done.7.refs_0_), channel_id=1, source_target_pairs={{0,2},{2,0},{4,6},{6,4},{8,10},{10,8},{12,14},{14,12},{1,3},{3,1},... | collective-permute-start | bytes 184328 | tf_op jit(solution)/shard_map/ppermute | solution.py:284
  34.3 2.4 %collective-permute-start.14 = (f32[544,128]{1,0:T(8,128)S(1)}, f32[544,128]{1,0:T(8,128)S(1)}, u32[]{:S(2)}, u32[]{:S(2)}) collective-permute-start(f32[544,128]{1,0:T(8,128)S(1)} %shard_map.95.mine_ref), channel_id=1, source_target_pairs={{0,1},{1,0},{2,3},{3,2},{4,5},{5,4},{6,7},{7,6},{8,9},{9,8},{10,11... | collective-permute-start | bytes 835592 | tf_op jit(solution)/shard_map/ppermute | solution.py:287
  34.4 1.6 %collective-permute-start.6 = (f32[32,256]{1,0:T(8,128)S(1)}, f32[32,256]{1,0:T(8,128)S(1)}, u32[]{:S(2)}, u32[]{:S(2)}) collective-permute-start(f32[32,256]{1,0:T(8,128)S(1)} %get-tuple-element.23.sums_ref), channel_id=1, source_target_pairs={{0,1},{1,0},{2,3},{3,2},{4,5},{5,4},{6,7},{7,6},{8,9},{9,8},{10,11... | collective-permute-start | bytes 98312 | tf_op jit(solution)/shard_map/ppermute | solution.py:287

commit v6 on v5

--- a/solution.py
+++ b/solution.py
@@ -42,11 +42,9 @@
     width = dosage.shape[1]
     both = dot(jnp.concatenate([counts, counts], axis=0), table, TN)
     recon, total = both[:, :width], both[:, width:]
-    rest = total - recon
-    inverse = 1.0 / (recon * rest)
-    part_b = (2.0 - dosage) * recon * inverse
-    part = dosage * rest * inverse - part_b
-    return part, part_b, total
+    inverse = 1.0 / (recon * (total - recon))
+    part = (dosage * total - (recon + recon)) * inverse
+    return part, recon, inverse, total
 
 
 def half_gradient(shares, place, start, geno_ref, counts_ref, freqs, grad_ref, excess_ref, before):
@@ -58,7 +56,7 @@
         first = pl.multiple_of(start + row, LANES)
         counts = counts_ref[:, pl.ds(first, LANES)].astype(F32).astype(BF16)
         dosage = geno_ref[pl.ds(first, LANES), :].astype(F32)
-        part, _, total = ratio_parts(counts, dosage, table)
+        part, _, _, total = ratio_parts(counts, dosage, table)
         high, low = split(part * total)
         excess_ref[pl.ds(row, LANES), :width] = high
         excess_ref[pl.ds(row, LANES), width:] = low
@@ -92,7 +90,7 @@
     freqs_copy.start()
     moves = [pair(far + i * size, size, i) for i in range(pieces)]
     moves.append(pair(near, half_rows, pieces))
-    for move in moves:
+    for move in moves[:pieces]:
         for copy in move:
             copy.start()
     freqs_copy.wait()
@@ -101,6 +99,9 @@
         if row % size == 0:
             for copy in moves[row // size]:
                 copy.wait()
+        if row == half_rows // 2 // size * size:
+            for copy in moves[pieces]:
+                copy.start()
 
     half_gradient(shares, place, far, geno_ref, counts_ref, freqs_ref[...], grad_ref, excess_ref, before)
     for copy in moves[pieces]:
@@ -115,23 +116,32 @@
     )
 
 
-def sums_kernel(place_ref, geno_ref, counts_ref, freqs_ref, resid_ref, sums_ref, traits_ref, own_ref, parts_ref):
-    rows, width = geno_ref.shape
+def sums_kernel(first, place_ref, geno_ref, counts_ref, freqs_ref, *refs):
+    other_ref, refs = refs[0], refs[1:]
+    sums_ref, parts_ref = refs[0], refs[-1]
+    half_rows = parts_ref.shape[0] // 2
+    width = freqs_ref.shape[1]
+    start = 0 if first else half_rows
     table = count_table(freqs_ref[...])
-    for row in range(0, rows, LANES):
-        counts = counts_ref[:, pl.ds(row, LANES)].astype(F32).astype(BF16)
-        dosage = geno_ref[pl.ds(row, LANES), :].astype(F32)
-        part, part_b, _ = ratio_parts(counts, dosage, table)
-        for at, value in enumerate((part, part_b)):
+    for row in range(0, half_rows, LANES):
+        counts = counts_ref[:, pl.ds(start + row, LANES)].astype(F32).astype(BF16)
+        dosage = geno_ref[pl.ds(start + row, LANES), :].astype(F32)
+        part, recon, inverse, _ = ratio_parts(counts, dosage, table)
+        for at, value in enumerate((part, (2.0 - dosage) * (recon * inverse))):
             high, low = split(value)
             parts_ref[pl.ds(row, LANES), pl.ds(at * width, width)] = high
-            parts_ref[pl.ds(rows + row, LANES), pl.ds(at * width, width)] = low
+            parts_ref[pl.ds(half_rows + row, LANES), pl.ds(at * width, width)] = low
+    left = counts_ref[:, pl.ds(start, half_rows)].astype(F32).astype(BF16)
+    sums = dot(jnp.concatenate([left, left], axis=1), parts_ref[...], NN)
+    if not first:
+        sums_ref[...] = sums + other_ref[...]
+        return
+    sums_ref[...] = sums
+    traits_ref, own_ref = refs[1:3]
+    residual = other_ref[...].astype(F32) / 1000.0
     counts = counts_ref[...].astype(F32)
-    left = counts.astype(BF16)
-    sums_ref[...] = dot(jnp.concatenate([left, left], axis=1), parts_ref[...], NN)
-    residual = resid_ref[...].astype(F32) / 1000.0
     share = traits_ref.shape[2]
-    for c in range(rows // share):
+    for c in range(traits_ref.shape[0]):
         traits_ref[c] = residual[:, c * share : (c + 1) * share]
         own_ref[c] = counts[:, c * share : (c + 1) * share]
 
@@ -309,11 +319,20 @@
     arrived = [near[0]] + [move(near[m], m) for m in range(1, half)]
     arrived += [move(joined[c], half + 2 * c) for c in range(half // 2)]
 
+    halves = VMEM((rows, 2 * width), BF16)
     sums, trait_parts, count_parts = call(
-        sums_kernel,
+        functools.partial(sums_kernel, True),
         (place, geno, counts, freqs, residuals.T),
         [(anc, 2 * width), (var_count, traits, share), (var_count, anc, share)],
-        [VMEM((2 * rows, 2 * width), BF16)],
+        [halves],
+        cost=1200,
+    )
+    (sums,) = call(
+        functools.partial(sums_kernel, False),
+        (place, geno, counts, freqs, sums),
+        [(anc, 2 * width)],
+        [halves],
+        cost=1000,
     )
     sums_other = swap(sums)
 
@@ -325,13 +344,16 @@
     )
 
     shares = {0: q_new}
-    for m in (*range(half, var_count, 2), *range(1, half)):
+    for m in (*range(half, var_count, 2), *range(2, half, 2), 1):
         shares[m] = move(q_new, m)
-    for m in range(half + 1, var_count, 2):
-        shares[m] = move(shares[m - 1], 1)
+    early = range(2, var_count - 2, 2)
+    passed = move(jnp.stack([shares[m] for m in early]), 1)
+    for at, m in enumerate(early):
+        shares[m + 1] = passed[at]
+    shares[var_count - 1] = move(shares[var_count - 2], 1)
 
     total = None
-    for m in (0, 2, 1, 4, 3, 6, 5, 7) if var_count == 8 else range(var_count):
+    for m in (0, 2, 1, 4, 6, 3, 5, 7) if var_count == 8 else range(var_count):
         inputs = (geno, trait_parts, freqs) + (() if total is None else (total,))
         (total,) = call(
             functools.partial(score_kernel, (m,), total is None),

time: 37.7 us -> 40.3 us (1.069)
  waiting for transfers between devices: 4.8 us -> 6.65 us
    ppermute x13 -> x12, waiting for transfers between devices: 3.7 us -> 5.79 us  [move(): return lax.ppermute(x, 'var', [(i, i ^ m) for i in range(var_count)])]
    ppermute x13 -> x12, starting transfers between devices: 18 us -> 18.5 us  [move(): return lax.ppermute(x, 'var', [(i, i ^ m) for i in range(var_count)])]
    pallas_call x14 -> x15, Pallas kernels: 13.2 us -> 13.4 us  [call(): pl.pallas_call(kernel, in_specs=specs, out_specs=out_specs, out_shape=out...]
  transfers between devices with their start and end apart: 15 -> 14, of which waited for: 4 -> 5; matrix products, arithmetic and copies ran while one was open for 0% -> 0% of each run, Pallas kernels for 23% -> 23%
where the time goes in v6:
time: 40.3 us; the launch traced here: 40.1 us
  starting transfers between devices  19 us (47%)
  Pallas kernels  13.4 us (33%)
  waiting for transfers between devices  6.65 us (17%)
  between operations  0.84 us (2%)
    ppermute x12, starting transfers between devices, move(): return lax.ppermute(x, 'var', [(i, i ^ m) for i in range(var_count)])  18.5 us
    pallas_call x15, Pallas kernels, call(): pl.pallas_call(kernel, in_specs=specs, out_specs=out_specs, out_shape=out...  13.4 us
    ppermute x12, waiting for transfers between devices, move(): return lax.ppermute(x, 'var', [(i, i ^ m) for i in range(var_count)])  5.79 us
    ppermute x2, waiting for transfers between devices, swap(): return lax.ppermute(x, 'smp', [(0, 1), (1, 0)])  0.86 us
  transfers between devices with their start and end apart: 14, of which 5 were waited for; matrix products, arithmetic and copies ran while one was open for 0% of the time, Pallas kernels for 23%

profile of v6, /device:TPU:0, one launch (start us, length us, event | category | flops | bytes accessed | tf_op | source)
XLA Modules:
  0.0 40.1 jit_solution(11991428859631240372)
XLA Ops:
  0.6 2.8 %shard_map.83 = (f32[4,32,480]{2,1,0:T(8,128)S(1)}, bf16[3840,128]{1,0:T(8,128)(2,1)S(1)}, s32[32,3840]{1,0:T(8,128)S(1)}) custom-call(s32[1]{0:T(128)} %bitcast.place_ref.own_ref, bf16[3840,128]{1,0:T(8,128)(2,1)} %geno_hbm.1, s32[32,3840]{1,0:T(8,128)} %bitcast.39, f32[32,128]{1,0:T(8,128)} %refs_3_.15), custom_call_target="tpu_custom_call" | custom-call | flops 800000000 | tf_op jit(solution)/shard_map/pallas_call | solution.py:270
  3.5 0.0 copy-start
  3.5 3.0 %collective-permute-start.3 = (f32[2,32,480]{2,1,0:T(8,128)S(1)}, f32[2,32,480]{2,1,0:T(8,128)S(1)}, u32[]{:S(2)}, u32[]{:S(2)}) collective-permute-start(f32[2,32,480]{2,1,0:T(8,128)S(1)} %slice_bitcast_fusion), channel_id=1, source_target_pairs={{0,2},{2,0},{4,6},{6,4},{8,10},{10,8},{12,14},{14,12},{1,3},{3,1},... | collective-permute-start | bytes 368648 | tf_op jit(solution)/shard_map/ppermute | solution.py:294
  6.5 0.0 copy-done
  6.5 0.9 %shard_map.85 = f32[4,32,480]{2,1,0:T(8,128)S(1)} custom-call(s32[1]{0:T(128)} %bitcast.place_ref.own_ref, bf16[3840,128]{1,0:T(8,128)(2,1)S(1)} %get-tuple-element.17.geno_ref.refs_1_, s32[32,3840]{1,0:T(8,128)S(1)} %get-tuple-element.18.counts_ref, f32[32,128]{1,0:T(8,128)S(1)} %copy-done), custom_call_target="tpu_custom_call" | custom-call | flops 800000000 | tf_op jit(solution)/shard_map/pallas_call | solution.py:270
  7.5 1.7 %collective-permute-start.2 = (f32[32,480]{1,0:T(8,128)S(1)}, f32[32,480]{1,0:T(8,128)S(1)}, u32[]{:S(2)}, u32[]{:S(2)}) collective-permute-start(f32[32,480]{1,0:T(8,128)S(1)} %get-tuple-element.29), channel_id=1, source_target_pairs={{0,6},{2,4},{4,2},{6,0},{8,14},{10,12},{12,10},{14,8},{1,7},{3,5},... | collective-permute-start | bytes 184328 | tf_op jit(solution)/shard_map/ppermute | solution.py:294
  9.2 0.5 %collective-permute-start.1 = (f32[32,480]{1,0:T(8,128)S(1)}, f32[32,480]{1,0:T(8,128)S(1)}, u32[]{:S(2)}, u32[]{:S(2)}) collective-permute-start(f32[32,480]{1,0:T(8,128)S(1)} %get-tuple-element.30), channel_id=1, source_target_pairs={{0,4},{2,6},{4,0},{6,2},{8,12},{10,14},{12,8},{14,10},{1,5},{3,7},... | collective-permute-start | bytes 184328 | tf_op jit(solution)/shard_map/ppermute | solution.py:294
  9.7 0.0 copy-start.1
  9.7 1.4 %collective-permute-start = (f32[32,480]{1,0:T(8,128)S(1)}, f32[32,480]{1,0:T(8,128)S(1)}, u32[]{:S(2)}, u32[]{:S(2)}) collective-permute-start(f32[32,480]{1,0:T(8,128)S(1)} %get-tuple-element.31), channel_id=1, source_target_pairs={{0,2},{2,0},{4,6},{6,4},{8,10},{10,8},{12,14},{14,12},{1,3},{3,1},... | collective-permute-start | bytes 184328 | tf_op jit(solution)/shard_map/ppermute | solution.py:294
  11.1 0.0 collective-permute-done.3
  11.1 3.7 %collective-permute-start.5 = (f32[32,480]{1,0:T(8,128)S(1)}, f32[32,480]{1,0:T(8,128)S(1)}, u32[]{:S(2)}, u32[]{:S(2)}) collective-permute-start(f32[32,480]{1,0:T(8,128)S(1)} %get-tuple-element.35), channel_id=1, source_target_pairs={{0,12},{2,14},{4,8},{6,10},{8,4},{10,6},{12,0},{14,2},{1,13},{3,15... | collective-permute-start | bytes 184328 | tf_op jit(solution)/shard_map/ppermute | solution.py:294
  14.8 0.0 collective-permute-start.4
  14.8 0.0 copy-done.1
  14.8 1.3 %shard_map.84 = (f32[32,256]{1,0:T(8,128)S(1)}, f32[8,16,480]{2,1,0:T(8,128)S(1)}, f32[8,32,480]{2,1,0:T(8,128)S(1)}) custom-call(s32[1]{0:T(128)} %bitcast.place_ref.own_ref, bf16[3840,128]{1,0:T(8,128)(2,1)S(1)} %get-tuple-element.17.geno_ref.refs_1_, s32[32,3840]{1,0:T(8,128)S(1)} %get-tuple-element.18.counts_ref, f32[32,128]{1,0:T(8,128)S(1)} %copy-done, ...), custom_call_target="tpu_custom_call" | custom-call | flops 480000000 | tf_op jit(solution)/shard_map/pallas_call | solution.py:270
  16.1 0.0 collective-permute-done.2.refs_3_
  16.1 0.0 collective-permute-done.1.refs_2_
  16.2 0.0 collective-permute-done.refs_1_
  16.2 1.4 %collective-permute-done.5.refs_5_ = f32[32,480]{1,0:T(8,128)S(1)} collective-permute-done((f32[32,480]{1,0:T(8,128)S(1)}, f32[32,480]{1,0:T(8,128)S(1)}, u32[]{:S(2)}, u32[]{:S(2)}) %collective-permute-start.5) | collective-permute-done | bytes 61472 | tf_op jit(solution)/shard_map/ppermute | solution.py:294
  17.5 2.5 %collective-permute-done.4.refs_4_ = f32[32,480]{1,0:T(8,128)S(1)} collective-permute-done((f32[32,480]{1,0:T(8,128)S(1)}, f32[32,480]{1,0:T(8,128)S(1)}, u32[]{:S(2)}, u32[]{:S(2)}) %collective-permute-start.4) | collective-permute-done | bytes 61472 | tf_op jit(solution)/shard_map/ppermute | solution.py:294
  20.0 0.1 shard_map.86
  20.1 0.8 %collective-permute-start.10 = (f32[32,480]{1,0:T(8,128)S(1)}, f32[32,480]{1,0:T(8,128)S(1)}, u32[]{:S(2)}, u32[]{:S(2)}) collective-permute-start(f32[32,480]{1,0:T(8,128)S(1)} %get-tuple-element.21.q_ref.refs_0_), channel_id=1, source_target_pairs={{0,8},{2,10},{4,12},{6,14},{8,0},{10,2},{12,4},{14,6},{1,9},{3,11}... | collective-permute-start | bytes 184328 | tf_op jit(solution)/shard_map/ppermute | solution.py:294
  20.9 1.9 %collective-permute-start.9 = (f32[32,480]{1,0:T(8,128)S(1)}, f32[32,480]{1,0:T(8,128)S(1)}, u32[]{:S(2)}, u32[]{:S(2)}) collective-permute-start(f32[32,480]{1,0:T(8,128)S(1)} %get-tuple-element.21.q_ref.refs_0_), channel_id=1, source_target_pairs={{0,4},{2,6},{4,0},{6,2},{8,12},{10,14},{12,8},{14,10},{1,5},{3,7},... | collective-permute-start | bytes 184328 | tf_op jit(solution)/shard_map/ppermute | solution.py:294
  22.8 1.0 %collective-permute-start.12 = (f32[32,480]{1,0:T(8,128)S(1)}, f32[32,480]{1,0:T(8,128)S(1)}, u32[]{:S(2)}, u32[]{:S(2)}) collective-permute-start(f32[32,480]{1,0:T(8,128)S(1)} %get-tuple-element.21.q_ref.refs_0_), channel_id=1, source_target_pairs={{0,2},{2,0},{4,6},{6,4},{8,10},{10,8},{12,14},{14,12},{1,3},{3,1},... | collective-permute-start | bytes 184328 | tf_op jit(solution)/shard_map/ppermute | solution.py:294
  23.8 2.1 %collective-permute-start.7 = (f32[32,480]{1,0:T(8,128)S(1)}, f32[32,480]{1,0:T(8,128)S(1)}, u32[]{:S(2)}, u32[]{:S(2)}) collective-permute-start(f32[32,480]{1,0:T(8,128)S(1)} %get-tuple-element.21.q_ref.refs_0_), channel_id=1, source_target_pairs={{0,12},{2,14},{4,8},{6,10},{8,4},{10,6},{12,0},{14,2},{1,13},{3,15... | collective-permute-start | bytes 184328 | tf_op jit(solution)/shard_map/ppermute | solution.py:294
  25.9 0.8 %collective-permute-done.10.refs_0_ = f32[32,480]{1,0:T(8,128)S(1)} collective-permute-done((f32[32,480]{1,0:T(8,128)S(1)}, f32[32,480]{1,0:T(8,128)S(1)}, u32[]{:S(2)}, u32[]{:S(2)}) %collective-permute-start.10) | collective-permute-done | bytes 61472 | tf_op jit(solution)/shard_map/ppermute | solution.py:294
  26.7 0.0 collective-permute-done.9.refs_0_
  26.7 1.4 %collective-permute-start.11 = (f32[2,32,480]{2,1,0:T(8,128)S(1)}, f32[2,32,480]{2,1,0:T(8,128)S(1)}, u32[]{:S(2)}, u32[]{:S(2)}) collective-permute-start(f32[2,32,480]{2,1,0:T(8,128)S(1)} %pad_maximum_fusion), channel_id=1, source_target_pairs={{0,2},{2,0},{4,6},{6,4},{8,10},{10,8},{12,14},{14,12},{1,3},{3,1},... | collective-permute-start | bytes 368648 | tf_op jit(solution)/shard_map/ppermute | solution.py:294
  28.0 0.7 %shard_map.89.refs_4_ = f32[544,128]{1,0:T(8,128)S(1)} custom-call(s32[1]{0:T(128)} %bitcast.place_ref.own_ref, f32[32,480]{1,0:T(8,128)S(1)} %get-tuple-element.21.q_ref.refs_0_, bf16[3840,128]{1,0:T(8,128)(2,1)S(1)} %get-tuple-element.17.geno_ref.refs_1_, f32[8,16,480]{2,1,0:T(8,128)S(1)} %get-tuple-element.28.refs_2_, f32[32,128]{1,0:T(8,128)S(1)} %copy-done), custom_call_target="tpu_custom_call" | custom-call | flops 280000000 | tf_op jit(solution)/shard_map/pallas_call | solution.py:270
  28.7 1.1 %collective-permute-done.7.refs_0_ = f32[32,480]{1,0:T(8,128)S(1)} collective-permute-done((f32[32,480]{1,0:T(8,128)S(1)}, f32[32,480]{1,0:T(8,128)S(1)}, u32[]{:S(2)}, u32[]{:S(2)}) %collective-permute-start.7) | collective-permute-done | bytes 61472 | tf_op jit(solution)/shard_map/ppermute | solution.py:294
  29.9 1.1 %collective-permute-start.8 = (f32[32,480]{1,0:T(8,128)S(1)}, f32[32,480]{1,0:T(8,128)S(1)}, u32[]{:S(2)}, u32[]{:S(2)}) collective-permute-start(f32[32,480]{1,0:T(8,128)S(1)} %collective-permute-done.7.refs_0_), channel_id=1, source_target_pairs={{0,2},{2,0},{4,6},{6,4},{8,10},{10,8},{12,14},{14,12},{1,3},{3,1},... | collective-permute-start | bytes 184328 | tf_op jit(solution)/shard_map/ppermute | solution.py:294
  30.9 0.7 %shard_map.90.refs_4_ = f32[544,128]{1,0:T(8,128)S(1)} custom-call(s32[1]{0:T(128)} %bitcast.place_ref.own_ref, f32[32,480]{1,0:T(8,128)S(1)} %collective-permute-done.9.refs_0_, bf16[3840,128]{1,0:T(8,128)(2,1)S(1)} %get-tuple-element.17.geno_ref.refs_1_, f32[8,16,480]{2,1,0:T(8,128)S(1)} %get-tuple-element.28.refs_2_, ...), custom_call_target="tpu_custom_call", output_to_operand_aliasing={{}: (5, {})} | custom-call | flops 280000000 | tf_op jit(solution)/shard_map/pallas_call | solution.py:270
  31.6 0.0 collective-permute-done.12.refs_0_
  31.6 0.7 %shard_map.91.refs_4_ = f32[544,128]{1,0:T(8,128)S(1)} custom-call(s32[1]{0:T(128)} %bitcast.place_ref.own_ref, f32[32,480]{1,0:T(8,128)S(1)} %collective-permute-done.12.refs_0_, bf16[3840,128]{1,0:T(8,128)(2,1)S(1)} %get-tuple-element.17.geno_ref.refs_1_, f32[8,16,480]{2,1,0:T(8,128)S(1)} %get-tuple-element.28.refs_2_, ...), custom_call_target="tpu_custom_call", output_to_operand_aliasing={{}: (5, {})} | custom-call | flops 280000000 | tf_op jit(solution)/shard_map/pallas_call | solution.py:270
  32.3 0.7 %shard_map.92.refs_4_ = f32[544,128]{1,0:T(8,128)S(1)} custom-call(s32[1]{0:T(128)} %bitcast.place_ref.own_ref, f32[32,480]{1,0:T(8,128)S(1)} %collective-permute-done.10.refs_0_, bf16[3840,128]{1,0:T(8,128)(2,1)S(1)} %get-tuple-element.17.geno_ref.refs_1_, f32[8,16,480]{2,1,0:T(8,128)S(1)} %get-tuple-element.28.refs_2_, ...), custom_call_target="tpu_custom_call", output_to_operand_aliasing={{}: (5, {})} | custom-call | flops 280000000 | tf_op jit(solution)/shard_map/pallas_call | solution.py:270
  33.0 0.7 %shard_map.93.refs_4_ = f32[544,128]{1,0:T(8,128)S(1)} custom-call(s32[1]{0:T(128)} %bitcast.place_ref.own_ref, f32[32,480]{1,0:T(8,128)S(1)} %collective-permute-done.7.refs_0_, bf16[3840,128]{1,0:T(8,128)(2,1)S(1)} %get-tuple-element.17.geno_ref.refs_1_, f32[8,16,480]{2,1,0:T(8,128)S(1)} %get-tuple-element.28.refs_2_, ...), custom_call_target="tpu_custom_call", output_to_operand_aliasing={{}: (5, {})} | custom-call | flops 280000000 | tf_op jit(solution)/shard_map/pallas_call | solution.py:270
  33.7 0.0 collective-permute-done.11
  33.7 0.7 %shard_map.94.refs_4_ = f32[544,128]{1,0:T(8,128)S(1)} custom-call(s32[1]{0:T(128)} %bitcast.place_ref.own_ref, f32[32,480]{1,0:T(8,128)S(1)} %get-tuple-element.33.refs_0_, bf16[3840,128]{1,0:T(8,128)(2,1)S(1)} %get-tuple-element.17.geno_ref.refs_1_, f32[8,16,480]{2,1,0:T(8,128)S(1)} %get-tuple-element.28.refs_2_, ...), custom_call_target="tpu_custom_call", output_to_operand_aliasing={{}: (5, {})} | custom-call | flops 280000000 | tf_op jit(solution)/shard_map/pallas_call | solution.py:270
  34.4 0.7 %shard_map.95.refs_4_ = f32[544,128]{1,0:T(8,128)S(1)} custom-call(s32[1]{0:T(128)} %bitcast.place_ref.own_ref, f32[32,480]{1,0:T(8,128)S(1)} %get-tuple-element.34.refs_0_, bf16[3840,128]{1,0:T(8,128)(2,1)S(1)} %get-tuple-element.17.geno_ref.refs_1_, f32[8,16,480]{2,1,0:T(8,128)S(1)} %get-tuple-element.28.refs_2_, ...), custom_call_target="tpu_custom_call", output_to_operand_aliasing={{}: (5, {})} | custom-call | flops 280000000 | tf_op jit(solution)/shard_map/pallas_call | solution.py:270
  35.1 0.0 collective-permute-done.8.refs_0_
  35.1 0.7 %shard_map.96.mine_ref = f32[544,128]{1,0:T(8,128)S(1)} custom-call(s32[1]{0:T(128)} %bitcast.place_ref.own_ref, f32[32,480]{1,0:T(8,128)S(1)} %collective-permute-done.8.refs_0_, bf16[3840,128]{1,0:T(8,128)(2,1)S(1)} %get-tuple-element.17.geno_ref.refs_1_, f32[8,16,480]{2,1,0:T(8,128)S(1)} %get-tuple-element.28.refs_2_, ...), custom_call_target="tpu_custom_call", output_to_operand_aliasing={{}: (5, {})} | custom-call | flops 280000000 | tf_op jit(solution)/shard_map/pallas_call | solution.py:270
  35.8 0.1 collective-permute-start.13
  35.9 1.3 %shard_map.87.sums_ref = f32[32,256]{1,0:T(8,128)S(1)} custom-call(s32[1]{0:T(128)} %bitcast.place_ref.own_ref, bf16[3840,128]{1,0:T(8,128)(2,1)S(1)} %get-tuple-element.17.geno_ref.refs_1_, s32[32,3840]{1,0:T(8,128)S(1)} %get-tuple-element.18.counts_ref, f32[32,128]{1,0:T(8,128)S(1)} %copy-done, f32[32,256]{1,0:T(8,128)S(1)} %get-tuple-element.23.refs_0_), custom_call_target="tpu_custom_call" | custom-call | flops 400000000 | tf_op jit(solution)/shard_map/pallas_call | solution.py:270
  37.2 0.5 %collective-permute-start.6 = (f32[32,256]{1,0:T(8,128)S(1)}, f32[32,256]{1,0:T(8,128)S(1)}, u32[]{:S(2)}, u32[]{:S(2)}) collective-permute-start(f32[32,256]{1,0:T(8,128)S(1)} %shard_map.87.sums_ref), channel_id=1, source_target_pairs={{0,1},{1,0},{2,3},{3,2},{4,5},{5,4},{6,7},{7,6},{8,9},{9,8},{10,11... | collective-permute-start | bytes 98312 | tf_op jit(solution)/shard_map/ppermute | solution.py:297
  37.7 0.9 %collective-permute-done.6.other_ref = f32[32,256]{1,0:T(8,128)S(1)} collective-permute-done((f32[32,256]{1,0:T(8,128)S(1)}, f32[32,256]{1,0:T(8,128)S(1)}, u32[]{:S(2)}, u32[]{:S(2)}) %collective-permute-start.6) | collective-permute-done | bytes 32800 | tf_op jit(solution)/shard_map/ppermute | solution.py:297
  38.6 0.7 %shard_map.88 = (f32[32,480]{1,0:T(8,128)}, f32[32,480]{1,0:T(8,128)}, f32[32,128]{1,0:T(8,128)}, f32[32,128]{1,0:T(8,128)}) custom-call(s32[1]{0:T(128)} %bitcast.place_ref.own_ref, f32[32,480]{1,0:T(8,128)S(1)} %get-tuple-element.21.q_ref.refs_0_, f32[32,480]{1,0:T(8,128)S(1)} %get-tuple-element.22.grad_ref, f32[32,256]{1,0:T(8,128)S(1)} %shard_map.87.sums_ref, ...), custom_call_target="tpu_custom_call" | custom-call | flops 240000000 | tf_op jit(solution)/shard_map/pallas_call | solution.py:270
  39.3 0.0 collective-permute-done.13.other_ref
  39.3 0.8 %shard_map.97 = f32[32,16,128]{2,1,0:T(8,128)} custom-call(s32[1]{0:T(128)} %bitcast.place_ref.own_ref, f32[544,128]{1,0:T(8,128)S(1)} %shard_map.96.mine_ref, f32[544,128]{1,0:T(8,128)S(1)} %collective-permute-done.13.other_ref), custom_call_target="tpu_custom_call" | custom-call | flops 120000000 | tf_op jit(solution)/shard_map/pallas_call | solution.py:270
  (6 shorter events, 0.1 us)
Async XLA Ops:
  3.5 3.1 %copy-start = (f32[32,128]{1,0:T(8,128)S(1)}, f32[32,128]{1,0:T(8,128)}, u32[]{:S(2)}) copy-start(f32[32,128]{1,0:T(8,128)} %refs_3_.15) | copy-start | bytes 49156
  3.5 7.6 %collective-permute-start.3 = (f32[2,32,480]{2,1,0:T(8,128)S(1)}, f32[2,32,480]{2,1,0:T(8,128)S(1)}, u32[]{:S(2)}, u32[]{:S(2)}) collective-permute-start(f32[2,32,480]{2,1,0:T(8,128)S(1)} %slice_bitcast_fusion), channel_id=1, source_target_pairs={{0,2},{2,0},{4,6},{6,4},{8,10},{10,8},{12,14},{14,12},{1,3},{3,1},... | collective-permute-start | bytes 368648 | tf_op jit(solution)/shard_map/ppermute | solution.py:294
  7.5 8.6 %collective-permute-start.2 = (f32[32,480]{1,0:T(8,128)S(1)}, f32[32,480]{1,0:T(8,128)S(1)}, u32[]{:S(2)}, u32[]{:S(2)}) collective-permute-start(f32[32,480]{1,0:T(8,128)S(1)} %get-tuple-element.29), channel_id=1, source_target_pairs={{0,6},{2,4},{4,2},{6,0},{8,14},{10,12},{12,10},{14,8},{1,7},{3,5},... | collective-permute-start | bytes 184328 | tf_op jit(solution)/shard_map/ppermute | solution.py:294
  9.2 6.9 %collective-permute-start.1 = (f32[32,480]{1,0:T(8,128)S(1)}, f32[32,480]{1,0:T(8,128)S(1)}, u32[]{:S(2)}, u32[]{:S(2)}) collective-permute-start(f32[32,480]{1,0:T(8,128)S(1)} %get-tuple-element.30), channel_id=1, source_target_pairs={{0,4},{2,6},{4,0},{6,2},{8,12},{10,14},{12,8},{14,10},{1,5},{3,7},... | collective-permute-start | bytes 184328 | tf_op jit(solution)/shard_map/ppermute | solution.py:294
  9.7 5.1 %copy-start.1 = (s32[3840,16]{0,1:T(8,128)S(1)}, s32[3840,16]{0,1:T(8,128)}, u32[]{:S(2)}) copy-start(s32[3840,16]{0,1:T(8,128)} %param.6) | copy-start | bytes 737284
  9.7 6.5 %collective-permute-start = (f32[32,480]{1,0:T(8,128)S(1)}, f32[32,480]{1,0:T(8,128)S(1)}, u32[]{:S(2)}, u32[]{:S(2)}) collective-permute-start(f32[32,480]{1,0:T(8,128)S(1)} %get-tuple-element.31), channel_id=1, source_target_pairs={{0,2},{2,0},{4,6},{6,4},{8,10},{10,8},{12,14},{14,12},{1,3},{3,1},... | collective-permute-start | bytes 184328 | tf_op jit(solution)/shard_map/ppermute | solution.py:294
  11.1 6.4 %collective-permute-start.5 = (f32[32,480]{1,0:T(8,128)S(1)}, f32[32,480]{1,0:T(8,128)S(1)}, u32[]{:S(2)}, u32[]{:S(2)}) collective-permute-start(f32[32,480]{1,0:T(8,128)S(1)} %get-tuple-element.35), channel_id=1, source_target_pairs={{0,12},{2,14},{4,8},{6,10},{8,4},{10,6},{12,0},{14,2},{1,13},{3,15... | collective-permute-start | bytes 184328 | tf_op jit(solution)/shard_map/ppermute | solution.py:294
  14.8 5.2 %collective-permute-start.4 = (f32[32,480]{1,0:T(8,128)S(1)}, f32[32,480]{1,0:T(8,128)S(1)}, u32[]{:S(2)}, u32[]{:S(2)}) collective-permute-start(f32[32,480]{1,0:T(8,128)S(1)} %get-tuple-element.36), channel_id=1, source_target_pairs={{0,8},{2,10},{4,12},{6,14},{8,0},{10,2},{12,4},{14,6},{1,9},{3,11}... | collective-permute-start | bytes 184328 | tf_op jit(solution)/shard_map/ppermute | solution.py:294
  20.1 6.6 %collective-permute-start.10 = (f32[32,480]{1,0:T(8,128)S(1)}, f32[32,480]{1,0:T(8,128)S(1)}, u32[]{:S(2)}, u32[]{:S(2)}) collective-permute-start(f32[32,480]{1,0:T(8,128)S(1)} %get-tuple-element.21.q_ref.refs_0_), channel_id=1, source_target_pairs={{0,8},{2,10},{4,12},{6,14},{8,0},{10,2},{12,4},{14,6},{1,9},{3,11}... | collective-permute-start | bytes 184328 | tf_op jit(solution)/shard_map/ppermute | solution.py:294
  20.9 5.8 %collective-permute-start.9 = (f32[32,480]{1,0:T(8,128)S(1)}, f32[32,480]{1,0:T(8,128)S(1)}, u32[]{:S(2)}, u32[]{:S(2)}) collective-permute-start(f32[32,480]{1,0:T(8,128)S(1)} %get-tuple-element.21.q_ref.refs_0_), channel_id=1, source_target_pairs={{0,4},{2,6},{4,0},{6,2},{8,12},{10,14},{12,8},{14,10},{1,5},{3,7},... | collective-permute-start | bytes 184328 | tf_op jit(solution)/shard_map/ppermute | solution.py:294
  22.8 8.8 %collective-permute-start.12 = (f32[32,480]{1,0:T(8,128)S(1)}, f32[32,480]{1,0:T(8,128)S(1)}, u32[]{:S(2)}, u32[]{:S(2)}) collective-permute-start(f32[32,480]{1,0:T(8,128)S(1)} %get-tuple-element.21.q_ref.refs_0_), channel_id=1, source_target_pairs={{0,2},{2,0},{4,6},{6,4},{8,10},{10,8},{12,14},{14,12},{1,3},{3,1},... | collective-permute-start | bytes 184328 | tf_op jit(solution)/shard_map/ppermute | solution.py:294
  23.8 6.1 %collective-permute-start.7 = (f32[32,480]{1,0:T(8,128)S(1)}, f32[32,480]{1,0:T(8,128)S(1)}, u32[]{:S(2)}, u32[]{:S(2)}) collective-permute-start(f32[32,480]{1,0:T(8,128)S(1)} %get-tuple-element.21.q_ref.refs_0_), channel_id=1, source_target_pairs={{0,12},{2,14},{4,8},{6,10},{8,4},{10,6},{12,0},{14,2},{1,13},{3,15... | collective-permute-start | bytes 184328 | tf_op jit(solution)/shard_map/ppermute | solution.py:294
  26.7 7.0 %collective-permute-start.11 = (f32[2,32,480]{2,1,0:T(8,128)S(1)}, f32[2,32,480]{2,1,0:T(8,128)S(1)}, u32[]{:S(2)}, u32[]{:S(2)}) collective-permute-start(f32[2,32,480]{2,1,0:T(8,128)S(1)} %pad_maximum_fusion), channel_id=1, source_target_pairs={{0,2},{2,0},{4,6},{6,4},{8,10},{10,8},{12,14},{14,12},{1,3},{3,1},... | collective-permute-start | bytes 368648 | tf_op jit(solution)/shard_map/ppermute | solution.py:294
  29.9 5.3 %collective-permute-start.8 = (f32[32,480]{1,0:T(8,128)S(1)}, f32[32,480]{1,0:T(8,128)S(1)}, u32[]{:S(2)}, u32[]{:S(2)}) collective-permute-start(f32[32,480]{1,0:T(8,128)S(1)} %collective-permute-done.7.refs_0_), channel_id=1, source_target_pairs={{0,2},{2,0},{4,6},{6,4},{8,10},{10,8},{12,14},{14,12},{1,3},{3,1},... | collective-permute-start | bytes 184328 | tf_op jit(solution)/shard_map/ppermute | solution.py:294
  35.8 3.5 %collective-permute-start.13 = (f32[544,128]{1,0:T(8,128)S(1)}, f32[544,128]{1,0:T(8,128)S(1)}, u32[]{:S(2)}, u32[]{:S(2)}) collective-permute-start(f32[544,128]{1,0:T(8,128)S(1)} %shard_map.96.mine_ref), channel_id=1, source_target_pairs={{0,1},{1,0},{2,3},{3,2},{4,5},{5,4},{6,7},{7,6},{8,9},{9,8},{10,11... | collective-permute-start | bytes 835592 | tf_op jit(solution)/shard_map/ppermute | solution.py:297
  37.2 1.4 %collective-permute-start.6 = (f32[32,256]{1,0:T(8,128)S(1)}, f32[32,256]{1,0:T(8,128)S(1)}, u32[]{:S(2)}, u32[]{:S(2)}) collective-permute-start(f32[32,256]{1,0:T(8,128)S(1)} %shard_map.87.sums_ref), channel_id=1, source_target_pairs={{0,1},{1,0},{2,3},{3,2},{4,5},{5,4},{6,7},{7,6},{8,9},{9,8},{10,11... | collective-permute-start | bytes 98312 | tf_op jit(solution)/shard_map/ppermute | solution.py:297

commit v7 on v6

--- a/solution.py
+++ b/solution.py
@@ -12,6 +12,7 @@
 F32 = jnp.float32
 BF16 = jnp.bfloat16
 LANES = 128
+VMEM_LIMIT = 60 * 1024 * 1024
 NN = ((1,), (0,))
 NT = ((1,), (1,))
 TN = ((0,), (0,))
@@ -160,13 +161,11 @@
 def score_kernel(shares, fresh, own_ref, *refs):
     q_refs, refs = refs[: len(shares)], refs[len(shares) :]
     geno_ref, traits_ref, freqs_ref = refs[:3]
-    total_ref = None if fresh else refs[3]
-    out_ref = refs[-1]
+    out_ref = refs[-2]
     freq_high, freq_low = split(freqs_ref[...])
     f_three = jnp.concatenate([freq_high, freq_high, freq_low], axis=0)
     anc, width = freqs_ref.shape
     traits = traits_ref.shape[1]
-    score, info = None, None
     for m, q_ref in zip(shares, q_refs):
         q_new = q_ref[...]
         rows = q_new.shape[1]
@@ -190,13 +189,12 @@
             NN,
         )
         part2 = wide2[:anc, :width] + wide2[:anc, width:] + wide2[anc:, :width]
-        score = part if score is None else score + part
-        info = part2 if info is None else info + part2
-    if not fresh:
-        score = score + total_ref[: anc * traits]
-        info = info + total_ref[anc * traits :]
-    out_ref[: anc * traits] = score
-    out_ref[anc * traits :] = info
+        if fresh and m == shares[0]:
+            out_ref[: anc * traits] = part
+            out_ref[anc * traits :] = part2
+        else:
+            out_ref[: anc * traits] += part
+            out_ref[anc * traits :] += part2
 
 
 def emit_kernel(
@@ -257,7 +255,7 @@
     specs = [SCALARS]
     held = [args[0]]
     for at, x in enumerate(args[1:], 1):
-        specs.append(pl.BlockSpec(memory_space=pl.ANY) if at in raw else IN_VMEM)
+        specs.append(pl.BlockSpec(memory_space=pltpu.HBM) if at in raw else IN_VMEM)
         held.append(x if at in raw else pltpu.with_memory_space_constraint(x, VMEM))
     out_specs, out_shape = [], []
     for out in outs:
@@ -275,6 +273,7 @@
         scratch_shapes=list(scratch),
         input_output_aliases=aliases or {},
         cost_estimate=pl.CostEstimate(flops=cost * 400_000, bytes_accessed=0, transcendentals=0),
+        compiler_params=pltpu.CompilerParams(vmem_limit_bytes=VMEM_LIMIT),
     )(*held)
 
 
@@ -297,8 +296,7 @@
         return lax.ppermute(x, "smp", [(0, 1), (1, 0)])
 
     half_rows = rows // 2
-    tiles = half_rows // LANES
-    pieces = next(p for p in (5, 4, 3, 2, 1) if tiles % p == 0)
+    pieces = 1
     excess = VMEM((half_rows, 2 * width), BF16)
 
     far, geno, counts = call(
@@ -344,23 +342,26 @@
     )
 
     shares = {0: q_new}
-    for m in (*range(half, var_count, 2), *range(2, half, 2), 1):
+    for m in (*range(half, var_count, 2), *range(1, half)):
         shares[m] = move(q_new, m)
-    early = range(2, var_count - 2, 2)
-    passed = move(jnp.stack([shares[m] for m in early]), 1)
-    for at, m in enumerate(early):
-        shares[m + 1] = passed[at]
-    shares[var_count - 1] = move(shares[var_count - 2], 1)
-
+    for m in range(half + 1, var_count, 2):
+        shares[m] = move(shares[m - 1], 1)
+
+    groups = (
+        (0,),
+        (*reversed(range(1, half - 1)), *range(half, var_count, 2)),
+        (half - 1, *range(half + 1, var_count - 1, 2)),
+        (var_count - 1,),
+    )
     total = None
-    for m in (0, 2, 1, 4, 6, 3, 5, 7) if var_count == 8 else range(var_count):
+    for ms in groups:
         inputs = (geno, trait_parts, freqs) + (() if total is None else (total,))
-        (total,) = call(
-            functools.partial(score_kernel, (m,), total is None),
-            (place, shares[m], *inputs),
-            [((anc * traits + anc), width)],
-            cost=700,
-            aliases=None if total is None else {5: 0},
+        total, trait_parts = call(
+            functools.partial(score_kernel, ms, total is None),
+            (place, *[shares[m] for m in ms], *inputs),
+            [((anc * traits + anc), width), trait_parts.shape],
+            cost=700 * len(ms),
+            aliases={len(ms) + 2: 1} | ({} if total is None else {len(ms) + 4: 0}),
         )
     total_other = swap(total)
     out = jax.ShapeDtypeStruct

time: 40.3 us -> 37.7 us (0.935)
  Pallas kernels: 13.4 us -> 12.1 us
  waiting for transfers between devices: 6.65 us -> 5.87 us
  starting transfers between devices: 19 us -> 18.3 us
    pallas_call x15 -> x11, Pallas kernels: 13.4 us -> 12.1 us  [call(): pl.pallas_call(kernel, in_specs=specs, out_specs=out_specs, out_shape=out...]
    ppermute x12 -> x13, waiting for transfers between devices: 5.79 us -> 4.91 us  [move(): return lax.ppermute(x, 'var', [(i, i ^ m) for i in range(var_count)])]
    ppermute x12 -> x13, starting transfers between devices: 18.5 us -> 18 us  [move(): return lax.ppermute(x, 'var', [(i, i ^ m) for i in range(var_count)])]
  transfers between devices with their start and end apart: 14 -> 15, of which waited for: 5 -> 5; matrix products, arithmetic and copies ran while one was open for 0% -> 0% of each run, Pallas kernels for 23% -> 22%
where the time goes in v7:
time: 37.7 us; the launch traced here: 37.4 us
  starting transfers between devices  18.3 us (49%)
  Pallas kernels  12.1 us (32%)
  waiting for transfers between devices  5.87 us (16%)
  between operations  0.81 us (2%)
    ppermute x13, starting transfers between devices, move(): return lax.ppermute(x, 'var', [(i, i ^ m) for i in range(var_count)])  18 us
    pallas_call x11, Pallas kernels, call(): pl.pallas_call(kernel, in_specs=specs, out_specs=out_specs, out_shape=out...  12.1 us
    ppermute x13, waiting for transfers between devices, move(): return lax.ppermute(x, 'var', [(i, i ^ m) for i in range(var_count)])  4.91 us
    ppermute x2, waiting for transfers between devices, swap(): return lax.ppermute(x, 'smp', [(0, 1), (1, 0)])  0.97 us
  transfers between devices with their start and end apart: 15, of which 5 were waited for; matrix products, arithmetic and copies ran while one was open for 0% of the time, Pallas kernels for 22%

profile of v7, /device:TPU:0, one launch (start us, length us, event | category | flops | bytes accessed | tf_op | source)
XLA Modules:
  0.0 37.4 jit_solution(1780264636529086953)
XLA Ops:
  0.6 2.4 %shard_map.83 = (f32[4,32,480]{2,1,0:T(8,128)S(1)}, bf16[3840,128]{1,0:T(8,128)(2,1)S(1)}, s32[32,3840]{1,0:T(8,128)S(1)}) custom-call(s32[1]{0:T(128)} %bitcast.place_ref.own_ref, bf16[3840,128]{1,0:T(8,128)(2,1)} %geno_hbm.1, s32[32,3840]{1,0:T(8,128)} %bitcast.31, f32[32,128]{1,0:T(8,128)} %refs_3_.3), custom_call_target="tpu_custom_call" | custom-call | flops 800000000 | tf_op jit(solution)/shard_map/pallas_call | solution.py:268
  3.0 0.0 copy-start
  3.0 0.0 copy-start.2
  3.1 3.0 %collective-permute-start.3 = (f32[2,32,480]{2,1,0:T(8,128)S(1)}, f32[2,32,480]{2,1,0:T(8,128)S(1)}, u32[]{:S(2)}, u32[]{:S(2)}) collective-permute-start(f32[2,32,480]{2,1,0:T(8,128)S(1)} %slice_bitcast_fusion), channel_id=1, source_target_pairs={{0,2},{2,0},{4,6},{6,4},{8,10},{10,8},{12,14},{14,12},{1,3},{3,1},... | collective-permute-start | bytes 368648 | tf_op jit(solution)/shard_map/ppermute | solution.py:293
  6.1 0.0 copy-done.2
  6.1 0.9 %shard_map.85 = f32[4,32,480]{2,1,0:T(8,128)S(1)} custom-call(s32[1]{0:T(128)} %bitcast.place_ref.own_ref, bf16[3840,128]{1,0:T(8,128)(2,1)S(1)} %get-tuple-element.24.geno_ref.refs_1_.refs_4_.refs_2_, s32[32,3840]{1,0:T(8,128)S(1)} %get-tuple-element.25.counts_ref, f32[32,128]{1,0:T(8,128)S(1)} %copy-done.2), custom_call_target="tpu_custom_call" | custom-call | flops 800000000 | tf_op jit(solution)/shard_map/pallas_call | solution.py:268
  7.1 1.7 %collective-permute-start.2 = (f32[32,480]{1,0:T(8,128)S(1)}, f32[32,480]{1,0:T(8,128)S(1)}, u32[]{:S(2)}, u32[]{:S(2)}) collective-permute-start(f32[32,480]{1,0:T(8,128)S(1)} %get-tuple-element.43), channel_id=1, source_target_pairs={{0,6},{2,4},{4,2},{6,0},{8,14},{10,12},{12,10},{14,8},{1,7},{3,5},... | collective-permute-start | bytes 184328 | tf_op jit(solution)/shard_map/ppermute | solution.py:293
  8.8 0.4 %collective-permute-start.1 = (f32[32,480]{1,0:T(8,128)S(1)}, f32[32,480]{1,0:T(8,128)S(1)}, u32[]{:S(2)}, u32[]{:S(2)}) collective-permute-start(f32[32,480]{1,0:T(8,128)S(1)} %get-tuple-element.44), channel_id=1, source_target_pairs={{0,4},{2,6},{4,0},{6,2},{8,12},{10,14},{12,8},{14,10},{1,5},{3,7},... | collective-permute-start | bytes 184328 | tf_op jit(solution)/shard_map/ppermute | solution.py:293
  9.3 0.0 copy-start.3
  9.3 1.4 %collective-permute-start = (f32[32,480]{1,0:T(8,128)S(1)}, f32[32,480]{1,0:T(8,128)S(1)}, u32[]{:S(2)}, u32[]{:S(2)}) collective-permute-start(f32[32,480]{1,0:T(8,128)S(1)} %get-tuple-element.45), channel_id=1, source_target_pairs={{0,2},{2,0},{4,6},{6,4},{8,10},{10,8},{12,14},{14,12},{1,3},{3,1},... | collective-permute-start | bytes 184328 | tf_op jit(solution)/shard_map/ppermute | solution.py:293
  10.7 0.0 collective-permute-done.3
  10.7 3.7 %collective-permute-start.5 = (f32[32,480]{1,0:T(8,128)S(1)}, f32[32,480]{1,0:T(8,128)S(1)}, u32[]{:S(2)}, u32[]{:S(2)}) collective-permute-start(f32[32,480]{1,0:T(8,128)S(1)} %get-tuple-element.47), channel_id=1, source_target_pairs={{0,12},{2,14},{4,8},{6,10},{8,4},{10,6},{12,0},{14,2},{1,13},{3,15... | collective-permute-start | bytes 184328 | tf_op jit(solution)/shard_map/ppermute | solution.py:293
  14.4 0.0 collective-permute-start.4
  14.4 0.0 copy-done
  14.4 0.0 copy-done.3
  14.4 1.3 %shard_map.84 = (f32[32,256]{1,0:T(8,128)S(1)}, f32[8,16,480]{2,1,0:T(8,128)S(1)}, f32[8,32,480]{2,1,0:T(8,128)S(1)}) custom-call(s32[1]{0:T(128)} %bitcast.place_ref.own_ref, bf16[3840,128]{1,0:T(8,128)(2,1)S(1)} %get-tuple-element.24.geno_ref.refs_1_.refs_4_.refs_2_, s32[32,3840]{1,0:T(8,128)S(1)} %get-tuple-element.25.counts_ref, ...), custom_call_target="tpu_custom_call" | custom-call | flops 480000000 | tf_op jit(solution)/shard_map/pallas_call | solution.py:268
  15.7 0.0 collective-permute-done.2.refs_3_
  15.7 0.0 collective-permute-done.1.refs_2_
  15.7 0.0 collective-permute-done.refs_1_
  15.7 1.4 %collective-permute-done.5.refs_5_ = f32[32,480]{1,0:T(8,128)S(1)} collective-permute-done((f32[32,480]{1,0:T(8,128)S(1)}, f32[32,480]{1,0:T(8,128)S(1)}, u32[]{:S(2)}, u32[]{:S(2)}) %collective-permute-start.5) | collective-permute-done | bytes 61472 | tf_op jit(solution)/shard_map/ppermute | solution.py:293
  17.1 2.5 %collective-permute-done.4.refs_4_ = f32[32,480]{1,0:T(8,128)S(1)} collective-permute-done((f32[32,480]{1,0:T(8,128)S(1)}, f32[32,480]{1,0:T(8,128)S(1)}, u32[]{:S(2)}, u32[]{:S(2)}) %collective-permute-start.4) | collective-permute-done | bytes 61472 | tf_op jit(solution)/shard_map/ppermute | solution.py:293
  19.6 0.1 shard_map.86
  19.7 0.8 %collective-permute-start.10 = (f32[32,480]{1,0:T(8,128)S(1)}, f32[32,480]{1,0:T(8,128)S(1)}, u32[]{:S(2)}, u32[]{:S(2)}) collective-permute-start(f32[32,480]{1,0:T(8,128)S(1)} %get-tuple-element.28.q_ref.refs_0_), channel_id=1, source_target_pairs={{0,8},{2,10},{4,12},{6,14},{8,0},{10,2},{12,4},{14,6},{1,9},{3,11}... | collective-permute-start | bytes 184328 | tf_op jit(solution)/shard_map/ppermute | solution.py:293
  20.5 1.4 %collective-permute-start.7 = (f32[32,480]{1,0:T(8,128)S(1)}, f32[32,480]{1,0:T(8,128)S(1)}, u32[]{:S(2)}, u32[]{:S(2)}) collective-permute-start(f32[32,480]{1,0:T(8,128)S(1)} %get-tuple-element.28.q_ref.refs_0_), channel_id=1, source_target_pairs={{0,12},{2,14},{4,8},{6,10},{8,4},{10,6},{12,0},{14,2},{1,13},{3,15... | collective-permute-start | bytes 184328 | tf_op jit(solution)/shard_map/ppermute | solution.py:293
  21.9 1.2 %collective-permute-start.13 = (f32[32,480]{1,0:T(8,128)S(1)}, f32[32,480]{1,0:T(8,128)S(1)}, u32[]{:S(2)}, u32[]{:S(2)}) collective-permute-start(f32[32,480]{1,0:T(8,128)S(1)} %get-tuple-element.28.q_ref.refs_0_), channel_id=1, source_target_pairs={{0,2},{2,0},{4,6},{6,4},{8,10},{10,8},{12,14},{14,12},{1,3},{3,1},... | collective-permute-start | bytes 184328 | tf_op jit(solution)/shard_map/ppermute | solution.py:293
  23.1 1.5 %collective-permute-start.12 = (f32[32,480]{1,0:T(8,128)S(1)}, f32[32,480]{1,0:T(8,128)S(1)}, u32[]{:S(2)}, u32[]{:S(2)}) collective-permute-start(f32[32,480]{1,0:T(8,128)S(1)} %get-tuple-element.28.q_ref.refs_0_), channel_id=1, source_target_pairs={{0,4},{2,6},{4,0},{6,2},{8,12},{10,14},{12,8},{14,10},{1,5},{3,7},... | collective-permute-start | bytes 184328 | tf_op jit(solution)/shard_map/ppermute | solution.py:293
  24.6 0.8 %collective-permute-start.9 = (f32[32,480]{1,0:T(8,128)S(1)}, f32[32,480]{1,0:T(8,128)S(1)}, u32[]{:S(2)}, u32[]{:S(2)}) collective-permute-start(f32[32,480]{1,0:T(8,128)S(1)} %get-tuple-element.28.q_ref.refs_0_), channel_id=1, source_target_pairs={{0,6},{2,4},{4,2},{6,0},{8,14},{10,12},{12,10},{14,8},{1,7},{3,5},... | collective-permute-start | bytes 184328 | tf_op jit(solution)/shard_map/ppermute | solution.py:293
  25.4 0.7 %shard_map.89 = (f32[544,128]{1,0:T(8,128)S(1)}, f32[8,16,480]{2,1,0:T(8,128)S(1)}) custom-call(s32[1]{0:T(128)} %bitcast.place_ref.own_ref, f32[32,480]{1,0:T(8,128)S(1)} %get-tuple-element.28.q_ref.refs_0_, bf16[3840,128]{1,0:T(8,128)(2,1)S(1)} %get-tuple-element.24.geno_ref.refs_1_.refs_4_.refs_2_, ...), custom_call_target="tpu_custom_call", output_to_operand_aliasing={{1}: (3, {})} | custom-call | flops 280000000 | tf_op jit(solution)/shard_map/pallas_call | solution.py:268
  26.1 0.9 %collective-permute-done.10.refs_2_ = f32[32,480]{1,0:T(8,128)S(1)} collective-permute-done((f32[32,480]{1,0:T(8,128)S(1)}, f32[32,480]{1,0:T(8,128)S(1)}, u32[]{:S(2)}, u32[]{:S(2)}) %collective-permute-start.10) | collective-permute-done | bytes 61472 | tf_op jit(solution)/shard_map/ppermute | solution.py:293
  27.0 0.4 collective-permute-start.11
  27.3 0.0 collective-permute-done.7.refs_3_
  27.3 1.7 %collective-permute-start.8 = (f32[32,480]{1,0:T(8,128)S(1)}, f32[32,480]{1,0:T(8,128)S(1)}, u32[]{:S(2)}, u32[]{:S(2)}) collective-permute-start(f32[32,480]{1,0:T(8,128)S(1)} %collective-permute-done.7.refs_3_), channel_id=1, source_target_pairs={{0,2},{2,0},{4,6},{6,4},{8,10},{10,8},{12,14},{14,12},{1,3},{3,1},... | collective-permute-start | bytes 184328 | tf_op jit(solution)/shard_map/ppermute | solution.py:293
  29.0 0.0 collective-permute-done.13.refs_1_
  29.0 0.0 collective-permute-done.12.refs_0_
  29.0 2.1 %shard_map.90 = (f32[544,128]{1,0:T(8,128)S(1)}, f32[8,16,480]{2,1,0:T(8,128)S(1)}) custom-call(s32[1]{0:T(128)} %bitcast.place_ref.own_ref, f32[32,480]{1,0:T(8,128)S(1)} %collective-permute-done.12.refs_0_, f32[32,480]{1,0:T(8,128)S(1)} %collective-permute-done.13.refs_1_, ...), custom_call_target="tpu_custom_call", output_to_operand_aliasing={{1}: (6, {}), {0}: (8, {})} | custom-call | flops 1120000000 | tf_op jit(solution)/shard_map/pallas_call | solution.py:268
  31.1 0.0 collective-permute-done.9.refs_0_
  31.1 0.1 collective-permute-done.11.refs_1_
  31.2 1.1 %shard_map.91 = (f32[544,128]{1,0:T(8,128)S(1)}, f32[8,16,480]{2,1,0:T(8,128)S(1)}) custom-call(s32[1]{0:T(128)} %bitcast.place_ref.own_ref, f32[32,480]{1,0:T(8,128)S(1)} %collective-permute-done.9.refs_0_, f32[32,480]{1,0:T(8,128)S(1)} %collective-permute-done.11.refs_1_, ...), custom_call_target="tpu_custom_call", output_to_operand_aliasing={{1}: (4, {}), {0}: (6, {})} | custom-call | flops 560000000 | tf_op jit(solution)/shard_map/pallas_call | solution.py:268
  32.4 0.0 collective-permute-done.8.refs_0_
  32.4 0.0 copy-start.1
  32.4 0.7 %shard_map.92 = (f32[544,128]{1,0:T(8,128)S(1)}, f32[8,16,480]{2,1,0:T(8,128)S(1)}) custom-call(s32[1]{0:T(128)} %bitcast.place_ref.own_ref, f32[32,480]{1,0:T(8,128)S(1)} %collective-permute-done.8.refs_0_, bf16[3840,128]{1,0:T(8,128)(2,1)S(1)} %get-tuple-element.24.geno_ref.refs_1_.refs_4_.refs_2_, ...), custom_call_target="tpu_custom_call", output_to_operand_aliasing={{1}: (3, {}), {0}: (5, {})} | custom-call | flops 280000000 | tf_op jit(solution)/shard_map/pallas_call | solution.py:268
  33.1 0.1 collective-permute-start.14
  33.2 0.3 copy-done.1
  33.4 1.3 %shard_map.87.sums_ref = f32[32,256]{1,0:T(8,128)S(1)} custom-call(s32[1]{0:T(128)} %bitcast.place_ref.own_ref, bf16[3840,128]{1,0:T(8,128)(2,1)S(1)} %get-tuple-element.24.geno_ref.refs_1_.refs_4_.refs_2_, s32[32,3840]{1,0:T(8,128)S(1)} %copy-done.1, f32[32,128]{1,0:T(8,128)S(1)} %copy-done.2, f32[32,256]{1,0:T(8,128)S(1)} %get-tuple-element.30.refs_0_), custom_call_target="tpu_custom_call" | custom-call | flops 400000000 | tf_op jit(solution)/shard_map/pallas_call | solution.py:268
  34.8 0.3 collective-permute-start.6
  35.0 1.0 %collective-permute-done.6.other_ref = f32[32,256]{1,0:T(8,128)S(1)} collective-permute-done((f32[32,256]{1,0:T(8,128)S(1)}, f32[32,256]{1,0:T(8,128)S(1)}, u32[]{:S(2)}, u32[]{:S(2)}) %collective-permute-start.6) | collective-permute-done | bytes 32800 | tf_op jit(solution)/shard_map/ppermute | solution.py:296
  36.0 0.7 %shard_map.88 = (f32[32,480]{1,0:T(8,128)}, f32[32,480]{1,0:T(8,128)}, f32[32,128]{1,0:T(8,128)}, f32[32,128]{1,0:T(8,128)}) custom-call(s32[1]{0:T(128)} %bitcast.place_ref.own_ref, f32[32,480]{1,0:T(8,128)S(1)} %get-tuple-element.28.q_ref.refs_0_, f32[32,480]{1,0:T(8,128)S(1)} %get-tuple-element.29.grad_ref, f32[32,256]{1,0:T(8,128)S(1)} %shard_map.87.sums_ref, ...), custom_call_target="tpu_custom_call" | custom-call | flops 240000000 | tf_op jit(solution)/shard_map/pallas_call | solution.py:268
  36.7 0.0 collective-permute-done.14.other_ref
  36.7 0.8 %shard_map.93 = f32[32,16,128]{2,1,0:T(8,128)} custom-call(s32[1]{0:T(128)} %bitcast.place_ref.own_ref, f32[544,128]{1,0:T(8,128)S(1)} %get-tuple-element.42.mine_ref, f32[544,128]{1,0:T(8,128)S(1)} %collective-permute-done.14.other_ref), custom_call_target="tpu_custom_call" | custom-call | flops 120000000 | tf_op jit(solution)/shard_map/pallas_call | solution.py:268
  (4 shorter events, 0.1 us)
Async XLA Ops:
  3.0 11.3 %copy-start = (s32[32,3840]{1,0:T(8,128)}, s32[32,3840]{1,0:T(8,128)S(1)}, u32[]{:S(2)}) copy-start(s32[32,3840]{1,0:T(8,128)S(1)} %get-tuple-element.25.counts_ref) | copy-start | bytes 1474564
  3.0 3.1 %copy-start.2 = (f32[32,128]{1,0:T(8,128)S(1)}, f32[32,128]{1,0:T(8,128)}, u32[]{:S(2)}) copy-start(f32[32,128]{1,0:T(8,128)} %refs_3_.3) | copy-start | bytes 49156
  3.1 7.6 %collective-permute-start.3 = (f32[2,32,480]{2,1,0:T(8,128)S(1)}, f32[2,32,480]{2,1,0:T(8,128)S(1)}, u32[]{:S(2)}, u32[]{:S(2)}) collective-permute-start(f32[2,32,480]{2,1,0:T(8,128)S(1)} %slice_bitcast_fusion), channel_id=1, source_target_pairs={{0,2},{2,0},{4,6},{6,4},{8,10},{10,8},{12,14},{14,12},{1,3},{3,1},... | collective-permute-start | bytes 368648 | tf_op jit(solution)/shard_map/ppermute | solution.py:293
  7.1 8.6 %collective-permute-start.2 = (f32[32,480]{1,0:T(8,128)S(1)}, f32[32,480]{1,0:T(8,128)S(1)}, u32[]{:S(2)}, u32[]{:S(2)}) collective-permute-start(f32[32,480]{1,0:T(8,128)S(1)} %get-tuple-element.43), channel_id=1, source_target_pairs={{0,6},{2,4},{4,2},{6,0},{8,14},{10,12},{12,10},{14,8},{1,7},{3,5},... | collective-permute-start | bytes 184328 | tf_op jit(solution)/shard_map/ppermute | solution.py:293
  8.8 6.9 %collective-permute-start.1 = (f32[32,480]{1,0:T(8,128)S(1)}, f32[32,480]{1,0:T(8,128)S(1)}, u32[]{:S(2)}, u32[]{:S(2)}) collective-permute-start(f32[32,480]{1,0:T(8,128)S(1)} %get-tuple-element.44), channel_id=1, source_target_pairs={{0,4},{2,6},{4,0},{6,2},{8,12},{10,14},{12,8},{14,10},{1,5},{3,7},... | collective-permute-start | bytes 184328 | tf_op jit(solution)/shard_map/ppermute | solution.py:293
  9.3 5.1 %copy-start.3 = (s32[3840,16]{0,1:T(8,128)S(1)}, s32[3840,16]{0,1:T(8,128)}, u32[]{:S(2)}) copy-start(s32[3840,16]{0,1:T(8,128)} %param.6) | copy-start | bytes 737284
  9.3 6.5 %collective-permute-start = (f32[32,480]{1,0:T(8,128)S(1)}, f32[32,480]{1,0:T(8,128)S(1)}, u32[]{:S(2)}, u32[]{:S(2)}) collective-permute-start(f32[32,480]{1,0:T(8,128)S(1)} %get-tuple-element.45), channel_id=1, source_target_pairs={{0,2},{2,0},{4,6},{6,4},{8,10},{10,8},{12,14},{14,12},{1,3},{3,1},... | collective-permute-start | bytes 184328 | tf_op jit(solution)/shard_map/ppermute | solution.py:293
  10.7 6.4 %collective-permute-start.5 = (f32[32,480]{1,0:T(8,128)S(1)}, f32[32,480]{1,0:T(8,128)S(1)}, u32[]{:S(2)}, u32[]{:S(2)}) collective-permute-start(f32[32,480]{1,0:T(8,128)S(1)} %get-tuple-element.47), channel_id=1, source_target_pairs={{0,12},{2,14},{4,8},{6,10},{8,4},{10,6},{12,0},{14,2},{1,13},{3,15... | collective-permute-start | bytes 184328 | tf_op jit(solution)/shard_map/ppermute | solution.py:293
  14.4 5.3 %collective-permute-start.4 = (f32[32,480]{1,0:T(8,128)S(1)}, f32[32,480]{1,0:T(8,128)S(1)}, u32[]{:S(2)}, u32[]{:S(2)}) collective-permute-start(f32[32,480]{1,0:T(8,128)S(1)} %get-tuple-element.48), channel_id=1, source_target_pairs={{0,8},{2,10},{4,12},{6,14},{8,0},{10,2},{12,4},{14,6},{1,9},{3,11}... | collective-permute-start | bytes 184328 | tf_op jit(solution)/shard_map/ppermute | solution.py:293
  19.7 7.3 %collective-permute-start.10 = (f32[32,480]{1,0:T(8,128)S(1)}, f32[32,480]{1,0:T(8,128)S(1)}, u32[]{:S(2)}, u32[]{:S(2)}) collective-permute-start(f32[32,480]{1,0:T(8,128)S(1)} %get-tuple-element.28.q_ref.refs_0_), channel_id=1, source_target_pairs={{0,8},{2,10},{4,12},{6,14},{8,0},{10,2},{12,4},{14,6},{1,9},{3,11}... | collective-permute-start | bytes 184328 | tf_op jit(solution)/shard_map/ppermute | solution.py:293
  20.5 6.9 %collective-permute-start.7 = (f32[32,480]{1,0:T(8,128)S(1)}, f32[32,480]{1,0:T(8,128)S(1)}, u32[]{:S(2)}, u32[]{:S(2)}) collective-permute-start(f32[32,480]{1,0:T(8,128)S(1)} %get-tuple-element.28.q_ref.refs_0_), channel_id=1, source_target_pairs={{0,12},{2,14},{4,8},{6,10},{8,4},{10,6},{12,0},{14,2},{1,13},{3,15... | collective-permute-start | bytes 184328 | tf_op jit(solution)/shard_map/ppermute | solution.py:293
  21.9 7.1 %collective-permute-start.13 = (f32[32,480]{1,0:T(8,128)S(1)}, f32[32,480]{1,0:T(8,128)S(1)}, u32[]{:S(2)}, u32[]{:S(2)}) collective-permute-start(f32[32,480]{1,0:T(8,128)S(1)} %get-tuple-element.28.q_ref.refs_0_), channel_id=1, source_target_pairs={{0,2},{2,0},{4,6},{6,4},{8,10},{10,8},{12,14},{14,12},{1,3},{3,1},... | collective-permute-start | bytes 184328 | tf_op jit(solution)/shard_map/ppermute | solution.py:293
  23.1 5.9 %collective-permute-start.12 = (f32[32,480]{1,0:T(8,128)S(1)}, f32[32,480]{1,0:T(8,128)S(1)}, u32[]{:S(2)}, u32[]{:S(2)}) collective-permute-start(f32[32,480]{1,0:T(8,128)S(1)} %get-tuple-element.28.q_ref.refs_0_), channel_id=1, source_target_pairs={{0,4},{2,6},{4,0},{6,2},{8,12},{10,14},{12,8},{14,10},{1,5},{3,7},... | collective-permute-start | bytes 184328 | tf_op jit(solution)/shard_map/ppermute | solution.py:293
  24.6 6.5 %collective-permute-start.9 = (f32[32,480]{1,0:T(8,128)S(1)}, f32[32,480]{1,0:T(8,128)S(1)}, u32[]{:S(2)}, u32[]{:S(2)}) collective-permute-start(f32[32,480]{1,0:T(8,128)S(1)} %get-tuple-element.28.q_ref.refs_0_), channel_id=1, source_target_pairs={{0,6},{2,4},{4,2},{6,0},{8,14},{10,12},{12,10},{14,8},{1,7},{3,5},... | collective-permute-start | bytes 184328 | tf_op jit(solution)/shard_map/ppermute | solution.py:293
  27.0 4.3 %collective-permute-start.11 = (f32[32,480]{1,0:T(8,128)S(1)}, f32[32,480]{1,0:T(8,128)S(1)}, u32[]{:S(2)}, u32[]{:S(2)}) collective-permute-start(f32[32,480]{1,0:T(8,128)S(1)} %collective-permute-done.10.refs_2_), channel_id=1, source_target_pairs={{0,2},{2,0},{4,6},{6,4},{8,10},{10,8},{12,14},{14,12},{1,3},{3,1},... | collective-permute-start | bytes 184328 | tf_op jit(solution)/shard_map/ppermute | solution.py:293
  27.3 5.1 %collective-permute-start.8 = (f32[32,480]{1,0:T(8,128)S(1)}, f32[32,480]{1,0:T(8,128)S(1)}, u32[]{:S(2)}, u32[]{:S(2)}) collective-permute-start(f32[32,480]{1,0:T(8,128)S(1)} %collective-permute-done.7.refs_3_), channel_id=1, source_target_pairs={{0,2},{2,0},{4,6},{6,4},{8,10},{10,8},{12,14},{14,12},{1,3},{3,1},... | collective-permute-start | bytes 184328 | tf_op jit(solution)/shard_map/ppermute | solution.py:293
  32.4 1.0 %copy-start.1 = (s32[32,3840]{1,0:T(8,128)S(1)}, s32[32,3840]{1,0:T(8,128)}, u32[]{:S(2)}) copy-start(s32[32,3840]{1,0:T(8,128)} %copy-done) | copy-start | bytes 1474564
  33.1 3.6 %collective-permute-start.14 = (f32[544,128]{1,0:T(8,128)S(1)}, f32[544,128]{1,0:T(8,128)S(1)}, u32[]{:S(2)}, u32[]{:S(2)}) collective-permute-start(f32[544,128]{1,0:T(8,128)S(1)} %get-tuple-element.42.mine_ref), channel_id=1, source_target_pairs={{0,1},{1,0},{2,3},{3,2},{4,5},{5,4},{6,7},{7,6},{8,9},{9,8},{10,11... | collective-permute-start | bytes 835592 | tf_op jit(solution)/shard_map/ppermute | solution.py:296
  34.8 1.2 %collective-permute-start.6 = (f32[32,256]{1,0:T(8,128)S(1)}, f32[32,256]{1,0:T(8,128)S(1)}, u32[]{:S(2)}, u32[]{:S(2)}) collective-permute-start(f32[32,256]{1,0:T(8,128)S(1)} %shard_map.87.sums_ref), channel_id=1, source_target_pairs={{0,1},{1,0},{2,3},{3,2},{4,5},{5,4},{6,7},{7,6},{8,9},{9,8},{10,11... | collective-permute-start | bytes 98312 | tf_op jit(solution)/shard_map/ppermute | solution.py:296

commit v8 on v7

--- a/solution.py
+++ b/solution.py
@@ -28,20 +28,17 @@
 
 
 def count_table(freqs):
-    high, low = split(freqs)
+    high, middle = split(freqs)
+    low = (freqs - high.astype(F32) - middle.astype(F32)).astype(BF16)
     ones = jnp.ones_like(high)
-    return jnp.concatenate(
-        [
-            jnp.concatenate([high, ones], axis=1),
-            jnp.concatenate([low, jnp.zeros_like(ones)], axis=1),
-        ],
-        axis=0,
-    )
+    zeros = jnp.zeros_like(high)
+    left = jnp.concatenate([high, middle, low], axis=0)
+    return jnp.concatenate([left, jnp.concatenate([ones, zeros, zeros], axis=0)], axis=1)
 
 
 def ratio_parts(counts, dosage, table):
     width = dosage.shape[1]
-    both = dot(jnp.concatenate([counts, counts], axis=0), table, TN)
+    both = dot(jnp.concatenate([counts, counts, counts], axis=0), table, TN)
     recon, total = both[:, :width], both[:, width:]
     inverse = 1.0 / (recon * (total - recon))
     part = (dosage * total - (recon + recon)) * inverse

time: 37.7 us -> 37.7 us (level)
  no operation moved by 1% of the time
where the time goes in v8:
time: 37.7 us; the launch traced here: 37.4 us
  starting transfers between devices  18.3 us (49%)
  Pallas kernels  12.1 us (32%)
  waiting for transfers between devices  5.87 us (16%)
  between operations  0.81 us (2%)
    ppermute x13, starting transfers between devices, move(): return lax.ppermute(x, 'var', [(i, i ^ m) for i in range(var_count)])  18 us
    pallas_call x11, Pallas kernels, call(): pl.pallas_call(kernel, in_specs=specs, out_specs=out_specs, out_shape=out...  12.1 us
    ppermute x13, waiting for transfers between devices, move(): return lax.ppermute(x, 'var', [(i, i ^ m) for i in range(var_count)])  4.92 us
    ppermute x2, waiting for transfers between devices, swap(): return lax.ppermute(x, 'smp', [(0, 1), (1, 0)])  0.96 us
  transfers between devices with their start and end apart: 15, of which 5 were waited for; matrix products, arithmetic and copies ran while one was open for 0% of the time, Pallas kernels for 22%

profile of v8, /device:TPU:0, one launch (start us, length us, event | category | flops | bytes accessed | tf_op | source)
XLA Modules:
  0.0 37.4 jit_solution(3279205698142891243)
XLA Ops:
  0.6 2.4 %shard_map.83 = (f32[4,32,480]{2,1,0:T(8,128)S(1)}, bf16[3840,128]{1,0:T(8,128)(2,1)S(1)}, s32[32,3840]{1,0:T(8,128)S(1)}) custom-call(s32[1]{0:T(128)} %bitcast.place_ref.own_ref, bf16[3840,128]{1,0:T(8,128)(2,1)} %geno_hbm.1, s32[32,3840]{1,0:T(8,128)} %bitcast.31, f32[32,128]{1,0:T(8,128)} %refs_3_.3), custom_call_target="tpu_custom_call" | custom-call | flops 800000000 | tf_op jit(solution)/shard_map/pallas_call | solution.py:265
  3.0 0.0 copy-start
  3.0 0.0 copy-start.2
  3.1 3.0 %collective-permute-start.3 = (f32[2,32,480]{2,1,0:T(8,128)S(1)}, f32[2,32,480]{2,1,0:T(8,128)S(1)}, u32[]{:S(2)}, u32[]{:S(2)}) collective-permute-start(f32[2,32,480]{2,1,0:T(8,128)S(1)} %slice_bitcast_fusion), channel_id=1, source_target_pairs={{0,2},{2,0},{4,6},{6,4},{8,10},{10,8},{12,14},{14,12},{1,3},{3,1},... | collective-permute-start | bytes 368648 | tf_op jit(solution)/shard_map/ppermute | solution.py:290
  6.1 0.0 copy-done.2
  6.1 1.0 %shard_map.85 = f32[4,32,480]{2,1,0:T(8,128)S(1)} custom-call(s32[1]{0:T(128)} %bitcast.place_ref.own_ref, bf16[3840,128]{1,0:T(8,128)(2,1)S(1)} %get-tuple-element.24.geno_ref.refs_1_.refs_4_.refs_2_, s32[32,3840]{1,0:T(8,128)S(1)} %get-tuple-element.25.counts_ref, f32[32,128]{1,0:T(8,128)S(1)} %copy-done.2), custom_call_target="tpu_custom_call" | custom-call | flops 800000000 | tf_op jit(solution)/shard_map/pallas_call | solution.py:265
  7.1 1.7 %collective-permute-start.2 = (f32[32,480]{1,0:T(8,128)S(1)}, f32[32,480]{1,0:T(8,128)S(1)}, u32[]{:S(2)}, u32[]{:S(2)}) collective-permute-start(f32[32,480]{1,0:T(8,128)S(1)} %get-tuple-element.43), channel_id=1, source_target_pairs={{0,6},{2,4},{4,2},{6,0},{8,14},{10,12},{12,10},{14,8},{1,7},{3,5},... | collective-permute-start | bytes 184328 | tf_op jit(solution)/shard_map/ppermute | solution.py:290
  8.8 0.4 %collective-permute-start.1 = (f32[32,480]{1,0:T(8,128)S(1)}, f32[32,480]{1,0:T(8,128)S(1)}, u32[]{:S(2)}, u32[]{:S(2)}) collective-permute-start(f32[32,480]{1,0:T(8,128)S(1)} %get-tuple-element.44), channel_id=1, source_target_pairs={{0,4},{2,6},{4,0},{6,2},{8,12},{10,14},{12,8},{14,10},{1,5},{3,7},... | collective-permute-start | bytes 184328 | tf_op jit(solution)/shard_map/ppermute | solution.py:290
  9.3 0.0 copy-start.3
  9.3 1.4 %collective-permute-start = (f32[32,480]{1,0:T(8,128)S(1)}, f32[32,480]{1,0:T(8,128)S(1)}, u32[]{:S(2)}, u32[]{:S(2)}) collective-permute-start(f32[32,480]{1,0:T(8,128)S(1)} %get-tuple-element.45), channel_id=1, source_target_pairs={{0,2},{2,0},{4,6},{6,4},{8,10},{10,8},{12,14},{14,12},{1,3},{3,1},... | collective-permute-start | bytes 184328 | tf_op jit(solution)/shard_map/ppermute | solution.py:290
  10.7 0.0 collective-permute-done.3
  10.7 3.7 %collective-permute-start.5 = (f32[32,480]{1,0:T(8,128)S(1)}, f32[32,480]{1,0:T(8,128)S(1)}, u32[]{:S(2)}, u32[]{:S(2)}) collective-permute-start(f32[32,480]{1,0:T(8,128)S(1)} %get-tuple-element.47), channel_id=1, source_target_pairs={{0,12},{2,14},{4,8},{6,10},{8,4},{10,6},{12,0},{14,2},{1,13},{3,15... | collective-permute-start | bytes 184328 | tf_op jit(solution)/shard_map/ppermute | solution.py:290
  14.4 0.0 collective-permute-start.4
  14.4 0.0 copy-done
  14.4 0.0 copy-done.3
  14.4 1.3 %shard_map.84 = (f32[32,256]{1,0:T(8,128)S(1)}, f32[8,16,480]{2,1,0:T(8,128)S(1)}, f32[8,32,480]{2,1,0:T(8,128)S(1)}) custom-call(s32[1]{0:T(128)} %bitcast.place_ref.own_ref, bf16[3840,128]{1,0:T(8,128)(2,1)S(1)} %get-tuple-element.24.geno_ref.refs_1_.refs_4_.refs_2_, s32[32,3840]{1,0:T(8,128)S(1)} %get-tuple-element.25.counts_ref, ...), custom_call_target="tpu_custom_call" | custom-call | flops 480000000 | tf_op jit(solution)/shard_map/pallas_call | solution.py:265
  15.7 0.0 collective-permute-done.2.refs_3_
  15.7 0.0 collective-permute-done.1.refs_2_
  15.7 0.0 collective-permute-done.refs_1_
  15.7 1.4 %collective-permute-done.5.refs_5_ = f32[32,480]{1,0:T(8,128)S(1)} collective-permute-done((f32[32,480]{1,0:T(8,128)S(1)}, f32[32,480]{1,0:T(8,128)S(1)}, u32[]{:S(2)}, u32[]{:S(2)}) %collective-permute-start.5) | collective-permute-done | bytes 61472 | tf_op jit(solution)/shard_map/ppermute | solution.py:290
  17.2 2.5 %collective-permute-done.4.refs_4_ = f32[32,480]{1,0:T(8,128)S(1)} collective-permute-done((f32[32,480]{1,0:T(8,128)S(1)}, f32[32,480]{1,0:T(8,128)S(1)}, u32[]{:S(2)}, u32[]{:S(2)}) %collective-permute-start.4) | collective-permute-done | bytes 61472 | tf_op jit(solution)/shard_map/ppermute | solution.py:290
  19.6 0.1 shard_map.86
  19.7 0.8 %collective-permute-start.10 = (f32[32,480]{1,0:T(8,128)S(1)}, f32[32,480]{1,0:T(8,128)S(1)}, u32[]{:S(2)}, u32[]{:S(2)}) collective-permute-start(f32[32,480]{1,0:T(8,128)S(1)} %get-tuple-element.28.q_ref.refs_0_), channel_id=1, source_target_pairs={{0,8},{2,10},{4,12},{6,14},{8,0},{10,2},{12,4},{14,6},{1,9},{3,11}... | collective-permute-start | bytes 184328 | tf_op jit(solution)/shard_map/ppermute | solution.py:290
  20.5 1.4 %collective-permute-start.7 = (f32[32,480]{1,0:T(8,128)S(1)}, f32[32,480]{1,0:T(8,128)S(1)}, u32[]{:S(2)}, u32[]{:S(2)}) collective-permute-start(f32[32,480]{1,0:T(8,128)S(1)} %get-tuple-element.28.q_ref.refs_0_), channel_id=1, source_target_pairs={{0,12},{2,14},{4,8},{6,10},{8,4},{10,6},{12,0},{14,2},{1,13},{3,15... | collective-permute-start | bytes 184328 | tf_op jit(solution)/shard_map/ppermute | solution.py:290
  21.9 1.2 %collective-permute-start.13 = (f32[32,480]{1,0:T(8,128)S(1)}, f32[32,480]{1,0:T(8,128)S(1)}, u32[]{:S(2)}, u32[]{:S(2)}) collective-permute-start(f32[32,480]{1,0:T(8,128)S(1)} %get-tuple-element.28.q_ref.refs_0_), channel_id=1, source_target_pairs={{0,2},{2,0},{4,6},{6,4},{8,10},{10,8},{12,14},{14,12},{1,3},{3,1},... | collective-permute-start | bytes 184328 | tf_op jit(solution)/shard_map/ppermute | solution.py:290
  23.1 1.5 %collective-permute-start.12 = (f32[32,480]{1,0:T(8,128)S(1)}, f32[32,480]{1,0:T(8,128)S(1)}, u32[]{:S(2)}, u32[]{:S(2)}) collective-permute-start(f32[32,480]{1,0:T(8,128)S(1)} %get-tuple-element.28.q_ref.refs_0_), channel_id=1, source_target_pairs={{0,4},{2,6},{4,0},{6,2},{8,12},{10,14},{12,8},{14,10},{1,5},{3,7},... | collective-permute-start | bytes 184328 | tf_op jit(solution)/shard_map/ppermute | solution.py:290
  24.6 0.9 %collective-permute-start.9 = (f32[32,480]{1,0:T(8,128)S(1)}, f32[32,480]{1,0:T(8,128)S(1)}, u32[]{:S(2)}, u32[]{:S(2)}) collective-permute-start(f32[32,480]{1,0:T(8,128)S(1)} %get-tuple-element.28.q_ref.refs_0_), channel_id=1, source_target_pairs={{0,6},{2,4},{4,2},{6,0},{8,14},{10,12},{12,10},{14,8},{1,7},{3,5},... | collective-permute-start | bytes 184328 | tf_op jit(solution)/shard_map/ppermute | solution.py:290
  25.4 0.7 %shard_map.89 = (f32[544,128]{1,0:T(8,128)S(1)}, f32[8,16,480]{2,1,0:T(8,128)S(1)}) custom-call(s32[1]{0:T(128)} %bitcast.place_ref.own_ref, f32[32,480]{1,0:T(8,128)S(1)} %get-tuple-element.28.q_ref.refs_0_, bf16[3840,128]{1,0:T(8,128)(2,1)S(1)} %get-tuple-element.24.geno_ref.refs_1_.refs_4_.refs_2_, ...), custom_call_target="tpu_custom_call", output_to_operand_aliasing={{1}: (3, {})} | custom-call | flops 280000000 | tf_op jit(solution)/shard_map/pallas_call | solution.py:265
  26.1 0.9 %collective-permute-done.10.refs_2_ = f32[32,480]{1,0:T(8,128)S(1)} collective-permute-done((f32[32,480]{1,0:T(8,128)S(1)}, f32[32,480]{1,0:T(8,128)S(1)}, u32[]{:S(2)}, u32[]{:S(2)}) %collective-permute-start.10) | collective-permute-done | bytes 61472 | tf_op jit(solution)/shard_map/ppermute | solution.py:290
  27.0 0.4 collective-permute-start.11
  27.3 0.0 collective-permute-done.7.refs_3_
  27.3 1.7 %collective-permute-start.8 = (f32[32,480]{1,0:T(8,128)S(1)}, f32[32,480]{1,0:T(8,128)S(1)}, u32[]{:S(2)}, u32[]{:S(2)}) collective-permute-start(f32[32,480]{1,0:T(8,128)S(1)} %collective-permute-done.7.refs_3_), channel_id=1, source_target_pairs={{0,2},{2,0},{4,6},{6,4},{8,10},{10,8},{12,14},{14,12},{1,3},{3,1},... | collective-permute-start | bytes 184328 | tf_op jit(solution)/shard_map/ppermute | solution.py:290
  29.0 0.0 collective-permute-done.13.refs_1_
  29.0 0.0 collective-permute-done.12.refs_0_
  29.0 2.1 %shard_map.90 = (f32[544,128]{1,0:T(8,128)S(1)}, f32[8,16,480]{2,1,0:T(8,128)S(1)}) custom-call(s32[1]{0:T(128)} %bitcast.place_ref.own_ref, f32[32,480]{1,0:T(8,128)S(1)} %collective-permute-done.12.refs_0_, f32[32,480]{1,0:T(8,128)S(1)} %collective-permute-done.13.refs_1_, ...), custom_call_target="tpu_custom_call", output_to_operand_aliasing={{1}: (6, {}), {0}: (8, {})} | custom-call | flops 1120000000 | tf_op jit(solution)/shard_map/pallas_call | solution.py:265
  31.1 0.0 collective-permute-done.9.refs_0_
  31.1 0.1 collective-permute-done.11.refs_1_
  31.2 1.1 %shard_map.91 = (f32[544,128]{1,0:T(8,128)S(1)}, f32[8,16,480]{2,1,0:T(8,128)S(1)}) custom-call(s32[1]{0:T(128)} %bitcast.place_ref.own_ref, f32[32,480]{1,0:T(8,128)S(1)} %collective-permute-done.9.refs_0_, f32[32,480]{1,0:T(8,128)S(1)} %collective-permute-done.11.refs_1_, ...), custom_call_target="tpu_custom_call", output_to_operand_aliasing={{1}: (4, {}), {0}: (6, {})} | custom-call | flops 560000000 | tf_op jit(solution)/shard_map/pallas_call | solution.py:265
  32.4 0.0 collective-permute-done.8.refs_0_
  32.4 0.0 copy-start.1
  32.4 0.7 %shard_map.92 = (f32[544,128]{1,0:T(8,128)S(1)}, f32[8,16,480]{2,1,0:T(8,128)S(1)}) custom-call(s32[1]{0:T(128)} %bitcast.place_ref.own_ref, f32[32,480]{1,0:T(8,128)S(1)} %collective-permute-done.8.refs_0_, bf16[3840,128]{1,0:T(8,128)(2,1)S(1)} %get-tuple-element.24.geno_ref.refs_1_.refs_4_.refs_2_, ...), custom_call_target="tpu_custom_call", output_to_operand_aliasing={{1}: (3, {}), {0}: (5, {})} | custom-call | flops 280000000 | tf_op jit(solution)/shard_map/pallas_call | solution.py:265
  33.1 0.1 collective-permute-start.14
  33.2 0.2 copy-done.1
  33.4 1.3 %shard_map.87.sums_ref = f32[32,256]{1,0:T(8,128)S(1)} custom-call(s32[1]{0:T(128)} %bitcast.place_ref.own_ref, bf16[3840,128]{1,0:T(8,128)(2,1)S(1)} %get-tuple-element.24.geno_ref.refs_1_.refs_4_.refs_2_, s32[32,3840]{1,0:T(8,128)S(1)} %copy-done.1, f32[32,128]{1,0:T(8,128)S(1)} %copy-done.2, f32[32,256]{1,0:T(8,128)S(1)} %get-tuple-element.30.refs_0_), custom_call_target="tpu_custom_call" | custom-call | flops 400000000 | tf_op jit(solution)/shard_map/pallas_call | solution.py:265
  34.7 0.3 collective-permute-start.6
  35.0 1.0 %collective-permute-done.6.other_ref = f32[32,256]{1,0:T(8,128)S(1)} collective-permute-done((f32[32,256]{1,0:T(8,128)S(1)}, f32[32,256]{1,0:T(8,128)S(1)}, u32[]{:S(2)}, u32[]{:S(2)}) %collective-permute-start.6) | collective-permute-done | bytes 32800 | tf_op jit(solution)/shard_map/ppermute | solution.py:293
  36.0 0.7 %shard_map.88 = (f32[32,480]{1,0:T(8,128)}, f32[32,480]{1,0:T(8,128)}, f32[32,128]{1,0:T(8,128)}, f32[32,128]{1,0:T(8,128)}) custom-call(s32[1]{0:T(128)} %bitcast.place_ref.own_ref, f32[32,480]{1,0:T(8,128)S(1)} %get-tuple-element.28.q_ref.refs_0_, f32[32,480]{1,0:T(8,128)S(1)} %get-tuple-element.29.grad_ref, f32[32,256]{1,0:T(8,128)S(1)} %shard_map.87.sums_ref, ...), custom_call_target="tpu_custom_call" | custom-call | flops 240000000 | tf_op jit(solution)/shard_map/pallas_call | solution.py:265
  36.7 0.0 collective-permute-done.14.other_ref
  36.7 0.8 %shard_map.93 = f32[32,16,128]{2,1,0:T(8,128)} custom-call(s32[1]{0:T(128)} %bitcast.place_ref.own_ref, f32[544,128]{1,0:T(8,128)S(1)} %get-tuple-element.42.mine_ref, f32[544,128]{1,0:T(8,128)S(1)} %collective-permute-done.14.other_ref), custom_call_target="tpu_custom_call" | custom-call | flops 120000000 | tf_op jit(solution)/shard_map/pallas_call | solution.py:265
  (4 shorter events, 0.1 us)
Async XLA Ops:
  3.0 11.3 %copy-start = (s32[32,3840]{1,0:T(8,128)}, s32[32,3840]{1,0:T(8,128)S(1)}, u32[]{:S(2)}) copy-start(s32[32,3840]{1,0:T(8,128)S(1)} %get-tuple-element.25.counts_ref) | copy-start | bytes 1474564
  3.0 3.1 %copy-start.2 = (f32[32,128]{1,0:T(8,128)S(1)}, f32[32,128]{1,0:T(8,128)}, u32[]{:S(2)}) copy-start(f32[32,128]{1,0:T(8,128)} %refs_3_.3) | copy-start | bytes 49156
  3.1 7.6 %collective-permute-start.3 = (f32[2,32,480]{2,1,0:T(8,128)S(1)}, f32[2,32,480]{2,1,0:T(8,128)S(1)}, u32[]{:S(2)}, u32[]{:S(2)}) collective-permute-start(f32[2,32,480]{2,1,0:T(8,128)S(1)} %slice_bitcast_fusion), channel_id=1, source_target_pairs={{0,2},{2,0},{4,6},{6,4},{8,10},{10,8},{12,14},{14,12},{1,3},{3,1},... | collective-permute-start | bytes 368648 | tf_op jit(solution)/shard_map/ppermute | solution.py:290
  7.1 8.6 %collective-permute-start.2 = (f32[32,480]{1,0:T(8,128)S(1)}, f32[32,480]{1,0:T(8,128)S(1)}, u32[]{:S(2)}, u32[]{:S(2)}) collective-permute-start(f32[32,480]{1,0:T(8,128)S(1)} %get-tuple-element.43), channel_id=1, source_target_pairs={{0,6},{2,4},{4,2},{6,0},{8,14},{10,12},{12,10},{14,8},{1,7},{3,5},... | collective-permute-start | bytes 184328 | tf_op jit(solution)/shard_map/ppermute | solution.py:290
  8.8 6.9 %collective-permute-start.1 = (f32[32,480]{1,0:T(8,128)S(1)}, f32[32,480]{1,0:T(8,128)S(1)}, u32[]{:S(2)}, u32[]{:S(2)}) collective-permute-start(f32[32,480]{1,0:T(8,128)S(1)} %get-tuple-element.44), channel_id=1, source_target_pairs={{0,4},{2,6},{4,0},{6,2},{8,12},{10,14},{12,8},{14,10},{1,5},{3,7},... | collective-permute-start | bytes 184328 | tf_op jit(solution)/shard_map/ppermute | solution.py:290
  9.3 5.1 %copy-start.3 = (s32[3840,16]{0,1:T(8,128)S(1)}, s32[3840,16]{0,1:T(8,128)}, u32[]{:S(2)}) copy-start(s32[3840,16]{0,1:T(8,128)} %param.6) | copy-start | bytes 737284
  9.3 6.5 %collective-permute-start = (f32[32,480]{1,0:T(8,128)S(1)}, f32[32,480]{1,0:T(8,128)S(1)}, u32[]{:S(2)}, u32[]{:S(2)}) collective-permute-start(f32[32,480]{1,0:T(8,128)S(1)} %get-tuple-element.45), channel_id=1, source_target_pairs={{0,2},{2,0},{4,6},{6,4},{8,10},{10,8},{12,14},{14,12},{1,3},{3,1},... | collective-permute-start | bytes 184328 | tf_op jit(solution)/shard_map/ppermute | solution.py:290
  10.7 6.4 %collective-permute-start.5 = (f32[32,480]{1,0:T(8,128)S(1)}, f32[32,480]{1,0:T(8,128)S(1)}, u32[]{:S(2)}, u32[]{:S(2)}) collective-permute-start(f32[32,480]{1,0:T(8,128)S(1)} %get-tuple-element.47), channel_id=1, source_target_pairs={{0,12},{2,14},{4,8},{6,10},{8,4},{10,6},{12,0},{14,2},{1,13},{3,15... | collective-permute-start | bytes 184328 | tf_op jit(solution)/shard_map/ppermute | solution.py:290
  14.4 5.3 %collective-permute-start.4 = (f32[32,480]{1,0:T(8,128)S(1)}, f32[32,480]{1,0:T(8,128)S(1)}, u32[]{:S(2)}, u32[]{:S(2)}) collective-permute-start(f32[32,480]{1,0:T(8,128)S(1)} %get-tuple-element.48), channel_id=1, source_target_pairs={{0,8},{2,10},{4,12},{6,14},{8,0},{10,2},{12,4},{14,6},{1,9},{3,11}... | collective-permute-start | bytes 184328 | tf_op jit(solution)/shard_map/ppermute | solution.py:290
  19.7 7.3 %collective-permute-start.10 = (f32[32,480]{1,0:T(8,128)S(1)}, f32[32,480]{1,0:T(8,128)S(1)}, u32[]{:S(2)}, u32[]{:S(2)}) collective-permute-start(f32[32,480]{1,0:T(8,128)S(1)} %get-tuple-element.28.q_ref.refs_0_), channel_id=1, source_target_pairs={{0,8},{2,10},{4,12},{6,14},{8,0},{10,2},{12,4},{14,6},{1,9},{3,11}... | collective-permute-start | bytes 184328 | tf_op jit(solution)/shard_map/ppermute | solution.py:290
  20.5 6.8 %collective-permute-start.7 = (f32[32,480]{1,0:T(8,128)S(1)}, f32[32,480]{1,0:T(8,128)S(1)}, u32[]{:S(2)}, u32[]{:S(2)}) collective-permute-start(f32[32,480]{1,0:T(8,128)S(1)} %get-tuple-element.28.q_ref.refs_0_), channel_id=1, source_target_pairs={{0,12},{2,14},{4,8},{6,10},{8,4},{10,6},{12,0},{14,2},{1,13},{3,15... | collective-permute-start | bytes 184328 | tf_op jit(solution)/shard_map/ppermute | solution.py:290
  21.9 7.1 %collective-permute-start.13 = (f32[32,480]{1,0:T(8,128)S(1)}, f32[32,480]{1,0:T(8,128)S(1)}, u32[]{:S(2)}, u32[]{:S(2)}) collective-permute-start(f32[32,480]{1,0:T(8,128)S(1)} %get-tuple-element.28.q_ref.refs_0_), channel_id=1, source_target_pairs={{0,2},{2,0},{4,6},{6,4},{8,10},{10,8},{12,14},{14,12},{1,3},{3,1},... | collective-permute-start | bytes 184328 | tf_op jit(solution)/shard_map/ppermute | solution.py:290
  23.1 5.9 %collective-permute-start.12 = (f32[32,480]{1,0:T(8,128)S(1)}, f32[32,480]{1,0:T(8,128)S(1)}, u32[]{:S(2)}, u32[]{:S(2)}) collective-permute-start(f32[32,480]{1,0:T(8,128)S(1)} %get-tuple-element.28.q_ref.refs_0_), channel_id=1, source_target_pairs={{0,4},{2,6},{4,0},{6,2},{8,12},{10,14},{12,8},{14,10},{1,5},{3,7},... | collective-permute-start | bytes 184328 | tf_op jit(solution)/shard_map/ppermute | solution.py:290
  24.6 6.5 %collective-permute-start.9 = (f32[32,480]{1,0:T(8,128)S(1)}, f32[32,480]{1,0:T(8,128)S(1)}, u32[]{:S(2)}, u32[]{:S(2)}) collective-permute-start(f32[32,480]{1,0:T(8,128)S(1)} %get-tuple-element.28.q_ref.refs_0_), channel_id=1, source_target_pairs={{0,6},{2,4},{4,2},{6,0},{8,14},{10,12},{12,10},{14,8},{1,7},{3,5},... | collective-permute-start | bytes 184328 | tf_op jit(solution)/shard_map/ppermute | solution.py:290
  27.0 4.3 %collective-permute-start.11 = (f32[32,480]{1,0:T(8,128)S(1)}, f32[32,480]{1,0:T(8,128)S(1)}, u32[]{:S(2)}, u32[]{:S(2)}) collective-permute-start(f32[32,480]{1,0:T(8,128)S(1)} %collective-permute-done.10.refs_2_), channel_id=1, source_target_pairs={{0,2},{2,0},{4,6},{6,4},{8,10},{10,8},{12,14},{14,12},{1,3},{3,1},... | collective-permute-start | bytes 184328 | tf_op jit(solution)/shard_map/ppermute | solution.py:290
  27.3 5.0 %collective-permute-start.8 = (f32[32,480]{1,0:T(8,128)S(1)}, f32[32,480]{1,0:T(8,128)S(1)}, u32[]{:S(2)}, u32[]{:S(2)}) collective-permute-start(f32[32,480]{1,0:T(8,128)S(1)} %collective-permute-done.7.refs_3_), channel_id=1, source_target_pairs={{0,2},{2,0},{4,6},{6,4},{8,10},{10,8},{12,14},{14,12},{1,3},{3,1},... | collective-permute-start | bytes 184328 | tf_op jit(solution)/shard_map/ppermute | solution.py:290
  32.4 1.0 %copy-start.1 = (s32[32,3840]{1,0:T(8,128)S(1)}, s32[32,3840]{1,0:T(8,128)}, u32[]{:S(2)}) copy-start(s32[32,3840]{1,0:T(8,128)} %copy-done) | copy-start | bytes 1474564
  33.1 3.6 %collective-permute-start.14 = (f32[544,128]{1,0:T(8,128)S(1)}, f32[544,128]{1,0:T(8,128)S(1)}, u32[]{:S(2)}, u32[]{:S(2)}) collective-permute-start(f32[544,128]{1,0:T(8,128)S(1)} %get-tuple-element.42.mine_ref), channel_id=1, source_target_pairs={{0,1},{1,0},{2,3},{3,2},{4,5},{5,4},{6,7},{7,6},{8,9},{9,8},{10,11... | collective-permute-start | bytes 835592 | tf_op jit(solution)/shard_map/ppermute | solution.py:293
  34.7 1.2 %collective-permute-start.6 = (f32[32,256]{1,0:T(8,128)S(1)}, f32[32,256]{1,0:T(8,128)S(1)}, u32[]{:S(2)}, u32[]{:S(2)}) collective-permute-start(f32[32,256]{1,0:T(8,128)S(1)} %shard_map.87.sums_ref), channel_id=1, source_target_pairs={{0,1},{1,0},{2,3},{3,2},{4,5},{5,4},{6,7},{7,6},{8,9},{9,8},{10,11... | collective-permute-start | bytes 98312 | tf_op jit(solution)/shard_map/ppermute | solution.py:293

commit v9 on v8

--- a/solution.py
+++ b/solution.py
@@ -346,8 +346,8 @@
 
     groups = (
         (0,),
-        (*reversed(range(1, half - 1)), *range(half, var_count, 2)),
-        (half - 1, *range(half + 1, var_count - 1, 2)),
+        (*reversed(range(1, half - 1)), half),
+        (*range(half + 2, var_count, 2), half - 1, *range(half + 1, var_count - 1, 2)),
         (var_count - 1,),
     )
     total = None
@@ -373,7 +373,7 @@
         final_kernel,
         (place, total, total_other),
         [out((anc, traits, width), F32)],
-        [VMEM((anc, traits, width), F32), dma((4 if anc % 4 == 0 else 1,))],
+        [VMEM((anc, traits, width), F32), dma((2 if anc % 2 == 0 else 1,))],
         cost=300,
     )
     return (q_out.T, grad_out.T, freq_next, freq_gradient, z_score)

time: 37.7 us -> 38 us (level)
    ppermute x13, waiting for transfers between devices: 4.92 us -> 5.35 us  [move(): return lax.ppermute(x, 'var', [(i, i ^ m) for i in range(var_count)])]
where the time goes in v9:
time: 38 us; the launch traced here: 37.8 us
  starting transfers between devices  18.6 us (49%)
  Pallas kernels  12.1 us (32%)
  waiting for transfers between devices  6.21 us (16%)
  between operations  0.79 us (2%)
    ppermute x13, starting transfers between devices, move(): return lax.ppermute(x, 'var', [(i, i ^ m) for i in range(var_count)])  18 us
    pallas_call x11, Pallas kernels, call(): pl.pallas_call(kernel, in_specs=specs, out_specs=out_specs, out_shape=out...  12.1 us
    ppermute x13, waiting for transfers between devices, move(): return lax.ppermute(x, 'var', [(i, i ^ m) for i in range(var_count)])  5.35 us
    ppermute x2, waiting for transfers between devices, swap(): return lax.ppermute(x, 'smp', [(0, 1), (1, 0)])  0.86 us
  transfers between devices with their start and end apart: 15, of which 5 were waited for; matrix products, arithmetic and copies ran while one was open for 0% of the time, Pallas kernels for 22%

profile of v9, /device:TPU:0, one launch (start us, length us, event | category | flops | bytes accessed | tf_op | source)
XLA Modules:
  0.0 37.8 jit_solution(1035567636938720601)
XLA Ops:
  0.6 2.4 %shard_map.83 = (f32[4,32,480]{2,1,0:T(8,128)S(1)}, bf16[3840,128]{1,0:T(8,128)(2,1)S(1)}, s32[32,3840]{1,0:T(8,128)S(1)}) custom-call(s32[1]{0:T(128)} %bitcast.place_ref.own_ref, bf16[3840,128]{1,0:T(8,128)(2,1)} %geno_hbm.1, s32[32,3840]{1,0:T(8,128)} %bitcast.31, f32[32,128]{1,0:T(8,128)} %refs_3_.3), custom_call_target="tpu_custom_call" | custom-call | flops 800000000 | tf_op jit(solution)/shard_map/pallas_call | solution.py:265
  3.0 0.0 copy-start
  3.1 3.0 %collective-permute-start.3 = (f32[2,32,480]{2,1,0:T(8,128)S(1)}, f32[2,32,480]{2,1,0:T(8,128)S(1)}, u32[]{:S(2)}, u32[]{:S(2)}) collective-permute-start(f32[2,32,480]{2,1,0:T(8,128)S(1)} %slice_bitcast_fusion), channel_id=1, source_target_pairs={{0,2},{2,0},{4,6},{6,4},{8,10},{10,8},{12,14},{14,12},{1,3},{3,1},... | collective-permute-start | bytes 368648 | tf_op jit(solution)/shard_map/ppermute | solution.py:290
  6.1 0.0 copy-done
  6.1 0.9 %shard_map.85 = f32[4,32,480]{2,1,0:T(8,128)S(1)} custom-call(s32[1]{0:T(128)} %bitcast.place_ref.own_ref, bf16[3840,128]{1,0:T(8,128)(2,1)S(1)} %get-tuple-element.24.geno_ref.refs_1_.refs_3_, s32[32,3840]{1,0:T(8,128)S(1)} %get-tuple-element.25.counts_ref, f32[32,128]{1,0:T(8,128)S(1)} %copy-done), custom_call_target="tpu_custom_call" | custom-call | flops 800000000 | tf_op jit(solution)/shard_map/pallas_call | solution.py:265
  7.1 1.7 %collective-permute-start.2 = (f32[32,480]{1,0:T(8,128)S(1)}, f32[32,480]{1,0:T(8,128)S(1)}, u32[]{:S(2)}, u32[]{:S(2)}) collective-permute-start(f32[32,480]{1,0:T(8,128)S(1)} %get-tuple-element.43), channel_id=1, source_target_pairs={{0,6},{2,4},{4,2},{6,0},{8,14},{10,12},{12,10},{14,8},{1,7},{3,5},... | collective-permute-start | bytes 184328 | tf_op jit(solution)/shard_map/ppermute | solution.py:290
  8.8 0.4 %collective-permute-start.1 = (f32[32,480]{1,0:T(8,128)S(1)}, f32[32,480]{1,0:T(8,128)S(1)}, u32[]{:S(2)}, u32[]{:S(2)}) collective-permute-start(f32[32,480]{1,0:T(8,128)S(1)} %get-tuple-element.44), channel_id=1, source_target_pairs={{0,4},{2,6},{4,0},{6,2},{8,12},{10,14},{12,8},{14,10},{1,5},{3,7},... | collective-permute-start | bytes 184328 | tf_op jit(solution)/shard_map/ppermute | solution.py:290
  9.2 0.0 copy-start.1
  9.2 1.4 %collective-permute-start = (f32[32,480]{1,0:T(8,128)S(1)}, f32[32,480]{1,0:T(8,128)S(1)}, u32[]{:S(2)}, u32[]{:S(2)}) collective-permute-start(f32[32,480]{1,0:T(8,128)S(1)} %get-tuple-element.45), channel_id=1, source_target_pairs={{0,2},{2,0},{4,6},{6,4},{8,10},{10,8},{12,14},{14,12},{1,3},{3,1},... | collective-permute-start | bytes 184328 | tf_op jit(solution)/shard_map/ppermute | solution.py:290
  10.6 0.0 collective-permute-done.3
  10.7 3.7 %collective-permute-start.5 = (f32[32,480]{1,0:T(8,128)S(1)}, f32[32,480]{1,0:T(8,128)S(1)}, u32[]{:S(2)}, u32[]{:S(2)}) collective-permute-start(f32[32,480]{1,0:T(8,128)S(1)} %get-tuple-element.47), channel_id=1, source_target_pairs={{0,12},{2,14},{4,8},{6,10},{8,4},{10,6},{12,0},{14,2},{1,13},{3,15... | collective-permute-start | bytes 184328 | tf_op jit(solution)/shard_map/ppermute | solution.py:290
  14.4 0.0 collective-permute-start.4
  14.4 0.0 copy-done.1
  14.4 1.3 %shard_map.84 = (f32[32,256]{1,0:T(8,128)S(1)}, f32[8,16,480]{2,1,0:T(8,128)S(1)}, f32[8,32,480]{2,1,0:T(8,128)S(1)}) custom-call(s32[1]{0:T(128)} %bitcast.place_ref.own_ref, bf16[3840,128]{1,0:T(8,128)(2,1)S(1)} %get-tuple-element.24.geno_ref.refs_1_.refs_3_, s32[32,3840]{1,0:T(8,128)S(1)} %get-tuple-element.25.counts_ref, f32[32,128]{1,0:T(8,128)S(1)} %copy-done, ...), custom_call_target="tpu_custom_call" | custom-call | flops 480000000 | tf_op jit(solution)/shard_map/pallas_call | solution.py:265
  15.7 0.0 collective-permute-done.2.refs_3_
  15.7 0.0 collective-permute-done.1.refs_2_
  15.7 0.0 collective-permute-done.refs_1_
  15.7 1.4 %collective-permute-done.5.refs_5_ = f32[32,480]{1,0:T(8,128)S(1)} collective-permute-done((f32[32,480]{1,0:T(8,128)S(1)}, f32[32,480]{1,0:T(8,128)S(1)}, u32[]{:S(2)}, u32[]{:S(2)}) %collective-permute-start.5) | collective-permute-done | bytes 61472 | tf_op jit(solution)/shard_map/ppermute | solution.py:290
  17.1 2.5 %collective-permute-done.4.refs_4_ = f32[32,480]{1,0:T(8,128)S(1)} collective-permute-done((f32[32,480]{1,0:T(8,128)S(1)}, f32[32,480]{1,0:T(8,128)S(1)}, u32[]{:S(2)}, u32[]{:S(2)}) %collective-permute-start.4) | collective-permute-done | bytes 61472 | tf_op jit(solution)/shard_map/ppermute | solution.py:290
  19.6 0.1 shard_map.86
  19.7 0.8 %collective-permute-start.10 = (f32[32,480]{1,0:T(8,128)S(1)}, f32[32,480]{1,0:T(8,128)S(1)}, u32[]{:S(2)}, u32[]{:S(2)}) collective-permute-start(f32[32,480]{1,0:T(8,128)S(1)} %get-tuple-element.28.q_ref.refs_0_), channel_id=1, source_target_pairs={{0,8},{2,10},{4,12},{6,14},{8,0},{10,2},{12,4},{14,6},{1,9},{3,11}... | collective-permute-start | bytes 184328 | tf_op jit(solution)/shard_map/ppermute | solution.py:290
  20.5 1.4 %collective-permute-start.7 = (f32[32,480]{1,0:T(8,128)S(1)}, f32[32,480]{1,0:T(8,128)S(1)}, u32[]{:S(2)}, u32[]{:S(2)}) collective-permute-start(f32[32,480]{1,0:T(8,128)S(1)} %get-tuple-element.28.q_ref.refs_0_), channel_id=1, source_target_pairs={{0,12},{2,14},{4,8},{6,10},{8,4},{10,6},{12,0},{14,2},{1,13},{3,15... | collective-permute-start | bytes 184328 | tf_op jit(solution)/shard_map/ppermute | solution.py:290
  21.9 1.2 %collective-permute-start.13 = (f32[32,480]{1,0:T(8,128)S(1)}, f32[32,480]{1,0:T(8,128)S(1)}, u32[]{:S(2)}, u32[]{:S(2)}) collective-permute-start(f32[32,480]{1,0:T(8,128)S(1)} %get-tuple-element.28.q_ref.refs_0_), channel_id=1, source_target_pairs={{0,2},{2,0},{4,6},{6,4},{8,10},{10,8},{12,14},{14,12},{1,3},{3,1},... | collective-permute-start | bytes 184328 | tf_op jit(solution)/shard_map/ppermute | solution.py:290
  23.1 1.5 %collective-permute-start.12 = (f32[32,480]{1,0:T(8,128)S(1)}, f32[32,480]{1,0:T(8,128)S(1)}, u32[]{:S(2)}, u32[]{:S(2)}) collective-permute-start(f32[32,480]{1,0:T(8,128)S(1)} %get-tuple-element.28.q_ref.refs_0_), channel_id=1, source_target_pairs={{0,4},{2,6},{4,0},{6,2},{8,12},{10,14},{12,8},{14,10},{1,5},{3,7},... | collective-permute-start | bytes 184328 | tf_op jit(solution)/shard_map/ppermute | solution.py:290
  24.5 0.9 %collective-permute-start.9 = (f32[32,480]{1,0:T(8,128)S(1)}, f32[32,480]{1,0:T(8,128)S(1)}, u32[]{:S(2)}, u32[]{:S(2)}) collective-permute-start(f32[32,480]{1,0:T(8,128)S(1)} %get-tuple-element.28.q_ref.refs_0_), channel_id=1, source_target_pairs={{0,6},{2,4},{4,2},{6,0},{8,14},{10,12},{12,10},{14,8},{1,7},{3,5},... | collective-permute-start | bytes 184328 | tf_op jit(solution)/shard_map/ppermute | solution.py:290
  25.4 0.7 %shard_map.89 = (f32[544,128]{1,0:T(8,128)S(1)}, f32[8,16,480]{2,1,0:T(8,128)S(1)}) custom-call(s32[1]{0:T(128)} %bitcast.place_ref.own_ref, f32[32,480]{1,0:T(8,128)S(1)} %get-tuple-element.28.q_ref.refs_0_, bf16[3840,128]{1,0:T(8,128)(2,1)S(1)} %get-tuple-element.24.geno_ref.refs_1_.refs_3_, ...), custom_call_target="tpu_custom_call", output_to_operand_aliasing={{1}: (3, {})} | custom-call | flops 280000000 | tf_op jit(solution)/shard_map/pallas_call | solution.py:265
  26.1 0.8 %collective-permute-done.10.refs_2_ = f32[32,480]{1,0:T(8,128)S(1)} collective-permute-done((f32[32,480]{1,0:T(8,128)S(1)}, f32[32,480]{1,0:T(8,128)S(1)}, u32[]{:S(2)}, u32[]{:S(2)}) %collective-permute-start.10) | collective-permute-done | bytes 61472 | tf_op jit(solution)/shard_map/ppermute | solution.py:290
  26.9 0.4 %collective-permute-start.11 = (f32[32,480]{1,0:T(8,128)S(1)}, f32[32,480]{1,0:T(8,128)S(1)}, u32[]{:S(2)}, u32[]{:S(2)}) collective-permute-start(f32[32,480]{1,0:T(8,128)S(1)} %collective-permute-done.10.refs_2_), channel_id=1, source_target_pairs={{0,2},{2,0},{4,6},{6,4},{8,10},{10,8},{12,14},{14,12},{1,3},{3,1},... | collective-permute-start | bytes 184328 | tf_op jit(solution)/shard_map/ppermute | solution.py:290
  27.3 0.0 collective-permute-done.7.refs_0_
  27.3 1.6 %collective-permute-start.8 = (f32[32,480]{1,0:T(8,128)S(1)}, f32[32,480]{1,0:T(8,128)S(1)}, u32[]{:S(2)}, u32[]{:S(2)}) collective-permute-start(f32[32,480]{1,0:T(8,128)S(1)} %collective-permute-done.7.refs_0_), channel_id=1, source_target_pairs={{0,2},{2,0},{4,6},{6,4},{8,10},{10,8},{12,14},{14,12},{1,3},{3,1},... | collective-permute-start | bytes 184328 | tf_op jit(solution)/shard_map/ppermute | solution.py:290
  29.0 0.0 collective-permute-done.13.refs_1_
  29.0 0.0 collective-permute-done.12.refs_0_
  29.0 1.6 %shard_map.90 = (f32[544,128]{1,0:T(8,128)S(1)}, f32[8,16,480]{2,1,0:T(8,128)S(1)}) custom-call(s32[1]{0:T(128)} %bitcast.place_ref.own_ref, f32[32,480]{1,0:T(8,128)S(1)} %collective-permute-done.12.refs_0_, f32[32,480]{1,0:T(8,128)S(1)} %collective-permute-done.13.refs_1_, ...), custom_call_target="tpu_custom_call", output_to_operand_aliasing={{1}: (5, {}), {0}: (7, {})} | custom-call | flops 840000000 | tf_op jit(solution)/shard_map/pallas_call | solution.py:265
  30.6 0.0 collective-permute-done.9.refs_1_
  30.6 0.6 %collective-permute-done.11.refs_2_ = f32[32,480]{1,0:T(8,128)S(1)} collective-permute-done((f32[32,480]{1,0:T(8,128)S(1)}, f32[32,480]{1,0:T(8,128)S(1)}, u32[]{:S(2)}, u32[]{:S(2)}) %collective-permute-start.11) | collective-permute-done | bytes 61472 | tf_op jit(solution)/shard_map/ppermute | solution.py:290
  31.2 1.6 %shard_map.91 = (f32[544,128]{1,0:T(8,128)S(1)}, f32[8,16,480]{2,1,0:T(8,128)S(1)}) custom-call(s32[1]{0:T(128)} %bitcast.place_ref.own_ref, f32[32,480]{1,0:T(8,128)S(1)} %collective-permute-done.7.refs_0_, f32[32,480]{1,0:T(8,128)S(1)} %collective-permute-done.9.refs_1_, ...), custom_call_target="tpu_custom_call", output_to_operand_aliasing={{1}: (5, {}), {0}: (7, {})} | custom-call | flops 840000000 | tf_op jit(solution)/shard_map/pallas_call | solution.py:265
  32.8 0.0 collective-permute-done.8.refs_0_
  32.8 0.7 %shard_map.92 = (f32[544,128]{1,0:T(8,128)S(1)}, f32[8,16,480]{2,1,0:T(8,128)S(1)}) custom-call(s32[1]{0:T(128)} %bitcast.place_ref.own_ref, f32[32,480]{1,0:T(8,128)S(1)} %collective-permute-done.8.refs_0_, bf16[3840,128]{1,0:T(8,128)(2,1)S(1)} %get-tuple-element.24.geno_ref.refs_1_.refs_3_, ...), custom_call_target="tpu_custom_call", output_to_operand_aliasing={{1}: (3, {}), {0}: (5, {})} | custom-call | flops 280000000 | tf_op jit(solution)/shard_map/pallas_call | solution.py:265
  33.5 0.1 collective-permute-start.14
  33.6 1.3 %shard_map.87.sums_ref = f32[32,256]{1,0:T(8,128)S(1)} custom-call(s32[1]{0:T(128)} %bitcast.place_ref.own_ref, bf16[3840,128]{1,0:T(8,128)(2,1)S(1)} %get-tuple-element.24.geno_ref.refs_1_.refs_3_, s32[32,3840]{1,0:T(8,128)S(1)} %get-tuple-element.25.counts_ref, f32[32,128]{1,0:T(8,128)S(1)} %copy-done, f32[32,256]{1,0:T(8,128)S(1)} %get-tuple-element.30.refs_0_), custom_call_target="tpu_custom_call" | custom-call | flops 400000000 | tf_op jit(solution)/shard_map/pallas_call | solution.py:265
  34.9 0.5 %collective-permute-start.6 = (f32[32,256]{1,0:T(8,128)S(1)}, f32[32,256]{1,0:T(8,128)S(1)}, u32[]{:S(2)}, u32[]{:S(2)}) collective-permute-start(f32[32,256]{1,0:T(8,128)S(1)} %shard_map.87.sums_ref), channel_id=1, source_target_pairs={{0,1},{1,0},{2,3},{3,2},{4,5},{5,4},{6,7},{7,6},{8,9},{9,8},{10,11... | collective-permute-start | bytes 98312 | tf_op jit(solution)/shard_map/ppermute | solution.py:293
  35.4 0.9 %collective-permute-done.6.other_ref = f32[32,256]{1,0:T(8,128)S(1)} collective-permute-done((f32[32,256]{1,0:T(8,128)S(1)}, f32[32,256]{1,0:T(8,128)S(1)}, u32[]{:S(2)}, u32[]{:S(2)}) %collective-permute-start.6) | collective-permute-done | bytes 32800 | tf_op jit(solution)/shard_map/ppermute | solution.py:293
  36.3 0.7 %shard_map.88 = (f32[32,480]{1,0:T(8,128)}, f32[32,480]{1,0:T(8,128)}, f32[32,128]{1,0:T(8,128)}, f32[32,128]{1,0:T(8,128)}) custom-call(s32[1]{0:T(128)} %bitcast.place_ref.own_ref, f32[32,480]{1,0:T(8,128)S(1)} %get-tuple-element.28.q_ref.refs_0_, f32[32,480]{1,0:T(8,128)S(1)} %get-tuple-element.29.grad_ref, f32[32,256]{1,0:T(8,128)S(1)} %shard_map.87.sums_ref, ...), custom_call_target="tpu_custom_call" | custom-call | flops 240000000 | tf_op jit(solution)/shard_map/pallas_call | solution.py:265
  37.0 0.0 collective-permute-done.14.other_ref
  37.0 0.8 %shard_map.93 = f32[32,16,128]{2,1,0:T(8,128)} custom-call(s32[1]{0:T(128)} %bitcast.place_ref.own_ref, f32[544,128]{1,0:T(8,128)S(1)} %get-tuple-element.42.mine_ref, f32[544,128]{1,0:T(8,128)S(1)} %collective-permute-done.14.other_ref), custom_call_target="tpu_custom_call" | custom-call | flops 120000000 | tf_op jit(solution)/shard_map/pallas_call | solution.py:265
  (4 shorter events, 0.1 us)
Async XLA Ops:
  3.0 3.1 %copy-start = (f32[32,128]{1,0:T(8,128)S(1)}, f32[32,128]{1,0:T(8,128)}, u32[]{:S(2)}) copy-start(f32[32,128]{1,0:T(8,128)} %refs_3_.3) | copy-start | bytes 49156
  3.1 7.6 %collective-permute-start.3 = (f32[2,32,480]{2,1,0:T(8,128)S(1)}, f32[2,32,480]{2,1,0:T(8,128)S(1)}, u32[]{:S(2)}, u32[]{:S(2)}) collective-permute-start(f32[2,32,480]{2,1,0:T(8,128)S(1)} %slice_bitcast_fusion), channel_id=1, source_target_pairs={{0,2},{2,0},{4,6},{6,4},{8,10},{10,8},{12,14},{14,12},{1,3},{3,1},... | collective-permute-start | bytes 368648 | tf_op jit(solution)/shard_map/ppermute | solution.py:290
  7.1 8.6 %collective-permute-start.2 = (f32[32,480]{1,0:T(8,128)S(1)}, f32[32,480]{1,0:T(8,128)S(1)}, u32[]{:S(2)}, u32[]{:S(2)}) collective-permute-start(f32[32,480]{1,0:T(8,128)S(1)} %get-tuple-element.43), channel_id=1, source_target_pairs={{0,6},{2,4},{4,2},{6,0},{8,14},{10,12},{12,10},{14,8},{1,7},{3,5},... | collective-permute-start | bytes 184328 | tf_op jit(solution)/shard_map/ppermute | solution.py:290
  8.8 6.9 %collective-permute-start.1 = (f32[32,480]{1,0:T(8,128)S(1)}, f32[32,480]{1,0:T(8,128)S(1)}, u32[]{:S(2)}, u32[]{:S(2)}) collective-permute-start(f32[32,480]{1,0:T(8,128)S(1)} %get-tuple-element.44), channel_id=1, source_target_pairs={{0,4},{2,6},{4,0},{6,2},{8,12},{10,14},{12,8},{14,10},{1,5},{3,7},... | collective-permute-start | bytes 184328 | tf_op jit(solution)/shard_map/ppermute | solution.py:290
  9.2 5.1 %copy-start.1 = (s32[3840,16]{0,1:T(8,128)S(1)}, s32[3840,16]{0,1:T(8,128)}, u32[]{:S(2)}) copy-start(s32[3840,16]{0,1:T(8,128)} %param.6) | copy-start | bytes 737284
  9.2 6.5 %collective-permute-start = (f32[32,480]{1,0:T(8,128)S(1)}, f32[32,480]{1,0:T(8,128)S(1)}, u32[]{:S(2)}, u32[]{:S(2)}) collective-permute-start(f32[32,480]{1,0:T(8,128)S(1)} %get-tuple-element.45), channel_id=1, source_target_pairs={{0,2},{2,0},{4,6},{6,4},{8,10},{10,8},{12,14},{14,12},{1,3},{3,1},... | collective-permute-start | bytes 184328 | tf_op jit(solution)/shard_map/ppermute | solution.py:290
  10.7 6.4 %collective-permute-start.5 = (f32[32,480]{1,0:T(8,128)S(1)}, f32[32,480]{1,0:T(8,128)S(1)}, u32[]{:S(2)}, u32[]{:S(2)}) collective-permute-start(f32[32,480]{1,0:T(8,128)S(1)} %get-tuple-element.47), channel_id=1, source_target_pairs={{0,12},{2,14},{4,8},{6,10},{8,4},{10,6},{12,0},{14,2},{1,13},{3,15... | collective-permute-start | bytes 184328 | tf_op jit(solution)/shard_map/ppermute | solution.py:290
  14.4 5.2 %collective-permute-start.4 = (f32[32,480]{1,0:T(8,128)S(1)}, f32[32,480]{1,0:T(8,128)S(1)}, u32[]{:S(2)}, u32[]{:S(2)}) collective-permute-start(f32[32,480]{1,0:T(8,128)S(1)} %get-tuple-element.48), channel_id=1, source_target_pairs={{0,8},{2,10},{4,12},{6,14},{8,0},{10,2},{12,4},{14,6},{1,9},{3,11}... | collective-permute-start | bytes 184328 | tf_op jit(solution)/shard_map/ppermute | solution.py:290
  19.7 7.3 %collective-permute-start.10 = (f32[32,480]{1,0:T(8,128)S(1)}, f32[32,480]{1,0:T(8,128)S(1)}, u32[]{:S(2)}, u32[]{:S(2)}) collective-permute-start(f32[32,480]{1,0:T(8,128)S(1)} %get-tuple-element.28.q_ref.refs_0_), channel_id=1, source_target_pairs={{0,8},{2,10},{4,12},{6,14},{8,0},{10,2},{12,4},{14,6},{1,9},{3,11}... | collective-permute-start | bytes 184328 | tf_op jit(solution)/shard_map/ppermute | solution.py:290
  20.5 6.9 %collective-permute-start.7 = (f32[32,480]{1,0:T(8,128)S(1)}, f32[32,480]{1,0:T(8,128)S(1)}, u32[]{:S(2)}, u32[]{:S(2)}) collective-permute-start(f32[32,480]{1,0:T(8,128)S(1)} %get-tuple-element.28.q_ref.refs_0_), channel_id=1, source_target_pairs={{0,12},{2,14},{4,8},{6,10},{8,4},{10,6},{12,0},{14,2},{1,13},{3,15... | collective-permute-start | bytes 184328 | tf_op jit(solution)/shard_map/ppermute | solution.py:290
  21.9 7.1 %collective-permute-start.13 = (f32[32,480]{1,0:T(8,128)S(1)}, f32[32,480]{1,0:T(8,128)S(1)}, u32[]{:S(2)}, u32[]{:S(2)}) collective-permute-start(f32[32,480]{1,0:T(8,128)S(1)} %get-tuple-element.28.q_ref.refs_0_), channel_id=1, source_target_pairs={{0,2},{2,0},{4,6},{6,4},{8,10},{10,8},{12,14},{14,12},{1,3},{3,1},... | collective-permute-start | bytes 184328 | tf_op jit(solution)/shard_map/ppermute | solution.py:290
  23.1 5.9 %collective-permute-start.12 = (f32[32,480]{1,0:T(8,128)S(1)}, f32[32,480]{1,0:T(8,128)S(1)}, u32[]{:S(2)}, u32[]{:S(2)}) collective-permute-start(f32[32,480]{1,0:T(8,128)S(1)} %get-tuple-element.28.q_ref.refs_0_), channel_id=1, source_target_pairs={{0,4},{2,6},{4,0},{6,2},{8,12},{10,14},{12,8},{14,10},{1,5},{3,7},... | collective-permute-start | bytes 184328 | tf_op jit(solution)/shard_map/ppermute | solution.py:290
  24.5 6.0 %collective-permute-start.9 = (f32[32,480]{1,0:T(8,128)S(1)}, f32[32,480]{1,0:T(8,128)S(1)}, u32[]{:S(2)}, u32[]{:S(2)}) collective-permute-start(f32[32,480]{1,0:T(8,128)S(1)} %get-tuple-element.28.q_ref.refs_0_), channel_id=1, source_target_pairs={{0,6},{2,4},{4,2},{6,0},{8,14},{10,12},{12,10},{14,8},{1,7},{3,5},... | collective-permute-start | bytes 184328 | tf_op jit(solution)/shard_map/ppermute | solution.py:290
  26.9 4.3 %collective-permute-start.11 = (f32[32,480]{1,0:T(8,128)S(1)}, f32[32,480]{1,0:T(8,128)S(1)}, u32[]{:S(2)}, u32[]{:S(2)}) collective-permute-start(f32[32,480]{1,0:T(8,128)S(1)} %collective-permute-done.10.refs_2_), channel_id=1, source_target_pairs={{0,2},{2,0},{4,6},{6,4},{8,10},{10,8},{12,14},{14,12},{1,3},{3,1},... | collective-permute-start | bytes 184328 | tf_op jit(solution)/shard_map/ppermute | solution.py:290
  27.3 5.5 %collective-permute-start.8 = (f32[32,480]{1,0:T(8,128)S(1)}, f32[32,480]{1,0:T(8,128)S(1)}, u32[]{:S(2)}, u32[]{:S(2)}) collective-permute-start(f32[32,480]{1,0:T(8,128)S(1)} %collective-permute-done.7.refs_0_), channel_id=1, source_target_pairs={{0,2},{2,0},{4,6},{6,4},{8,10},{10,8},{12,14},{14,12},{1,3},{3,1},... | collective-permute-start | bytes 184328 | tf_op jit(solution)/shard_map/ppermute | solution.py:290
  33.5 3.5 %collective-permute-start.14 = (f32[544,128]{1,0:T(8,128)S(1)}, f32[544,128]{1,0:T(8,128)S(1)}, u32[]{:S(2)}, u32[]{:S(2)}) collective-permute-start(f32[544,128]{1,0:T(8,128)S(1)} %get-tuple-element.42.mine_ref), channel_id=1, source_target_pairs={{0,1},{1,0},{2,3},{3,2},{4,5},{5,4},{6,7},{7,6},{8,9},{9,8},{10,11... | collective-permute-start | bytes 835592 | tf_op jit(solution)/shard_map/ppermute | solution.py:293
  34.9 1.4 %collective-permute-start.6 = (f32[32,256]{1,0:T(8,128)S(1)}, f32[32,256]{1,0:T(8,128)S(1)}, u32[]{:S(2)}, u32[]{:S(2)}) collective-permute-start(f32[32,256]{1,0:T(8,128)S(1)} %shard_map.87.sums_ref), channel_id=1, source_target_pairs={{0,1},{1,0},{2,3},{3,2},{4,5},{5,4},{6,7},{7,6},{8,9},{9,8},{10,11... | collective-permute-start | bytes 98312 | tf_op jit(solution)/shard_map/ppermute | solution.py:293
